TPU v7x, 128 devices: a whole 4x4x4 slice. The times are simulated.
128 devices in a mesh: req: 16 (over z, x), tok: 8 (over y, core).
Axes of the slice: x: 4, y: 4, z: 4, core: 2. Of those that a mesh axis runs over, the one named last changes fastest.
Arguments:
- queries: bfloat16 [8192, 2048], P('req', 'tok'), may hold values from -6 to 6
- suffix_kv: bfloat16 [8192, 2048], P('req'), may hold values from -6 to 6
- prefix_cache: bfloat16 [8192, 2048], P('req'), may hold values from -24 to 24
- q_gain: float32 [256], replicated, may hold values from 0.1 to 1.9
- k_gain: float32 [256], replicated, may hold values from 0.1 to 1.9
- lengths: int32 [16, 3], P('req'), may hold values from 1 to 256, 512 in all within a row
- group_of: int32 [16], replicated, may hold values from 0 to 1
- owner_order: int32 [16], replicated, may hold values from 0 to 15, each once
- residual: bfloat16 [8192, 2560], P('req'), may hold values from -6 to 6
- w_out: bfloat16 [2048, 2560], P('tok'), may hold values from -0.125 to 0.125
- attn_gain: float32 [2560], replicated, may hold values from 0.1 to 1.9
- ffn_in_gain: float32 [2560], replicated, may hold values from 0.1 to 1.9
- ffn_out_gain: float32 [2560], replicated, may hold values from 0.1 to 1.9
- w_gate: bfloat16 [2560, 10240], P(None, 'tok'), may hold values from -0.125 to 0.125
- w_up: bfloat16 [2560, 10240], P(None, 'tok'), may hold values from -0.125 to 0.125
- w_down: bfloat16 [10240, 2560], P('tok'), may hold values from -0.0625 to 0.0625
Outputs:
- layer_out: bfloat16 [8192, 2560], P(('req', 'tok'))
Inputs may be any that keep to these rules, and one draw needn't show every extreme that they name: The 3 lengths of each req index sum to 512; the largest is exactly 256. `owner_order`: each req index appears once; entries g * 8 to g * 8 + 7 name the holders of group g's prefix.
All inputs are finite; a program needn't handle non-finite values.
Results may differ from a plain program's by a relative error of at most 0.02.
Values may be sent and summed in bfloat16 or wider, within the bound.
A program may use at most 128 MiB of HBM per device.

v0:
```python
import jax
import jax.numpy as jnp
from jax import lax
from jax.sharding import PartitionSpec as P

H = 8
KVH = 4
HD = 256
GROUPS = 2


EPSILON = 1e-06
MASKED = -1e30


def rms_scale(values_in, gain_vec):
    return (
        values_in
        * lax.rsqrt(jnp.mean(values_in * values_in, axis=-1, keepdims=True) + EPSILON)
        * gain_vec
    )


def norm_heads(values_in, gain_vec, head_count):
    row_count = values_in.shape[0]
    shaped = values_in.astype(jnp.float32).reshape(row_count, head_count, HD)
    return rms_scale(shaped, gain_vec).astype(jnp.bfloat16).reshape(row_count, head_count * HD)


def softmax_part(query_head, key_head, value_head, visible):
    scores = jnp.einsum(
        "...qd,kd->...qk", query_head, key_head, preferred_element_type=jnp.float32
    ) * HD ** (-0.5)
    scores = jnp.where(visible, scores, MASKED)
    row_max = jnp.max(scores, axis=-1)
    weights = jnp.exp(scores - row_max[..., None])
    row_sum = jnp.sum(weights, axis=-1)
    output = jnp.einsum(
        "...qk,kd->...qd",
        weights.astype(jnp.bfloat16),
        value_head,
        preferred_element_type=jnp.float32,
    )
    return (row_max, row_sum, output)


def heads_parts(query_rows, keys_local, values_local, visible, kv_map):
    maxima, totals, outputs = ([], [], [])
    for head_idx, kv_idx in enumerate(kv_map):
        part_max, part_sum, part_out = softmax_part(query_rows, keys_local, values_local, visible)
        maxima.append(part_max)
        totals.append(part_sum)
        outputs.append(part_out)
    return (
        jnp.stack(maxima, axis=-1),
        jnp.stack(totals, axis=-1),
        jnp.concatenate(outputs, axis=-1),
    )


def split_heads(values_in, head_count):
    return values_in.reshape(values_in.shape[:-1] + (head_count, HD))


def owner_groups(owner_order):
    count_all = owner_order.shape[0]
    slots = jnp.arange(count_all, dtype=jnp.int32)
    match_table = (owner_order[None, :] == slots[:, None]).astype(jnp.int32)
    place = jnp.sum(match_table * slots[None, :], axis=1)
    return place // (count_all // GROUPS)


def local(
    queries,
    suffix_kv,
    prefix_cache,
    q_gain,
    k_gain,
    lengths,
    group_of,
    owner_order,
    residual,
    w_out,
    attn_gain,
    ffn_in_gain,
    ffn_out_gain,
    w_gate,
    w_up,
    w_down,
):
    tok_count = lax.axis_size("tok")
    req_index = lax.axis_index("req")
    tok_index = lax.axis_index("tok")
    row_count = queries.shape[0]
    heads_here = queries.shape[1] // HD
    head_ratio = H // KVH
    kv_count = max(1, heads_here // head_ratio)
    kv_map = [0]
    kv_first = tok_index * heads_here // head_ratio
    kv_width = KVH * HD
    query_normed = norm_heads(queries, q_gain, heads_here)
    suf_keys = norm_heads(
        lax.dynamic_slice_in_dim(suffix_kv, kv_first * HD, kv_count * HD, 1), k_gain, kv_count
    )
    suf_vals = lax.dynamic_slice_in_dim(suffix_kv, kv_width + kv_first * HD, kv_count * HD, 1)
    seg_ends = jnp.cumsum(lengths[0])
    positions = jnp.arange(row_count, dtype=jnp.int32)
    segment = jnp.sum((positions[:, None] >= seg_ends[None, :]).astype(jnp.int32), axis=1)
    causal = (segment[:, None] == segment[None, :]) & (positions[None, :] <= positions[:, None])
    suffix_part = heads_parts(query_normed, suf_keys, suf_vals, causal, kv_map)
    own_group = group_of[req_index]
    holder_groups = owner_groups(owner_order)
    member = holder_groups == own_group
    pref_keys = lax.dynamic_slice_in_dim(prefix_cache, kv_first * HD, kv_count * HD, 1)
    pref_vals = lax.dynamic_slice_in_dim(prefix_cache, kv_width + kv_first * HD, kv_count * HD, 1)
    outgoing = jnp.where(member[:, None, None], query_normed[None], jnp.zeros((), jnp.bfloat16))
    holder_group = holder_groups[req_index]
    sender_match = group_of == holder_group
    arrived = lax.all_to_all(outgoing, "req", split_axis=0, concat_axis=0, tiled=True)
    item_count = arrived.shape[1]

    def skip_slot(slot_rows):
        return (
            jnp.full((item_count, heads_here), MASKED, jnp.float32),
            jnp.zeros((item_count, heads_here), jnp.float32),
            jnp.zeros((item_count, heads_here * HD), jnp.float32),
        )

    def work_slot(slot_rows):
        return heads_parts(slot_rows, pref_keys, pref_vals, True, kv_map)

    def one_slot(pair):
        slot_rows, wanted = pair
        return lax.cond(wanted, work_slot, skip_slot, slot_rows)

    slot_max, slot_sum, slot_out = lax.map(one_slot, (arrived, sender_match))
    slot_max, slot_sum, slot_out = (
        lax.all_to_all(slot_max, "req", split_axis=0, concat_axis=0, tiled=True),
        lax.all_to_all(slot_sum, "req", split_axis=0, concat_axis=0, tiled=True),
        lax.all_to_all(slot_out, "req", split_axis=0, concat_axis=0, tiled=True),
    )
    slot_max = jnp.where(member[:, None, None], slot_max, MASKED)
    suf_max, suf_sum, suf_out = suffix_part
    row_max = jnp.maximum(jnp.max(slot_max, axis=0), suf_max)
    slot_scale = jnp.exp(slot_max - row_max[None])
    suf_scale = jnp.exp(suf_max - row_max)
    row_sum = suf_sum * suf_scale + jnp.sum(slot_sum * slot_scale, axis=0)
    merged = split_heads(suf_out, heads_here) * suf_scale[..., None] + jnp.sum(
        split_heads(slot_out, heads_here) * slot_scale[..., None], axis=0
    )
    attention = (
        (merged / row_sum[..., None]).reshape(row_count, heads_here * HD).astype(jnp.bfloat16)
    )
    share = row_count // tok_count
    first_row = tok_index * share
    projected = lax.psum(jnp.dot(attention, w_out, preferred_element_type=jnp.float32), "tok")
    mixed_rows = residual.astype(jnp.float32) + rms_scale(projected, attn_gain)
    normed = rms_scale(mixed_rows, ffn_in_gain).astype(jnp.bfloat16)
    mixed_share = lax.dynamic_slice_in_dim(mixed_rows, first_row, share, 0)
    gate = jnp.dot(normed, w_gate, preferred_element_type=jnp.float32)
    upward = jnp.dot(normed, w_up, preferred_element_type=jnp.float32)
    hidden = (jax.nn.gelu(gate, approximate=True) * upward).astype(jnp.bfloat16)
    down_share = lax.psum_scatter(
        jnp.dot(hidden, w_down, preferred_element_type=jnp.float32),
        "tok",
        scatter_dimension=0,
        tiled=True,
    )
    return (mixed_share + rms_scale(down_share, ffn_out_gain)).astype(jnp.bfloat16)


def solution(mesh):
    in_specs = (
        P("req", "tok"),
        P("req", None),
        P("req", None),
        P(),
        P(),
        P("req", None),
        P(),
        P(),
        P("req", None),
        P("tok", None),
        P(),
        P(),
        P(),
        P(None, "tok"),
        P(None, "tok"),
        P("tok", None),
    )
    out_specs = P(("req", "tok"), None)
    return jax.shard_map(local, mesh=mesh, in_specs=in_specs, out_specs=out_specs, check_vma=False)
```

profile of v0, /device:TPU:1, one launch (start us, length us, event | category | flops | bytes accessed | tf_op | source)
XLA Modules:
  0.0 475.8 jit_solution(2692065483275270627)
XLA Ops:
  11.5 2.3 broadcast_select_fusion
  13.9 8.6 %all-to-all-start = ((bf16[16,512,256]{2,1,0:T(8,128)(2,1)}), bf16[16,512,256]{2,1,0:T(8,128)(2,1)}, u32[]{:S(2)}, u32[]{:S(2)}) async-start(bf16[16,512,256]{2,1,0:T(8,128)(2,1)} %broadcast_select_fusion), calls=%async_computation | async-start | bytes 8388608 | tf_op jit(solution)/shard_map/all_to_all | solution.py:119
  24.9 60.0 %all-to-all-done = bf16[16,512,256]{2,1,0:T(8,128)(2,1)} async-done(((bf16[16,512,256]{2,1,0:T(8,128)(2,1)}), bf16[16,512,256]{2,1,0:T(8,128)(2,1)}, u32[]{:S(2)}, u32[]{:S(2)}) %all-to-all-start) | async-done | bytes 4194336 | tf_op jit(solution)/shard_map/all_to_all | solution.py:119
  84.8 79.8 %while.14 = (s32[]{:T(128)}, f32[16,512,1]{1,2,0:T(1,128)S(1)}, f32[16,512,1]{1,2,0:T(1,128)S(1)}, f32[16,512,256]{2,1,0:T(8,128)}, pred[16]{0:T(512)(128)(4,1)S...) while((s32[]{:T(128)}, f32[16,512,1]{1,2,0:T(1,128)S(1)}, ...), condition=%wide.region_11.12_spmd, body=%wide.region_6.11_spmd.sunk | while | flops 270007296 | bytes 5522596 | solution.py:136
  92.9 3.8 conditional.2
  113.0 3.8 conditional.2
  113.1 1.9 fusion.53
  119.6 3.8 conditional.2
  119.6 1.9 fusion.53
  126.2 3.8 conditional.2
  126.2 1.9 fusion.53
  132.8 3.8 conditional.2
  132.8 1.9 fusion.53
  139.3 3.8 conditional.2
  139.3 1.9 fusion.53
  149.3 3.8 conditional.2
  149.3 1.9 fusion.53
  159.3 3.8 conditional.2
  164.6 10.5 %all_to_all.20 = f32[16,512,1]{1,2,0:T(1,128)S(1)} all-to-all(f32[16,512,1]{1,2,0:T(1,128)S(1)} %get-tuple-element.78), channel_id=1, replica_groups=mesh['req'=16,'tok'=8] {'req'}, dimensions={0} | all-to-all | bytes 65536 | tf_op jit(solution)/shard_map/all_to_all | solution.py:138
  175.1 9.5 %all_to_all.21 = f32[16,512,1]{1,2,0:T(1,128)S(1)} all-to-all(f32[16,512,1]{1,2,0:T(1,128)S(1)} %get-tuple-element.80), channel_id=1, replica_groups=mesh['req'=16,'tok'=8] {'req'}, dimensions={0} | all-to-all | bytes 65536 | tf_op jit(solution)/shard_map/all_to_all | solution.py:139
  184.7 4.9 %all-to-all-start.2 = ((f32[16,512,256]{2,1,0:T(8,128)}), f32[16,512,256]{2,1,0:T(8,128)}, u32[]{:S(2)}, u32[]{:S(2)}) async-start(f32[16,512,256]{2,1,0:T(8,128)} %get-tuple-element.79), calls=%async_computation.2 | async-start | bytes 16777216 | tf_op jit(solution)/shard_map/all_to_all | solution.py:140
  192.8 112.5 %all-to-all-done.2 = f32[16,512,256]{2,1,0:T(8,128)} async-done(((f32[16,512,256]{2,1,0:T(8,128)}), f32[16,512,256]{2,1,0:T(8,128)}, u32[]{:S(2)}, u32[]{:S(2)}) %all-to-all-start.2) | async-done | bytes 8388640 | tf_op jit(solution)/shard_map/all_to_all | solution.py:140
  305.3 4.1 multiply_reduce_fusion
  309.4 4.6 fusion.19
  314.3 81.0 %all-reduce.2.cloned.1.call-done = f32[512,2560]{1,0:T(8,128)} async-done(((f32[512,2560]{1,0:T(8,128)}), f32[512,2560]{1,0:T(8,128)}) %all-reduce.2.cloned.1.call-update) | async-done | bytes 5242896 | tf_op jit(solution)/shard_map/psum | solution.py:156
  395.3 3.1 multiply_reduce_fusion.2
  399.3 3.2 multiply_reduce_fusion.1
  402.6 2.3 copy-done.3
  404.9 5.1 %fusion.52 = f32[512,1280]{1,0:T(8,128)} fusion(bf16[2560,1280]{1,0:T(8,128)(2,1)S(1)} %bitcast.28, f32[512,2560]{1,0:T(8,128)S(1)} %get-tuple-element.98, f32[2560]{0:T(1024)S(1)} %copy-done.6, f32[512]{0:T(512)S(1)} %add_rsqrt_fusion), kind=kOutput, calls=%fused_computation.91 | convolution fusion | flops 3359375360 | bytes 14430208 | tf_op jit(solution)/shard_map/dot_general | solution.py:160
  410.0 17.4 %fusion.23 = f32[512,2560]{1,0:T(8,128)} fusion(bf16[1280,2560]{1,0:T(8,128)(2,1)} %param.35, bf16[2560,1280]{1,0:T(8,128)(2,1)} %param.34, f32[512,1280]{1,0:T(8,128)} %fusion.52, f32[512,2560]{1,0:T(8,128)} %copy-done.3, f32[2560]{0:T(1024)S(1)} %copy-done.6, f32[512]{0:T(512)S(1)} %add_rsqrt_fusion), kind=kOutput, calls=%fused_computation.40 | convolution fusion | flops 6721372160 | bytes 26226688 | tf_op jit(solution)/shard_map/dot_general | solution.py:164
  427.4 38.1 %reduce-scatter.2.cloned.1.call-done = f32[64,2560]{1,0:T(8,128)} async-done(((f32[512,2560]{1,0:T(8,128)}), f32[64,2560]{1,0:T(8,128)}) %reduce-scatter.2.cloned.1.call-update) | async-done | bytes 655376 | tf_op jit(solution)/shard_map/reduce_scatter | solution.py:163
  466.8 2.2 add_convert_fusion
  (152 shorter events, 75.7 us)
Async XLA Ops:
  6.5 302.9 %copy-start = (bf16[256,2560]{1,0:T(8,128)(2,1)S(1)}, bf16[256,2560]{1,0:T(8,128)(2,1)}, u32[]{:S(2)}) copy-start(bf16[256,2560]{1,0:T(8,128)(2,1)} %param.29) | copy-start | bytes 3932164
  13.8 10.3 %copy-start.8 = (s32[16]{0:T(128)S(1)}, s32[16]{0:T(128)}, u32[]{:S(2)}) copy-start(s32[16]{0:T(128)} %param.26) | copy-start | bytes 196
  13.9 71.0 %all-to-all-start = ((bf16[16,512,256]{2,1,0:T(8,128)(2,1)}), bf16[16,512,256]{2,1,0:T(8,128)(2,1)}, u32[]{:S(2)}, u32[]{:S(2)}) async-start(bf16[16,512,256]{2,1,0:T(8,128)(2,1)} %broadcast_select_fusion), calls=%async_computation | async-start | bytes 8388608 | tf_op jit(solution)/shard_map/all_to_all | solution.py:119
  184.7 5.0 %copy-start.9 = (s32[1,3]{1,0:T(1,128)S(1)}, s32[1,3]{1,0:T(1,128)}, u32[]{:S(2)}) copy-start(s32[1,3]{1,0:T(1,128)} %param.25) | copy-start | bytes 40
  184.7 6.4 %copy-start.7 = (f32[256]{0:T(256)S(1)}, f32[256]{0:T(256)}, u32[]{:S(2)}) copy-start(f32[256]{0:T(256)} %param.24) | copy-start | bytes 3076
  184.7 120.6 %all-to-all-start.2 = ((f32[16,512,256]{2,1,0:T(8,128)}), f32[16,512,256]{2,1,0:T(8,128)}, u32[]{:S(2)}, u32[]{:S(2)}) async-start(f32[16,512,256]{2,1,0:T(8,128)} %get-tuple-element.79), calls=%async_computation.2 | async-start | bytes 16777216 | tf_op jit(solution)/shard_map/all_to_all | solution.py:140
  189.6 205.7 %all-reduce.2.cloned.1.call-start = ((), (), s32[]{:S(2)}) async-start(), calls=%async_computation.5 | async-start | bytes 10485760 | tf_op jit(solution)/shard_map/psum | solution.py:156
  314.0 84.3 %copy-start.4 = (f32[2560]{0:T(1024)S(1)}, f32[2560]{0:T(1024)}, u32[]{:S(2)}) copy-start(f32[2560]{0:T(1024)} %param.30) | copy-start | bytes 30724
  314.0 151.5 %reduce-scatter.2.cloned.1.call-start = ((), (), s32[]{:S(2)}) async-start(), calls=%async_computation.6 | async-start | bytes 5898240 | tf_op jit(solution)/shard_map/reduce_scatter | solution.py:163
  395.3 4.0 copy-start.2
  395.3 9.6 %slice-start = ((s8[6553600]{0:T(1024)(128)(4,1)}), s8[4194304]{0:T(1024)(128)(4,1)S(1)}, s32[]{:S(2)}) async-start(s8[6553600]{0:T(1024)(128)(4,1)} %bitcast.27), calls=%async_computation.7 | async-start | bytes 8388608
  399.3 5.6 %slice-start.1 = ((s8[6553600]{0:T(1024)(128)(4,1)}), s8[2359296]{0:T(1024)(128)(4,1)S(1)}, s32[]{:S(2)}) async-start(s8[6553600]{0:T(1024)(128)(4,1)} %bitcast.27), calls=%async_computation.8 | async-start | bytes 4718592
  399.3 5.6 %copy-start.6 = (f32[2560]{0:T(1024)S(1)}, f32[2560]{0:T(1024)}, u32[]{:S(2)}) copy-start(f32[2560]{0:T(1024)} %param.31) | copy-start | bytes 30724
  402.5 2.3 copy-start.3
  410.0 59.0 %copy-start.1 = (bf16[256,2560]{1,0:T(8,128)(2,1)S(1)}, bf16[256,2560]{1,0:T(8,128)(2,1)}, u32[]{:S(2)}) copy-start(bf16[256,2560]{1,0:T(8,128)(2,1)} %param.29) | copy-start | bytes 3932164
  427.4 39.4 %copy-start.5 = (f32[2560]{0:T(1024)S(1)}, f32[2560]{0:T(1024)}, u32[]{:S(2)}) copy-start(f32[2560]{0:T(1024)} %param.32) | copy-start | bytes 30724
Sparse Core Ops, SparseCore 0:
  314.1 81.0 all-reduce.1
  427.6 37.9 reduce-scatter.1
where the time goes:
time: 479 us; the launch traced here: 476 us
  waiting for transfers between devices  292 us (61%)
  matrix products  51.7 us (11%)
  local copies, waits for them, and re-layouts  44.9 us (9%)
  other arithmetic  29.3 us (6%)
  blocking collectives  20.1 us (4%)
  starting transfers between devices  13.8 us (3%)
  between operations  13.6 us (3%)
  loops' own time  10.9 us (2%)
    all_to_all x1, waiting for transfers between devices, local(): lax.all_to_all(slot_out, 'req', split_axis=0, concat_axis=0, tiled=True)  112 us
    psum x1, waiting for transfers between devices, local(): lax.psum(jnp.dot(attention, w_out, preferred_element_type=jnp.float32), '...  81 us
    all_to_all x1, waiting for transfers between devices, local(): lax.all_to_all(outgoing, 'req', split_axis=0, concat_axis=0, tiled=True)  60 us
    reduce_scatter x1, waiting for transfers between devices, local(): lax.psum_scatter(jnp.dot(hidden, w_down, preferred_element_type=jnp.float...  38.1 us
    dynamic_update_slice x32, local copies, waits for them, and re-layouts, local(): slot_max, slot_sum, slot_out = lax.map(one_slot, (arrived, sender_match))  24.4 us
    dot_general x1, matrix products, local(): jnp.dot(hidden, w_down, preferred_element_type=jnp.float32)  17.4 us
    dot_general x9, matrix products, softmax_part(): jnp.einsum('...qd,kd->...qk', query_head, key_head, preferred_element_typ...  16.4 us
    all_to_all x1, blocking collectives, local(): lax.all_to_all(slot_max, 'req', split_axis=0, concat_axis=0, tiled=True)  10.5 us
  transfers between devices with their start and end apart: 4, of which 4 were waited for; matrix products, arithmetic and copies ran while one was open for 1% of the time, Pallas kernels for 0%

commit v1 on v0

v1 whole, which is shorter than its diff:
```python
import jax
import jax.numpy as jnp
from jax import lax
from jax.sharding import PartitionSpec as P

H = 8
KVH = 4
HD = 256
GROUPS = 2


EPSILON = 1e-06
MASKED = -1e30


def rms_scale(values_in, gain_vec):
    return (
        values_in
        * lax.rsqrt(jnp.mean(values_in * values_in, axis=-1, keepdims=True) + EPSILON)
        * gain_vec
    )


def norm_heads(values_in, gain_vec, head_count):
    row_count = values_in.shape[0]
    shaped = values_in.astype(jnp.float32).reshape(row_count, head_count, HD)
    return rms_scale(shaped, gain_vec).astype(jnp.bfloat16).reshape(row_count, head_count * HD)


def local(
    queries,
    suffix_kv,
    prefix_cache,
    q_gain,
    k_gain,
    lengths,
    group_of,
    owner_order,
    residual,
    w_out,
    attn_gain,
    ffn_in_gain,
    ffn_out_gain,
    w_gate,
    w_up,
    w_down,
):
    req_count = lax.axis_size("req")
    tok_count = lax.axis_size("tok")
    req_index = lax.axis_index("req")
    tok_index = lax.axis_index("tok")
    row_count = queries.shape[0]
    heads_here = queries.shape[1] // HD
    head_ratio = H // KVH
    kv_first = tok_index * heads_here // head_ratio
    kv_width = KVH * HD
    own_count = req_count // GROUPS

    with jax.named_scope("prefix_gather"):
        pref_keys = lax.dynamic_slice_in_dim(prefix_cache, kv_first * HD, HD, 1)
        pref_vals = lax.dynamic_slice_in_dim(prefix_cache, kv_width + kv_first * HD, HD, 1)
        pref_kv = jnp.concatenate([pref_keys, pref_vals], axis=1)
        gathered = lax.all_gather(pref_kv, "req", axis=0, tiled=False)
        own_group = group_of[req_index]
        owner_ids = lax.dynamic_slice_in_dim(owner_order, own_group * own_count, own_count)
        shared = jnp.take(gathered, owner_ids, axis=0).reshape(-1, 2 * HD)

    with jax.named_scope("attention"):
        query_normed = norm_heads(queries, q_gain, heads_here)
        suf_keys = norm_heads(
            lax.dynamic_slice_in_dim(suffix_kv, kv_first * HD, HD, 1), k_gain, 1
        )
        suf_vals = lax.dynamic_slice_in_dim(suffix_kv, kv_width + kv_first * HD, HD, 1)
        all_keys = jnp.concatenate([shared[:, :HD], suf_keys], axis=0)
        all_vals = jnp.concatenate([shared[:, HD:], suf_vals], axis=0)
        seg_ends = jnp.cumsum(lengths[0])
        positions = jnp.arange(row_count, dtype=jnp.int32)
        segment = jnp.sum((positions[:, None] >= seg_ends[None, :]).astype(jnp.int32), axis=1)
        causal = (segment[:, None] == segment[None, :]) & (positions[None, :] <= positions[:, None])
        visible = jnp.concatenate(
            [jnp.ones((row_count, shared.shape[0]), jnp.bool_), causal], axis=1
        )
        outputs = []
        for head_idx in range(heads_here):
            head_q = query_normed[:, head_idx * HD:(head_idx + 1) * HD]
            scores = jnp.dot(head_q, all_keys.T, preferred_element_type=jnp.float32) * HD ** (-0.5)
            scores = jnp.where(visible, scores, MASKED)
            row_max = jnp.max(scores, axis=-1, keepdims=True)
            weights = jnp.exp(scores - row_max)
            row_sum = jnp.sum(weights, axis=-1, keepdims=True)
            head_out = jnp.dot(
                weights.astype(jnp.bfloat16), all_vals, preferred_element_type=jnp.float32
            ) / row_sum
            outputs.append(head_out)
        attention = jnp.concatenate(outputs, axis=1).astype(jnp.bfloat16)

    share = row_count // tok_count
    first_row = tok_index * share
    with jax.named_scope("out_projection"):
        projected = lax.psum_scatter(
            jnp.dot(attention, w_out, preferred_element_type=jnp.float32),
            "tok",
            scatter_dimension=0,
            tiled=True,
        )
        residual_share = lax.dynamic_slice_in_dim(residual, first_row, share, 0)
        mixed_share = residual_share.astype(jnp.float32) + rms_scale(projected, attn_gain)
        normed_share = rms_scale(mixed_share, ffn_in_gain).astype(jnp.bfloat16)
        normed = lax.all_gather(normed_share, "tok", axis=0, tiled=True)
    with jax.named_scope("feed_forward"):
        gate = jnp.dot(normed, w_gate, preferred_element_type=jnp.float32)
        upward = jnp.dot(normed, w_up, preferred_element_type=jnp.float32)
        hidden = (jax.nn.gelu(gate, approximate=True) * upward).astype(jnp.bfloat16)
        down_share = lax.psum_scatter(
            jnp.dot(hidden, w_down, preferred_element_type=jnp.float32),
            "tok",
            scatter_dimension=0,
            tiled=True,
        )
    return (mixed_share + rms_scale(down_share, ffn_out_gain)).astype(jnp.bfloat16)


def solution(mesh):
    in_specs = (
        P("req", "tok"),
        P("req", None),
        P("req", None),
        P(),
        P(),
        P("req", None),
        P(),
        P(),
        P("req", None),
        P("tok", None),
        P(),
        P(),
        P(),
        P(None, "tok"),
        P(None, "tok"),
        P("tok", None),
    )
    out_specs = P(("req", "tok"), None)
    return jax.shard_map(local, mesh=mesh, in_specs=in_specs, out_specs=out_specs, check_vma=False)
```

time: 479 us -> 254 us (0.53)
  waiting for transfers between devices: 292 us -> 172 us
  local copies, waits for them, and re-layouts: 44.9 us -> 12.2 us
  blocking collectives: 20.1 us -> 0 us
  matrix products: 51.7 us -> 36.3 us
  starting transfers between devices: 13.8 us -> 0.34 us
  other arithmetic: 29.3 us -> 17.4 us
  loops' own time: 10.9 us -> 0 us
    all_to_all x2 -> x0, waiting for transfers between devices: 172 us -> none  [the longest x1 112 us: local(): lax.all_to_all(slot_out, 'req', split_axis=0, concat_axis=0, tiled=True)]
    all_gather x0 -> x2, waiting for transfers between devices: none -> 97 us  [the longest x1 68.4 us: local(): gathered = lax.all_gather(pref_kv, 'req', axis=0, tiled=False)]
    psum x1 -> x0, waiting for transfers between devices: 81 us -> none  [local(): lax.psum(jnp.dot(attention, w_out, preferred_element_type=jnp.float32), '...]
    reduce_scatter x0 -> x1, waiting for transfers between devices: none -> 37 us  [local(): lax.psum_scatter(jnp.dot(attention, w_out, preferred_element_type=jnp.flo...]
    dynamic_update_slice x32 -> x0, local copies, waits for them, and re-layouts: 24.4 us -> none  [local(): slot_max, slot_sum, slot_out = lax.map(one_slot, (arrived, sender_match))]
    dot_general x17 -> x1, matrix products: 24.6 us -> 1.57 us  [local(): jnp.dot(head_q, all_keys.T, preferred_element_type=jnp.float32)]
    all_to_all x2 -> x0, blocking collectives: 20.1 us -> none  [the longest x1 10.5 us: local(): lax.all_to_all(slot_max, 'req', split_axis=0, concat_axis=0, tiled=True)]
    all_to_all x2 -> x0, starting transfers between devices: 13.5 us -> none  [the longest x1 8.61 us: local(): lax.all_to_all(outgoing, 'req', split_axis=0, concat_axis=0, tiled=True)]
  transfers between devices with their start and end apart: 4 -> 4, of which waited for: 4 -> 4; matrix products, arithmetic and copies ran while one was open for 1% -> 2% of each run, Pallas kernels for 0% -> 0%
where the time goes in v1:
time: 254 us; the launch traced here: 252 us
  waiting for transfers between devices  172 us (68%)
  matrix products  36.3 us (14%)
  other arithmetic  17.4 us (7%)
  between operations  14 us (6%)
  local copies, waits for them, and re-layouts  12.2 us (5%)
    all_gather x1, waiting for transfers between devices, local(): gathered = lax.all_gather(pref_kv, 'req', axis=0, tiled=False)  68.4 us
    reduce_scatter x1, waiting for transfers between devices, local(): lax.psum_scatter(jnp.dot(hidden, w_down, preferred_element_type=jnp.float...  37.6 us
    reduce_scatter x1, waiting for transfers between devices, local(): lax.psum_scatter(jnp.dot(attention, w_out, preferred_element_type=jnp.flo...  37 us
    all_gather x1, waiting for transfers between devices, local(): normed = lax.all_gather(normed_share, 'tok', axis=0, tiled=True)  28.5 us
    dot_general x1, matrix products, local(): jnp.dot(hidden, w_down, preferred_element_type=jnp.float32)  16.5 us
    dot_general x1, matrix products, local(): jnp.dot(attention, w_out, preferred_element_type=jnp.float32)  9.55 us
    dot_general x1, matrix products, local(): gate = jnp.dot(normed, w_gate, preferred_element_type=jnp.float32)  8.77 us
    gather x1, local copies, waits for them, and re-layouts, local(): shared = jnp.take(gathered, owner_ids, axis=0).reshape(-1, 2 * HD)  6.17 us
  transfers between devices with their start and end apart: 4, of which 4 were waited for; matrix products, arithmetic and copies ran while one was open for 2% of the time, Pallas kernels for 0%

profile of v1, /device:TPU:1, one launch (start us, length us, event | category | flops | bytes accessed | tf_op | source)
XLA Modules:
  0.0 251.9 jit_solution(10753798629921114018)
XLA Ops:
  6.6 2.0 constant_dynamic-slice_fusion.2
  8.6 0.9 pad_maximum_fusion
  9.6 0.6 dynamic_slice.22
  10.9 0.2 reduce-window.8
  11.0 0.1 compare_and_fusion
  11.2 1.1 fusion.39
  12.3 0.1 convert_reduce_fusion
  12.4 0.1 fusion.36
  12.6 1.8 fusion.41
  14.4 0.9 fusion.19
  15.3 68.4 %all-gather.6.cloned.1.call-done = bf16[8192,512]{1,0:T(8,128)(2,1)} async-done(((bf16[512,512]{1,0:T(8,128)(2,1)}), bf16[8192,512]{1,0:T(8,128)(2,1)}) %all-gather.6.cloned.1.call-update) | async-done | bytes 8388624 | tf_op jit(solution)/shard_map/prefix_gather/all_gather | solution.py:63
  83.8 6.2 %gather_fusion = bf16[8,512,512]{2,1,0:T(8,128)(2,1)} fusion(bf16[16,512,512]{2,1,0:T(8,128)(2,1)} %bitcast.15, s32[1024]{0:T(1024)S(1)} %pad_clamp_fusion), kind=kCustom, calls=%fused_computation | custom fusion | bytes 8388640 | tf_op jit(solution)/shard_map/prefix_gather/jit(_take)/gather | solution.py:66
  89.9 2.6 %bitcast_select_fusion = bf16[4096,512]{1,0:T(8,128)(2,1)S(1)} fusion(bf16[8,512,512]{2,1,0:T(8,128)(2,1)} %gather_fusion, pred[4096]{0:T(1024)(128)(4,1)S(1)} %bitcast.16), kind=kLoop, calls=%fused_computation.7 | loop fusion | flops 2097152 | bytes 8392704 | tf_op jit(solution)/shard_map/prefix_gather/jit(_take)/select_n | solution.py:66
  92.6 0.3 fusion.53
  92.8 0.6 copy-done.4
  93.5 0.1 copy-done.6
  93.5 0.1 copy-done.7
  93.6 1.6 fusion.54
  95.2 1.4 fusion
  96.6 2.2 copy-done.2
  98.8 9.6 %fusion.32 = f32[512,2560]{1,0:T(8,128)} fusion(bf16[256,2560]{1,0:T(8,128)(2,1)S(1)} %copy-done, bf16[512,256]{1,0:T(8,128)(2,1)} %get-tuple-element.13, bf16[4096,256]{1,0:T(8,128)(2,1)S(1)} %get-tuple-element.8, f32[512,4608]{1,0:T(8,128)} %copy-done.2, f32[512]{0:T(512)S(1)} %get-tuple-element.11, f32[512]{0:T(512)S(1)} %fusion), kind=kOutput, calls=%fused_computation.28 | convolution fusion | flops 1888747520 | bytes 18354176 | tf_op jit(solution)/shard_map/out_projection/dot_general | solution.py:101
  108.5 37.0 %reduce-scatter.3.cloned.1.call-done = f32[64,2560]{1,0:T(8,128)} async-done(((f32[512,2560]{1,0:T(8,128)}), f32[64,2560]{1,0:T(8,128)}) %reduce-scatter.3.cloned.1.call-update) | async-done | bytes 655376 | tf_op jit(solution)/shard_map/out_projection/reduce_scatter | solution.py:100
  145.5 1.2 multiply_reduce_fusion.2
  146.7 1.5 multiply_reduce_fusion.1
  148.2 2.1 multiply_convert_fusion
  150.4 0.2 reduce-scatter.5.cloned.1.call-start
  150.6 28.5 %all-gather.4.cloned.1.call-done = bf16[512,2560]{1,0:T(8,128)(2,1)} async-done(((bf16[64,2560]{1,0:T(8,128)(2,1)}), bf16[512,2560]{1,0:T(8,128)(2,1)}) %all-gather.4.cloned.1.call-update) | async-done | bytes 2621456 | tf_op jit(solution)/shard_map/out_projection/all_gather | solution.py:109
  179.1 8.8 %fusion.55 = f32[512,1280]{1,0:T(8,128)} fusion(bf16[512,2560]{1,0:T(8,128)(2,1)} %all-gather.4.cloned.1.call-done, bf16[2560,1280]{1,0:T(8,128)(2,1)} %param.29), kind=kOutput, calls=%fused_computation.72 | convolution fusion | flops 3355443200 | bytes 11796480 | tf_op jit(solution)/shard_map/feed_forward/dot_general | solution.py:111
  187.9 16.5 %fusion.35 = f32[512,2560]{1,0:T(8,128)} fusion(bf16[1280,2560]{1,0:T(8,128)(2,1)} %param.31, bf16[512,2560]{1,0:T(8,128)(2,1)} %all-gather.4.cloned.1.call-done, bf16[2560,1280]{1,0:T(8,128)(2,1)} %param.30, f32[512,1280]{1,0:T(8,128)} %fusion.55), kind=kOutput, calls=%fused_computation.29 | convolution fusion | flops 6717440000 | bytes 23592960 | tf_op jit(solution)/shard_map/feed_forward/dot_general | solution.py:115
  204.4 37.6 %reduce-scatter.5.cloned.1.call-done = f32[64,2560]{1,0:T(8,128)} async-done(((f32[512,2560]{1,0:T(8,128)}), f32[64,2560]{1,0:T(8,128)}) %reduce-scatter.5.cloned.1.call-update) | async-done | bytes 655376 | tf_op jit(solution)/shard_map/feed_forward/reduce_scatter | solution.py:114
  241.9 1.2 multiply_reduce_fusion
  243.2 2.2 add_convert_fusion
  (43 shorter events, 0.4 us)
Async XLA Ops:
  6.5 92.3 %copy-start = (bf16[256,2560]{1,0:T(8,128)(2,1)S(1)}, bf16[256,2560]{1,0:T(8,128)(2,1)}, u32[]{:S(2)}) copy-start(bf16[256,2560]{1,0:T(8,128)(2,1)} %param.25) | copy-start | bytes 3932164
  6.5 3.0 %copy-start.14 = (s32[16]{0:T(128)S(1)}, s32[16]{0:T(128)}, u32[]{:S(2)}) copy-start(s32[16]{0:T(128)} %param.22) | copy-start | bytes 196
  6.5 4.3 %copy-start.15 = (s32[1,3]{1,0:T(1,128)S(1)}, s32[1,3]{1,0:T(1,128)}, u32[]{:S(2)}) copy-start(s32[1,3]{1,0:T(1,128)} %param.21) | copy-start | bytes 40
  6.5 4.5 %copy-start.12 = (s32[16]{0:T(128)S(1)}, s32[16]{0:T(128)}, u32[]{:S(2)}) copy-start(s32[16]{0:T(128)} %param.23) | copy-start | bytes 196
  6.5 5.9 %copy-start.5 = (bf16[512,256]{1,0:T(8,128)(2,1)S(1)}, bf16[512,256]{1,0:T(8,128)(2,1)}, u32[]{:S(2)}) copy-start(bf16[512,256]{1,0:T(8,128)(2,1)} %param.16) | copy-start | bytes 786436
  6.6 6.0 %copy-start.11 = (f32[256]{0:T(256)S(1)}, f32[256]{0:T(256)}, u32[]{:S(2)}) copy-start(f32[256]{0:T(256)} %param.20) | copy-start | bytes 3076
  6.6 77.2 %all-gather.6.cloned.1.call-start = ((), (), s32[]{:S(2)}) async-start(), calls=%async_computation.5 | async-start | bytes 8912896 | tf_op jit(solution)/shard_map/prefix_gather/all_gather | solution.py:63
  9.5 135.9 %reduce-scatter.3.cloned.1.call-start = ((), (), s32[]{:S(2)}) async-start(), calls=%async_computation.2 | async-start | bytes 5898240 | tf_op jit(solution)/shard_map/out_projection/reduce_scatter | solution.py:100
  92.5 1.0 copy-start.4
  92.5 1.0 copy-start.6
  92.5 1.1 copy-start.7
  92.5 1.1 copy-start.13
  95.2 3.6 %copy-start.2 = (f32[512,4608]{1,0:T(8,128)}, f32[512,4608]{1,0:T(8,128)S(1)}, u32[]{:S(2)}) copy-start(f32[512,4608]{1,0:T(8,128)S(1)} %get-tuple-element.12) | copy-start | bytes 28311556
  108.4 38.3 %copy-start.8 = (f32[2560]{0:T(1024)S(1)}, f32[2560]{0:T(1024)}, u32[]{:S(2)}) copy-start(f32[2560]{0:T(1024)} %param.26) | copy-start | bytes 30724
  108.4 39.8 %copy-start.9 = (f32[2560]{0:T(1024)S(1)}, f32[2560]{0:T(1024)}, u32[]{:S(2)}) copy-start(f32[2560]{0:T(1024)} %param.27) | copy-start | bytes 30724
  108.4 70.7 %all-gather.4.cloned.1.call-start = ((), (), s32[]{:S(2)}) async-start(), calls=%async_computation.3 | async-start | bytes 2949120 | tf_op jit(solution)/shard_map/out_projection/all_gather | solution.py:109
  150.4 91.6 %reduce-scatter.5.cloned.1.call-start = ((), (), s32[]{:S(2)}) async-start(), calls=%async_computation.4 | async-start | bytes 5898240 | tf_op jit(solution)/shard_map/feed_forward/reduce_scatter | solution.py:114
  204.3 38.8 %copy-start.3 = (f32[64,2560]{1,0:T(8,128)S(1)}, f32[64,2560]{1,0:T(8,128)}, u32[]{:S(2)}) copy-start(f32[64,2560]{1,0:T(8,128)} %reduce-scatter.3.cloned.1.call-done) | copy-start | bytes 1966084
  204.3 38.9 %copy-start.10 = (f32[2560]{0:T(1024)S(1)}, f32[2560]{0:T(1024)}, u32[]{:S(2)}) copy-start(f32[2560]{0:T(1024)} %param.28) | copy-start | bytes 30724
  204.4 41.0 %copy-start.1 = (bf16[256,2560]{1,0:T(8,128)(2,1)S(1)}, bf16[256,2560]{1,0:T(8,128)(2,1)}, u32[]{:S(2)}) copy-start(bf16[256,2560]{1,0:T(8,128)(2,1)} %param.25) | copy-start | bytes 3932164
Sparse Core Ops, SparseCore 0:
  9.6 74.0 all-gather.5
  108.5 36.8 reduce-scatter.2
  150.5 28.6 all-gather.3
  204.5 37.4 reduce-scatter.4

commit v2 on v1

--- a/solution.py
+++ b/solution.py
@@ -60,10 +60,16 @@
         pref_keys = lax.dynamic_slice_in_dim(prefix_cache, kv_first * HD, HD, 1)
         pref_vals = lax.dynamic_slice_in_dim(prefix_cache, kv_width + kv_first * HD, HD, 1)
         pref_kv = jnp.concatenate([pref_keys, pref_vals], axis=1)
-        gathered = lax.all_gather(pref_kv, "req", axis=0, tiled=False)
+        half_rows = pref_kv.shape[0] // 2
+        core = tok_index % 2
+        my_half = lax.dynamic_slice_in_dim(pref_kv, core * half_rows, half_rows, 0)
+        gathered = lax.all_gather(my_half, "req", axis=0, tiled=False)
         own_group = group_of[req_index]
         owner_ids = lax.dynamic_slice_in_dim(owner_order, own_group * own_count, own_count)
-        shared = jnp.take(gathered, owner_ids, axis=0).reshape(-1, 2 * HD)
+        picked = jnp.take(gathered, owner_ids, axis=0).reshape(-1, 2 * HD)
+        partner = [(t, t ^ 1) for t in range(tok_count)]
+        swapped = lax.ppermute(picked, "tok", perm=partner)
+        shared = jnp.concatenate([picked, swapped], axis=0)
 
     with jax.named_scope("attention"):
         query_normed = norm_heads(queries, q_gain, heads_here)
@@ -98,13 +104,15 @@
     first_row = tok_index * share
     with jax.named_scope("out_projection"):
         projected = lax.psum_scatter(
-            jnp.dot(attention, w_out, preferred_element_type=jnp.float32),
+            jnp.dot(attention, w_out, preferred_element_type=jnp.float32).astype(jnp.bfloat16),
             "tok",
             scatter_dimension=0,
             tiled=True,
         )
         residual_share = lax.dynamic_slice_in_dim(residual, first_row, share, 0)
-        mixed_share = residual_share.astype(jnp.float32) + rms_scale(projected, attn_gain)
+        mixed_share = residual_share.astype(jnp.float32) + rms_scale(
+            projected.astype(jnp.float32), attn_gain
+        )
         normed_share = rms_scale(mixed_share, ffn_in_gain).astype(jnp.bfloat16)
         normed = lax.all_gather(normed_share, "tok", axis=0, tiled=True)
     with jax.named_scope("feed_forward"):
@@ -112,12 +120,14 @@
         upward = jnp.dot(normed, w_up, preferred_element_type=jnp.float32)
         hidden = (jax.nn.gelu(gate, approximate=True) * upward).astype(jnp.bfloat16)
         down_share = lax.psum_scatter(
-            jnp.dot(hidden, w_down, preferred_element_type=jnp.float32),
+            jnp.dot(hidden, w_down, preferred_element_type=jnp.float32).astype(jnp.bfloat16),
             "tok",
             scatter_dimension=0,
             tiled=True,
         )
-    return (mixed_share + rms_scale(down_share, ffn_out_gain)).astype(jnp.bfloat16)
+    return (mixed_share + rms_scale(down_share.astype(jnp.float32), ffn_out_gain)).astype(
+        jnp.bfloat16
+    )
 
 
 def solution(mesh):

time: 254 us -> 227 us (0.89)
  waiting for transfers between devices: 172 us -> 144 us
    all_gather x1, waiting for transfers between devices: 68.4 us -> 53.2 us  [local(): gathered = lax.all_gather(my_half, 'req', axis=0, tiled=False)]
    reduce_scatter x1, waiting for transfers between devices: 37 us -> 30.9 us  [local(): lax.psum_scatter(jnp.dot(attention, w_out, preferred_element_type=jnp.flo...]
    reduce_scatter x1, waiting for transfers between devices: 37.6 us -> 32 us  [local(): lax.psum_scatter(jnp.dot(hidden, w_down, preferred_element_type=jnp.float...]
  transfers between devices with their start and end apart: 4 -> 5, of which waited for: 4 -> 4; matrix products, arithmetic and copies ran while one was open for 2% -> 3% of each run, Pallas kernels for 0% -> 0%
where the time goes in v2:
time: 227 us; the launch traced here: 224 us
  waiting for transfers between devices  144 us (63%)
  matrix products  34.8 us (15%)
  other arithmetic  17.7 us (8%)
  between operations  13.9 us (6%)
  local copies, waits for them, and re-layouts  12 us (5%)
    all_gather x1, waiting for transfers between devices, local(): gathered = lax.all_gather(my_half, 'req', axis=0, tiled=False)  53.2 us
    reduce_scatter x1, waiting for transfers between devices, local(): lax.psum_scatter(jnp.dot(hidden, w_down, preferred_element_type=jnp.float...  32 us
    reduce_scatter x1, waiting for transfers between devices, local(): lax.psum_scatter(jnp.dot(attention, w_out, preferred_element_type=jnp.flo...  30.9 us
    all_gather x1, waiting for transfers between devices, local(): normed = lax.all_gather(normed_share, 'tok', axis=0, tiled=True)  28.2 us
    dot_general x1, matrix products, local(): jnp.dot(hidden, w_down, preferred_element_type=jnp.float32)  15.6 us
    dot_general x1, matrix products, local(): jnp.dot(attention, w_out, preferred_element_type=jnp.float32)  8.88 us
    dot_general x1, matrix products, local(): gate = jnp.dot(normed, w_gate, preferred_element_type=jnp.float32)  8.71 us
    reduce_sum x5, other arithmetic, rms_scale(): jnp.mean(values_in * values_in, axis=-1, keepdims=True) + EPSILON  5.86 us
  transfers between devices with their start and end apart: 5, of which 4 were waited for; matrix products, arithmetic and copies ran while one was open for 3% of the time, Pallas kernels for 0%

profile of v2, /device:TPU:1, one launch (start us, length us, event | category | flops | bytes accessed | tf_op | source)
XLA Modules:
  0.0 223.9 jit_solution(17054381908956839786)
XLA Ops:
  6.5 1.2 constant_dynamic-slice_fusion.1
  7.7 0.7 fusion.49
  8.5 1.2 dynamic_slice.25
  10.4 0.7 compare_and_fusion
  11.1 0.1 broadcast_in_dim.20
  11.2 53.2 %all-gather.6.cloned.1.call-done = bf16[4096,512]{1,0:T(8,128)(2,1)} async-done(((bf16[256,512]{1,0:T(8,128)(2,1)}), bf16[4096,512]{1,0:T(8,128)(2,1)}) %all-gather.6.cloned.1.call-update) | async-done | bytes 4194320 | tf_op jit(solution)/shard_map/prefix_gather/all_gather | solution.py:66
  64.4 4.2 %gather_fusion = bf16[8,256,512]{2,1,0:T(8,128)(2,1)} fusion(bf16[16,256,512]{2,1,0:T(8,128)(2,1)} %bitcast.12, s32[1024]{0:T(1024)S(1)} %pad_clamp_fusion), kind=kCustom, calls=%fused_computation | custom fusion | bytes 4194336 | tf_op jit(solution)/shard_map/prefix_gather/jit(_take)/gather | solution.py:69
  68.6 1.8 bitcast_select_fusion
  70.4 0.8 collective-permute-start
  71.2 0.2 reduce-window.8
  71.3 1.1 fusion.46
  72.4 0.1 convert_reduce_fusion
  72.5 1.7 constant_dynamic-slice_fusion
  74.2 1.1 fusion.43
  75.3 1.1 fusion.48
  76.4 0.2 fusion.21
  76.7 1.4 fusion.20
  78.1 1.6 fusion.61
  79.7 3.6 %copy-done.1 = f32[512,4608]{1,0:T(8,128)} copy-done((f32[512,4608]{1,0:T(8,128)}, f32[512,4608]{1,0:T(8,128)S(1)}, u32[]{:S(2)}) %copy-start.1) | copy-done | bytes 9437208
  83.3 1.4 fusion
  84.7 8.9 %convolution_convert_fusion.1 = bf16[512,2560]{1,0:T(8,128)(2,1)} fusion(bf16[256,2560]{1,0:T(8,128)(2,1)S(1)} %copy-done, bf16[2048,512]{1,0:T(8,128)(2,1)} %collective-permute-done, bf16[2048,512]{1,0:T(8,128)(2,1)S(1)} %bitcast_select_fusion, bf16[512,256]{1,0:T(8,128)(2,1)} %constant_dynamic-slice_fusion, f32[512,4608]{1,0:T(8,128)} %copy-done.1, ...), kind=kOutput, calls=%fused_computation.8 | convolution fusion | flops 1892417536 | bytes 17829888 | tf_op jit(solution)/shard_map/out_projection/dot_general | solution.py:107
  93.7 30.9 %reduce-scatter.3.cloned.1.call-done = bf16[64,2560]{1,0:T(8,128)(2,1)} async-done(((bf16[512,2560]{1,0:T(8,128)(2,1)}), bf16[64,2560]{1,0:T(8,128)(2,1)}) %reduce-scatter.3.cloned.1.call-update) | async-done | bytes 327696 | tf_op jit(solution)/shard_map/out_projection/reduce_scatter | solution.py:106
  124.6 1.1 fusion.36
  125.8 1.4 multiply_reduce_fusion
  127.2 2.1 multiply_convert_fusion
  129.2 0.2 reduce-scatter.5.cloned.1.call-start
  129.5 28.2 %all-gather.4.cloned.1.call-done = bf16[512,2560]{1,0:T(8,128)(2,1)} async-done(((bf16[64,2560]{1,0:T(8,128)(2,1)}), bf16[512,2560]{1,0:T(8,128)(2,1)}) %all-gather.4.cloned.1.call-update) | async-done | bytes 2621456 | tf_op jit(solution)/shard_map/out_projection/all_gather | solution.py:117
  157.7 8.7 %fusion.62 = f32[512,1280]{1,0:T(8,128)} fusion(bf16[512,2560]{1,0:T(8,128)(2,1)} %all-gather.4.cloned.1.call-done, bf16[2560,1280]{1,0:T(8,128)(2,1)} %param.29), kind=kOutput, calls=%fused_computation.83 | convolution fusion | flops 3355443200 | bytes 11796480 | tf_op jit(solution)/shard_map/feed_forward/dot_general | solution.py:119
  166.4 15.6 %convolution_convert_fusion = bf16[512,2560]{1,0:T(8,128)(2,1)} fusion(bf16[1280,2560]{1,0:T(8,128)(2,1)} %param.31, bf16[512,2560]{1,0:T(8,128)(2,1)} %all-gather.4.cloned.1.call-done, bf16[2560,1280]{1,0:T(8,128)(2,1)} %param.30, f32[512,1280]{1,0:T(8,128)} %fusion.62), kind=kOutput, calls=%fused_computation.7 | convolution fusion | flops 6718750720 | bytes 20971520 | tf_op jit(solution)/shard_map/feed_forward/dot_general | solution.py:123
  182.1 32.0 %reduce-scatter.5.cloned.1.call-done = bf16[64,2560]{1,0:T(8,128)(2,1)} async-done(((bf16[512,2560]{1,0:T(8,128)(2,1)}), bf16[64,2560]{1,0:T(8,128)(2,1)}) %reduce-scatter.5.cloned.1.call-update) | async-done | bytes 327696 | tf_op jit(solution)/shard_map/feed_forward/reduce_scatter | solution.py:122
  214.1 1.1 fusion.39
  215.3 2.1 fusion.42
  (34 shorter events, 0.2 us)
Async XLA Ops:
  6.5 78.2 %copy-start = (bf16[256,2560]{1,0:T(8,128)(2,1)S(1)}, bf16[256,2560]{1,0:T(8,128)(2,1)}, u32[]{:S(2)}) copy-start(bf16[256,2560]{1,0:T(8,128)(2,1)} %param.25) | copy-start | bytes 3932164
  6.5 57.9 %all-gather.6.cloned.1.call-start = ((), (), s32[]{:S(2)}) async-start(), calls=%async_computation.5 | async-start | bytes 4456448 | tf_op jit(solution)/shard_map/prefix_gather/all_gather | solution.py:66
  8.5 116.1 %reduce-scatter.3.cloned.1.call-start = ((), (), s32[]{:S(2)}) async-start(), calls=%async_computation.2 | async-start | bytes 2949120 | tf_op jit(solution)/shard_map/out_projection/reduce_scatter | solution.py:106
  68.6 2.6 %copy-start.9 = (s32[1,3]{1,0:T(1,128)S(1)}, s32[1,3]{1,0:T(1,128)}, u32[]{:S(2)}) copy-start(s32[1,3]{1,0:T(1,128)} %param.21) | copy-start | bytes 40
  68.6 6.7 %copy-start.7 = (f32[256]{0:T(256)S(1)}, f32[256]{0:T(256)}, u32[]{:S(2)}) copy-start(f32[256]{0:T(256)} %param.20) | copy-start | bytes 3076
  70.4 6.3 %collective-permute-start = (bf16[2048,512]{1,0:T(8,128)(2,1)S(1)}, bf16[2048,512]{1,0:T(8,128)(2,1)}, u32[]{:S(2)}, u32[]{:S(2)}) collective-permute-start(bf16[2048,512]{1,0:T(8,128)(2,1)S(1)} %bitcast_select_fusion), channel_id=1, source_target_pairs={{0,1},{1,0},{2,3},{3,2},{4,5},{5,4},{6,7},{7,6},{8,9},{9,8},{10,11... | collective-permute-start | bytes 6291464 | tf_op jit(solution)/shard_map/prefix_gather/ppermute | solution.py:71
  76.6 1.4 copy-start.3
  76.7 1.4 copy-start.8
  79.7 3.6 %copy-start.1 = (f32[512,4608]{1,0:T(8,128)}, f32[512,4608]{1,0:T(8,128)S(1)}, u32[]{:S(2)}) copy-start(f32[512,4608]{1,0:T(8,128)S(1)} %get-tuple-element.10) | copy-start | bytes 28311556
  93.6 32.2 %copy-start.4 = (f32[2560]{0:T(1024)S(1)}, f32[2560]{0:T(1024)}, u32[]{:S(2)}) copy-start(f32[2560]{0:T(1024)} %param.26) | copy-start | bytes 30724
  93.6 33.6 %copy-start.5 = (f32[2560]{0:T(1024)S(1)}, f32[2560]{0:T(1024)}, u32[]{:S(2)}) copy-start(f32[2560]{0:T(1024)} %param.27) | copy-start | bytes 30724
  93.6 64.1 %all-gather.4.cloned.1.call-start = ((), (), s32[]{:S(2)}) async-start(), calls=%async_computation.3 | async-start | bytes 2949120 | tf_op jit(solution)/shard_map/out_projection/all_gather | solution.py:117
  129.2 84.8 %reduce-scatter.5.cloned.1.call-start = ((), (), s32[]{:S(2)}) async-start(), calls=%async_computation.4 | async-start | bytes 2949120 | tf_op jit(solution)/shard_map/feed_forward/reduce_scatter | solution.py:122
  182.0 33.2 %copy-start.2 = (bf16[64,2560]{1,0:T(8,128)(2,1)S(1)}, bf16[64,2560]{1,0:T(8,128)(2,1)}, u32[]{:S(2)}) copy-start(bf16[64,2560]{1,0:T(8,128)(2,1)} %reduce-scatter.3.cloned.1.call-done) | copy-start | bytes 983044
  182.0 33.2 %copy-start.6 = (f32[2560]{0:T(1024)S(1)}, f32[2560]{0:T(1024)}, u32[]{:S(2)}) copy-start(f32[2560]{0:T(1024)} %param.28) | copy-start | bytes 30724
Sparse Core Ops, SparseCore 0:
  9.5 54.8 all-gather.5
  93.7 30.8 reduce-scatter.2
  129.4 28.2 all-gather.3
  182.2 31.8 reduce-scatter.4

commit v3 on v2

--- a/solution.py
+++ b/solution.py
@@ -2,6 +2,8 @@
 import jax.numpy as jnp
 from jax import lax
 from jax.sharding import PartitionSpec as P
+from jax.experimental import pallas as pl
+from jax.experimental.pallas import tpu as pltpu
 
 H = 8
 KVH = 4
@@ -25,6 +27,87 @@
     row_count = values_in.shape[0]
     shaped = values_in.astype(jnp.float32).reshape(row_count, head_count, HD)
     return rms_scale(shaped, gain_vec).astype(jnp.bfloat16).reshape(row_count, head_count * HD)
+
+
+def gather_tok_kernel(tok_count, w_ref, out_ref, send_sem, recv_sem, local_sem):
+    mesh_ids = pl.DeviceIdType.MESH
+    me = lax.axis_index("tok")
+    up = lax.rem(me + 2, tok_count)
+    down = lax.rem(me + tok_count - 2, tok_count)
+    far = lax.rem(me + 4, tok_count)
+    partner = me + 1 - 2 * lax.rem(me, 2)
+    half = w_ref.shape[0] // 2
+
+    barrier = pltpu.get_barrier_semaphore()
+    for peer in (up, down, partner):
+        pl.semaphore_signal(barrier, inc=1, device_id={"tok": peer}, device_id_type=mesh_ids)
+    pl.semaphore_wait(barrier, 3)
+
+    def remote(src, dst, slot, peer):
+        return pltpu.make_async_remote_copy(
+            src_ref=src,
+            dst_ref=dst,
+            send_sem=send_sem.at[slot],
+            recv_sem=recv_sem.at[slot],
+            device_id={"tok": peer},
+            device_id_type=mesh_ids,
+        )
+
+    local = pltpu.make_async_copy(w_ref, out_ref.at[me], local_sem.at[0])
+    local.start()
+    to_up = remote(w_ref, out_ref.at[me], 0, up)
+    to_down = remote(w_ref, out_ref.at[me], 1, down)
+    to_up.start()
+    to_down.start()
+    remote(w_ref, out_ref.at[down], 0, down).wait_recv()
+    remote(w_ref, out_ref.at[up], 1, up).wait_recv()
+
+    first = pl.ds(0, half)
+    second = pl.ds(half, half)
+    fwd_up = remote(out_ref.at[down, first], out_ref.at[down, first], 2, up)
+    fwd_down = remote(out_ref.at[up, second], out_ref.at[up, second], 3, down)
+    fwd_up.start()
+    fwd_down.start()
+    remote(out_ref.at[far, first], out_ref.at[far, first], 2, down).wait_recv()
+    remote(out_ref.at[far, second], out_ref.at[far, second], 3, up).wait_recv()
+    local.wait()
+
+    mine = (me, up, down, far)
+    theirs = (
+        partner,
+        lax.rem(partner + 2, tok_count),
+        lax.rem(partner + tok_count - 2, tok_count),
+        lax.rem(partner + 4, tok_count),
+    )
+    to_partner = []
+    for idx, slot in enumerate(mine):
+        copy = remote(out_ref.at[slot], out_ref.at[slot], 4 + idx, partner)
+        copy.start()
+        to_partner.append(copy)
+    for idx, slot in enumerate(theirs):
+        remote(out_ref.at[slot], out_ref.at[slot], 4 + idx, partner).wait_recv()
+    for copy in [to_up, to_down, fwd_up, fwd_down] + to_partner:
+        copy.wait_send()
+
+
+def gather_over_tok(block, tok_count):
+    assert tok_count == 8
+    rows, cols = block.shape
+    return pl.pallas_call(
+        lambda *refs: gather_tok_kernel(tok_count, *refs),
+        out_shape=jax.ShapeDtypeStruct((tok_count, rows, cols), block.dtype),
+        in_specs=[pl.BlockSpec(memory_space=pl.ANY)],
+        out_specs=pl.BlockSpec(memory_space=pl.ANY),
+        scratch_shapes=[
+            pltpu.SemaphoreType.DMA((8,)),
+            pltpu.SemaphoreType.DMA((8,)),
+            pltpu.SemaphoreType.DMA((1,)),
+        ],
+        compiler_params=pltpu.CompilerParams(collective_id=0, has_side_effects=True),
+        cost_estimate=pl.CostEstimate(
+            flops=0, transcendentals=0, bytes_accessed=2 * tok_count * rows * cols * 2
+        ),
+    )(block)
 
 
 def local(
@@ -64,6 +147,8 @@
         core = tok_index % 2
         my_half = lax.dynamic_slice_in_dim(pref_kv, core * half_rows, half_rows, 0)
         gathered = lax.all_gather(my_half, "req", axis=0, tiled=False)
+        w_out_all = gather_over_tok(w_out, tok_count).reshape(-1, w_out.shape[1])
+        gathered, w_out_all = lax.optimization_barrier((gathered, w_out_all))
         own_group = group_of[req_index]
         owner_ids = lax.dynamic_slice_in_dim(owner_order, own_group * own_count, own_count)
         picked = jnp.take(gathered, owner_ids, axis=0).reshape(-1, 2 * HD)
@@ -103,18 +188,11 @@
     share = row_count // tok_count
     first_row = tok_index * share
     with jax.named_scope("out_projection"):
-        projected = lax.psum_scatter(
-            jnp.dot(attention, w_out, preferred_element_type=jnp.float32).astype(jnp.bfloat16),
-            "tok",
-            scatter_dimension=0,
-            tiled=True,
-        )
-        residual_share = lax.dynamic_slice_in_dim(residual, first_row, share, 0)
-        mixed_share = residual_share.astype(jnp.float32) + rms_scale(
-            projected.astype(jnp.float32), attn_gain
-        )
-        normed_share = rms_scale(mixed_share, ffn_in_gain).astype(jnp.bfloat16)
-        normed = lax.all_gather(normed_share, "tok", axis=0, tiled=True)
+        attention_all = lax.all_gather(attention, "tok", axis=1, tiled=True)
+        projected = jnp.dot(attention_all, w_out_all, preferred_element_type=jnp.float32)
+        mixed_rows = residual.astype(jnp.float32) + rms_scale(projected, attn_gain)
+        normed = rms_scale(mixed_rows, ffn_in_gain).astype(jnp.bfloat16)
+        mixed_share = lax.dynamic_slice_in_dim(mixed_rows, first_row, share, 0)
     with jax.named_scope("feed_forward"):
         gate = jnp.dot(normed, w_gate, preferred_element_type=jnp.float32)
         upward = jnp.dot(normed, w_up, preferred_element_type=jnp.float32)

time: 227 us -> 198 us (0.87)
  waiting for transfers between devices: 144 us -> 60.5 us
  Pallas kernels: 0 us -> 59.5 us
  other arithmetic: 17.7 us -> 12.6 us
  matrix products: 34.8 us -> 38.7 us
    pallas_call x0 -> x1, Pallas kernels: none -> 59.5 us  [gather_over_tok(): pl.pallas_call(lambda *refs: gather_tok_kernel(tok_count, *refs), out_sha...]
    all_gather x1, waiting for transfers between devices: 53.2 us -> 0.02 us  [local(): gathered = lax.all_gather(my_half, 'req', axis=0, tiled=False)]
    reduce_scatter x1 -> x0, waiting for transfers between devices: 30.9 us -> none  [local(): lax.psum_scatter(jnp.dot(attention, w_out, preferred_element_type=jnp.flo...]
    dot_general x1 -> x2, matrix products: 8.88 us -> 12.6 us  [the longest x1 9.17 us: local(): jnp.dot(attention_all, w_out_all, preferred_element_type=jnp.float32)]
    reduce_sum x5 -> x4, other arithmetic: 5.86 us -> 3.6 us  [rms_scale(): jnp.mean(values_in * values_in, axis=-1, keepdims=True) + EPSILON]
  transfers between devices with their start and end apart: 5 -> 4, of which waited for: 4 -> 3; matrix products, arithmetic and copies ran while one was open for 3% -> 3% of each run, Pallas kernels for 0% -> 30%
where the time goes in v3:
time: 198 us; the launch traced here: 196 us
  waiting for transfers between devices  60.5 us (31%)
  Pallas kernels  59.5 us (30%)
  matrix products  38.7 us (20%)
  between operations  14 us (7%)
  other arithmetic  12.6 us (6%)
  local copies, waits for them, and re-layouts  10 us (5%)
    pallas_call x1, Pallas kernels, gather_over_tok(): pl.pallas_call(lambda *refs: gather_tok_kernel(tok_count, *refs), out_sha...  59.5 us
    reduce_scatter x1, waiting for transfers between devices, local(): lax.psum_scatter(jnp.dot(hidden, w_down, preferred_element_type=jnp.float...  32.3 us
    all_gather x1, waiting for transfers between devices, local(): attention_all = lax.all_gather(attention, 'tok', axis=1, tiled=True)  27.7 us
    dot_general x1, matrix products, local(): jnp.dot(hidden, w_down, preferred_element_type=jnp.float32)  16.5 us
    dot_general x1, matrix products, local(): jnp.dot(attention_all, w_out_all, preferred_element_type=jnp.float32)  9.17 us
    dot_general x1, matrix products, local(): gate = jnp.dot(normed, w_gate, preferred_element_type=jnp.float32)  8.08 us
    gather x1, local copies, waits for them, and re-layouts, local(): picked = jnp.take(gathered, owner_ids, axis=0).reshape(-1, 2 * HD)  4.24 us
  transfers between devices with their start and end apart: 4, of which 3 were waited for; matrix products, arithmetic and copies ran while one was open for 3% of the time, Pallas kernels for 30%

profile of v3, /device:TPU:1, one launch (start us, length us, event | category | flops | bytes accessed | tf_op | source)
XLA Modules:
  0.0 195.8 jit_solution(18317804320470221683)
XLA Ops:
  6.5 1.1 constant_dynamic-slice_fusion.1
  7.6 0.7 fusion.42
  8.4 0.0 all-gather.4.cloned.1.call-start
  8.4 1.3 dynamic_slice.24
  10.4 59.5 %prefix_gather.1 = bf16[8,256,2560]{2,1,0:T(8,128)(2,1)} custom-call(bf16[256,2560]{1,0:T(8,128)(2,1)} %refs_0_.1), custom_call_target="tpu_custom_call" | custom-call | bytes 20971520 | tf_op jit(solution)/shard_map/prefix_gather/pallas_call | solution.py:96
  69.9 0.1 compare_and_fusion
  70.0 0.1 broadcast_in_dim.20
  70.2 4.2 %gather_fusion = bf16[8,256,512]{2,1,0:T(8,128)(2,1)} fusion(bf16[16,256,512]{2,1,0:T(8,128)(2,1)} %bitcast.13, s32[1024]{0:T(1024)S(1)} %pad_clamp_fusion), kind=kCustom, calls=%fused_computation | custom fusion | bytes 4194336 | tf_op jit(solution)/shard_map/prefix_gather/jit(_take)/gather | solution.py:154
  74.4 1.8 bitcast_select_fusion
  76.2 0.2 collective-permute-start
  76.4 0.2 reduce-window.8
  76.6 1.1 fusion.39
  77.7 0.1 convert_reduce_fusion
  77.8 1.0 constant_dynamic-slice_fusion
  78.7 0.1 fusion.36
  78.9 1.1 fusion.41
  80.0 0.2 fusion.21
  80.2 0.3 collective-permute-done
  80.6 1.4 fusion.20
  81.9 1.6 fusion.53
  83.5 1.4 fusion
  84.9 3.4 %fusion.27 = bf16[512,256]{1,0:T(8,128)(2,1)} fusion(bf16[2048,512]{1,0:T(8,128)(2,1)} %collective-permute-done, bf16[2048,512]{1,0:T(8,128)(2,1)S(1)} %bitcast_select_fusion, bf16[512,256]{1,0:T(8,128)(2,1)S(1)} %constant_dynamic-slice_fusion, f32[512,4608]{1,0:T(8,128)S(1)} %get-tuple-element.16, f32[512]{0:T(512)S(1)} %get-tuple-element.15, f32[512]{0:T(512)S(1)} %fusion), kind=kOutput, calls=%fused_computation.36 | convolution fusion | flops 1220018176 | bytes 14159872 | tf_op jit(solution)/shard_map/attention/dot_general | solution.py:182
  88.4 0.2 reduce-scatter.2.cloned.1.call-start
  88.6 27.7 %all-gather.4.cloned.1.call-done = bf16[512,2048]{1,0:T(8,128)(2,1)} async-done(((bf16[512,256]{1,0:T(8,128)(2,1)}), bf16[512,2048]{1,0:T(8,128)(2,1)}) %all-gather.4.cloned.1.call-update) | async-done | bytes 2097168 | tf_op jit(solution)/shard_map/out_projection/all_gather | solution.py:191
  116.3 9.2 %multiply_reduce_fusion.1 = (f32[512]{0:T(512)S(1)}, f32[512,2560]{1,0:T(8,128)S(1)}) fusion(bf16[512,2048]{1,0:T(8,128)(2,1)} %all-gather.4.cloned.1.call-done, bf16[2048,2560]{1,0:T(8,128)(2,1)} %bitcast.12), kind=kOutput, calls=%fused_computation.8 | convolution fusion | flops 5371330048 | bytes 17827840 | tf_op jit(solution)/shard_map/out_projection/dot_general | solution.py:192
  125.5 1.2 multiply_reduce_fusion
  126.8 2.3 %copy-done = f32[512,2560]{1,0:T(8,128)} copy-done((f32[512,2560]{1,0:T(8,128)}, f32[512,2560]{1,0:T(8,128)S(1)}, u32[]{:S(2)}) %copy-start) | copy-done | bytes 5242904
  129.1 8.1 %fusion.52 = f32[512,1280]{1,0:T(8,128)} fusion(bf16[2560,1280]{1,0:T(8,128)(2,1)} %param.29, f32[512,2560]{1,0:T(8,128)S(1)} %get-tuple-element.10, f32[2560]{0:T(1024)S(1)} %copy-done.7, f32[512]{0:T(512)S(1)} %add_rsqrt_fusion), kind=kOutput, calls=%fused_computation.77 | convolution fusion | flops 3359375360 | bytes 14430208 | tf_op jit(solution)/shard_map/feed_forward/dot_general | solution.py:197
  137.2 16.5 %convolution_convert_fusion = bf16[512,2560]{1,0:T(8,128)(2,1)} fusion(bf16[1280,2560]{1,0:T(8,128)(2,1)} %param.31, bf16[2560,1280]{1,0:T(8,128)(2,1)} %param.30, f32[512,1280]{1,0:T(8,128)} %fusion.52, f32[512,2560]{1,0:T(8,128)} %copy-done, f32[2560]{0:T(1024)S(1)} %copy-done.7, f32[512]{0:T(512)S(1)} %add_rsqrt_fusion), kind=kOutput, calls=%fused_computation.11 | convolution fusion | flops 6722682880 | bytes 23605248 | tf_op jit(solution)/shard_map/feed_forward/dot_general | solution.py:201
  153.7 32.3 %reduce-scatter.2.cloned.1.call-done = bf16[64,2560]{1,0:T(8,128)(2,1)} async-done(((bf16[512,2560]{1,0:T(8,128)(2,1)}), bf16[64,2560]{1,0:T(8,128)(2,1)}) %reduce-scatter.2.cloned.1.call-update) | async-done | bytes 327696 | tf_op jit(solution)/shard_map/feed_forward/reduce_scatter | solution.py:200
  186.0 1.1 fusion.32
  187.2 2.1 %fusion.35 = bf16[64,2560]{1,0:T(8,128)(2,1)} fusion(bf16[64,2560]{1,0:T(8,128)(2,1)} %reduce-scatter.2.cloned.1.call-done, f32[512,2560]{1,0:T(8,128)} %copy-done, s32[]{:T(128)S(6)} %select_n.55, f32[2560]{0:T(1024)S(1)} %copy-done.4, f32[64]{0:T(128)S(1)} %add_rsqrt_fusion.4), kind=kLoop, calls=%fused_computation.46 | loop fusion | flops 819200 | bytes 1321220 | tf_op jit(solution)/shard_map/convert_element_type | solution.py:206
  (31 shorter events, 0.2 us)
Async XLA Ops:
  6.5 63.6 %all-gather.6.cloned.1.call-start = ((), (), s32[]{:S(2)}) async-start(), calls=%async_computation.3 | async-start | bytes 4456448 | tf_op jit(solution)/shard_map/prefix_gather/all_gather | solution.py:149
  8.4 107.9 %all-gather.4.cloned.1.call-start = ((), (), s32[]{:S(2)}) async-start(), calls=%async_computation.1 | async-start | bytes 2359296 | tf_op jit(solution)/shard_map/out_projection/all_gather | solution.py:191
  10.4 59.5 %copy-start.6 = (s32[16]{0:T(128)S(1)}, s32[16]{0:T(128)}, u32[]{:S(2)}) copy-start(s32[16]{0:T(128)} %param.23) | copy-start | bytes 196
  70.1 6.3 %copy-start.9 = (s32[1,3]{1,0:T(1,128)S(1)}, s32[1,3]{1,0:T(1,128)}, u32[]{:S(2)}) copy-start(s32[1,3]{1,0:T(1,128)} %param.21) | copy-start | bytes 40
  70.1 8.6 %copy-start.2 = (bf16[512,256]{1,0:T(8,128)(2,1)S(1)}, bf16[512,256]{1,0:T(8,128)(2,1)}, u32[]{:S(2)}) copy-start(bf16[512,256]{1,0:T(8,128)(2,1)} %param.16) | copy-start | bytes 786436
  70.2 8.8 %copy-start.5 = (f32[256]{0:T(256)S(1)}, f32[256]{0:T(256)}, u32[]{:S(2)}) copy-start(f32[256]{0:T(256)} %param.20) | copy-start | bytes 3076
  76.2 5.7 %copy-start.8 = (f32[256]{0:T(256)S(1)}, f32[256]{0:T(256)}, u32[]{:S(2)}) copy-start(f32[256]{0:T(256)} %param.19) | copy-start | bytes 3076
  76.2 4.4 %collective-permute-start = (bf16[2048,512]{1,0:T(8,128)(2,1)S(1)}, bf16[2048,512]{1,0:T(8,128)(2,1)}, u32[]{:S(2)}, u32[]{:S(2)}) collective-permute-start(bf16[2048,512]{1,0:T(8,128)(2,1)S(1)} %bitcast_select_fusion), channel_id=1, source_target_pairs={{0,1},{1,0},{2,3},{3,2},{4,5},{5,4},{6,7},{7,6},{8,9},{9,8},{10,11... | collective-permute-start | bytes 6291464 | tf_op jit(solution)/shard_map/prefix_gather/ppermute | solution.py:156
  88.3 37.2 %copy-start.1 = (bf16[512,2560]{1,0:T(8,128)(2,1)S(1)}, bf16[512,2560]{1,0:T(8,128)(2,1)}, u32[]{:S(2)}) copy-start(bf16[512,2560]{1,0:T(8,128)(2,1)} %param.24) | copy-start | bytes 7864324
  88.3 37.2 %copy-start.3 = (f32[2560]{0:T(1024)S(1)}, f32[2560]{0:T(1024)}, u32[]{:S(2)}) copy-start(f32[2560]{0:T(1024)} %param.26) | copy-start | bytes 30724
  88.4 97.7 %reduce-scatter.2.cloned.1.call-start = ((), (), s32[]{:S(2)}) async-start(), calls=%async_computation.2 | async-start | bytes 2949120 | tf_op jit(solution)/shard_map/feed_forward/reduce_scatter | solution.py:200
  125.5 3.6 %copy-start.7 = (f32[2560]{0:T(1024)S(1)}, f32[2560]{0:T(1024)}, u32[]{:S(2)}) copy-start(f32[2560]{0:T(1024)} %param.27) | copy-start | bytes 30724
  126.8 2.3 %copy-start = (f32[512,2560]{1,0:T(8,128)}, f32[512,2560]{1,0:T(8,128)S(1)}, u32[]{:S(2)}) copy-start(f32[512,2560]{1,0:T(8,128)S(1)} %get-tuple-element.10) | copy-start | bytes 15728644
  137.2 50.0 %copy-start.4 = (f32[2560]{0:T(1024)S(1)}, f32[2560]{0:T(1024)}, u32[]{:S(2)}) copy-start(f32[2560]{0:T(1024)} %param.28) | copy-start | bytes 30724
Sparse Core Ops, SparseCore 0:
  9.5 54.8 all-gather.5
  88.4 27.8 all-gather.3
  153.8 32.1 reduce-scatter.1

commit v4 on v3

--- a/solution.py
+++ b/solution.py
@@ -90,7 +90,7 @@
         copy.wait_send()
 
 
-def gather_over_tok(block, tok_count):
+def gather_over_tok(block, tok_count, collective_id):
     assert tok_count == 8
     rows, cols = block.shape
     return pl.pallas_call(
@@ -103,7 +103,7 @@
             pltpu.SemaphoreType.DMA((8,)),
             pltpu.SemaphoreType.DMA((1,)),
         ],
-        compiler_params=pltpu.CompilerParams(collective_id=0, has_side_effects=True),
+        compiler_params=pltpu.CompilerParams(collective_id=collective_id, has_side_effects=True),
         cost_estimate=pl.CostEstimate(
             flops=0, transcendentals=0, bytes_accessed=2 * tok_count * rows * cols * 2
         ),
@@ -147,7 +147,7 @@
         core = tok_index % 2
         my_half = lax.dynamic_slice_in_dim(pref_kv, core * half_rows, half_rows, 0)
         gathered = lax.all_gather(my_half, "req", axis=0, tiled=False)
-        w_out_all = gather_over_tok(w_out, tok_count).reshape(-1, w_out.shape[1])
+        w_out_all = gather_over_tok(w_out, tok_count, 0)
         gathered, w_out_all = lax.optimization_barrier((gathered, w_out_all))
         own_group = group_of[req_index]
         owner_ids = lax.dynamic_slice_in_dim(owner_order, own_group * own_count, own_count)
@@ -188,8 +188,10 @@
     share = row_count // tok_count
     first_row = tok_index * share
     with jax.named_scope("out_projection"):
-        attention_all = lax.all_gather(attention, "tok", axis=1, tiled=True)
-        projected = jnp.dot(attention_all, w_out_all, preferred_element_type=jnp.float32)
+        attention_all = gather_over_tok(attention, tok_count, 1)
+        projected = jnp.einsum(
+            "srd,sdc->rc", attention_all, w_out_all, preferred_element_type=jnp.float32
+        )
         mixed_rows = residual.astype(jnp.float32) + rms_scale(projected, attn_gain)
         normed = rms_scale(mixed_rows, ffn_in_gain).astype(jnp.bfloat16)
         mixed_share = lax.dynamic_slice_in_dim(mixed_rows, first_row, share, 0)

time: 198 us -> 187 us (0.944)
  waiting for transfers between devices: 60.5 us -> 33 us
  Pallas kernels: 59.5 us -> 77.2 us
  matrix products: 38.7 us -> 36.7 us
    all_gather x1 -> x0, waiting for transfers between devices: 27.7 us -> none  [local(): attention_all = lax.all_gather(attention, 'tok', axis=1, tiled=True)]
    pallas_call x1 -> x2, Pallas kernels: 59.5 us -> 77.2 us  [gather_over_tok(): pl.pallas_call(lambda *refs: gather_tok_kernel(tok_count, *refs), out_sha...]
  transfers between devices with their start and end apart: 4 -> 3, of which waited for: 3 -> 2; matrix products, arithmetic and copies ran while one was open for 3% -> 3% of each run, Pallas kernels for 30% -> 32%
where the time goes in v4:
time: 187 us; the launch traced here: 184 us
  Pallas kernels  77.2 us (41%)
  matrix products  36.7 us (20%)
  waiting for transfers between devices  33 us (18%)
  between operations  14.3 us (8%)
  other arithmetic  12.6 us (7%)
  local copies, waits for them, and re-layouts  10 us (5%)
    pallas_call x2, Pallas kernels, gather_over_tok(): pl.pallas_call(lambda *refs: gather_tok_kernel(tok_count, *refs), out_sha...  77.2 us
    reduce_scatter x1, waiting for transfers between devices, local(): lax.psum_scatter(jnp.dot(hidden, w_down, preferred_element_type=jnp.float...  32.7 us
    dot_general x1, matrix products, local(): jnp.dot(hidden, w_down, preferred_element_type=jnp.float32)  15.7 us
    dot_general x1, matrix products, local(): jnp.einsum('srd,sdc->rc', attention_all, w_out_all, preferred_element_typ...  9.5 us
    dot_general x1, matrix products, local(): gate = jnp.dot(normed, w_gate, preferred_element_type=jnp.float32)  6.5 us
    gather x1, local copies, waits for them, and re-layouts, local(): picked = jnp.take(gathered, owner_ids, axis=0).reshape(-1, 2 * HD)  4.24 us
  transfers between devices with their start and end apart: 3, of which 2 were waited for; matrix products, arithmetic and copies ran while one was open for 3% of the time, Pallas kernels for 32%

profile of v4, /device:TPU:1, one launch (start us, length us, event | category | flops | bytes accessed | tf_op | source)
XLA Modules:
  0.0 184.0 jit_solution(11292555682403450345)
XLA Ops:
  6.5 1.1 constant_dynamic-slice_fusion.1
  7.6 0.7 fusion.45
  8.4 0.0 reduce-scatter.2.cloned.1.call-start
  8.4 1.3 dynamic_slice.24
  10.4 59.5 %prefix_gather.1 = bf16[8,256,2560]{2,1,0:T(8,128)(2,1)} custom-call(bf16[256,2560]{1,0:T(8,128)(2,1)} %refs_0_.1), custom_call_target="tpu_custom_call" | custom-call | bytes 20971520 | tf_op jit(solution)/shard_map/prefix_gather/pallas_call | solution.py:96
  69.9 0.1 compare_and_fusion
  70.0 0.1 broadcast_in_dim.20
  70.1 0.0 all-gather.3.cloned.1.call-done
  70.2 4.2 %gather_fusion = bf16[8,256,512]{2,1,0:T(8,128)(2,1)} fusion(bf16[16,256,512]{2,1,0:T(8,128)(2,1)} %bitcast.21, s32[1024]{0:T(1024)S(1)} %pad_clamp_fusion), kind=kCustom, calls=%fused_computation | custom fusion | bytes 4194336 | tf_op jit(solution)/shard_map/prefix_gather/jit(_take)/gather | solution.py:154
  74.4 1.8 bitcast_select_fusion
  76.2 0.2 collective-permute-start
  76.4 0.2 reduce-window.8
  76.6 1.1 fusion.42
  77.7 0.1 convert_reduce_fusion
  77.8 1.0 constant_dynamic-slice_fusion
  78.7 0.1 fusion.39
  78.9 1.1 fusion.44
  80.0 0.2 fusion.24
  80.2 0.3 collective-permute-done
  80.6 1.4 fusion.23
  81.9 1.6 fusion.57
  83.5 1.4 fusion
  84.9 3.4 %fusion.30.refs_0_ = bf16[512,256]{1,0:T(8,128)(2,1)} fusion(bf16[2048,512]{1,0:T(8,128)(2,1)} %collective-permute-done, bf16[2048,512]{1,0:T(8,128)(2,1)S(1)} %bitcast_select_fusion, bf16[512,256]{1,0:T(8,128)(2,1)S(1)} %constant_dynamic-slice_fusion, f32[512,4608]{1,0:T(8,128)S(1)} %get-tuple-element.16, f32[512]{0:T(512)S(1)} %get-tuple-element.15, ...), kind=kOutput, calls=%fused_computation.39 | convolution fusion | flops 1220018176 | bytes 14159872 | tf_op jit(solution)/shard_map/attention/dot_general | solution.py:182
  88.3 17.7 %out_projection.1 = bf16[8,512,256]{2,1,0:T(8,128)(2,1)} custom-call(bf16[512,256]{1,0:T(8,128)(2,1)} %fusion.30.refs_0_), custom_call_target="tpu_custom_call" | custom-call | bytes 4194304 | tf_op jit(solution)/shard_map/out_projection/pallas_call | solution.py:96
  106.0 9.5 %fusion.2 = (f32[512]{0:T(512)S(1)}, f32[512,2560,1]{1,0,2:T(8,128)S(1)}) fusion(bf16[8,512,256]{2,1,0:T(8,128)(2,1)} %out_projection.1, bf16[8,256,2560]{2,1,0:T(8,128)(2,1)} %prefix_gather.1), kind=kOutput, calls=%fused_computation.7 | convolution fusion | flops 5371330048 | bytes 17827840 | tf_op jit(solution)/shard_map/out_projection/srd,sdc->rc/dot_general | solution.py:192
  115.5 1.2 multiply_reduce_fusion
  116.7 2.3 %copy-done = f32[512,2560]{1,0:T(8,128)} copy-done((f32[512,2560]{1,0:T(8,128)}, f32[512,2560]{1,0:T(8,128)S(1)}, u32[]{:S(2)}) %copy-start) | copy-done | bytes 5242904
  119.0 6.5 %fusion.55 = f32[512,1280]{1,0:T(8,128)S(1)} fusion(bf16[2560,1280]{1,0:T(8,128)(2,1)} %param.29, f32[512,2560]{1,0:T(8,128)S(1)} %get-tuple-element.10, f32[2560]{0:T(1024)S(1)} %copy-done.7, f32[512]{0:T(512)S(1)} %add_rsqrt_fusion), kind=kOutput, calls=%fused_computation.80 | convolution fusion | flops 3359375360 | bytes 14430208 | tf_op jit(solution)/shard_map/feed_forward/dot_general | solution.py:199
  125.5 15.7 %convolution_convert_fusion = bf16[512,2560]{1,0:T(8,128)(2,1)} fusion(bf16[1280,2560]{1,0:T(8,128)(2,1)} %param.31, bf16[2560,1280]{1,0:T(8,128)(2,1)} %param.30, f32[512,1280]{1,0:T(8,128)S(1)} %fusion.55, f32[512,2560]{1,0:T(8,128)} %copy-done, f32[2560]{0:T(1024)S(1)} %copy-done.7, f32[512]{0:T(512)S(1)} %add_rsqrt_fusion), kind=kOutput, calls=%fused_computation.14 | convolution fusion | flops 6722682880 | bytes 23605248 | tf_op jit(solution)/shard_map/feed_forward/dot_general | solution.py:203
  141.3 32.7 %reduce-scatter.2.cloned.1.call-done = bf16[64,2560]{1,0:T(8,128)(2,1)} async-done(((bf16[512,2560]{1,0:T(8,128)(2,1)}), bf16[64,2560]{1,0:T(8,128)(2,1)}) %reduce-scatter.2.cloned.1.call-update) | async-done | bytes 327696 | tf_op jit(solution)/shard_map/feed_forward/reduce_scatter | solution.py:202
  174.0 1.1 fusion.35
  175.1 2.1 %fusion.38 = bf16[64,2560]{1,0:T(8,128)(2,1)} fusion(bf16[64,2560]{1,0:T(8,128)(2,1)} %reduce-scatter.2.cloned.1.call-done, f32[512,2560]{1,0:T(8,128)} %copy-done, s32[]{:T(128)S(6)} %select_n.55, f32[2560]{0:T(1024)S(1)} %copy-done.4, f32[64]{0:T(128)S(1)} %add_rsqrt_fusion.4), kind=kLoop, calls=%fused_computation.49 | loop fusion | flops 819200 | bytes 1321220 | tf_op jit(solution)/shard_map/convert_element_type | solution.py:208
  (29 shorter events, 0.1 us)
Async XLA Ops:
  6.5 63.6 %all-gather.3.cloned.1.call-start = ((), (), s32[]{:S(2)}) async-start(), calls=%async_computation.2 | async-start | bytes 4456448 | tf_op jit(solution)/shard_map/prefix_gather/all_gather | solution.py:149
  8.4 165.6 %reduce-scatter.2.cloned.1.call-start = ((), (), s32[]{:S(2)}) async-start(), calls=%async_computation.1 | async-start | bytes 2949120 | tf_op jit(solution)/shard_map/feed_forward/reduce_scatter | solution.py:202
  10.4 59.5 %copy-start.6 = (s32[16]{0:T(128)S(1)}, s32[16]{0:T(128)}, u32[]{:S(2)}) copy-start(s32[16]{0:T(128)} %param.23) | copy-start | bytes 196
  70.1 6.3 %copy-start.9 = (s32[1,3]{1,0:T(1,128)S(1)}, s32[1,3]{1,0:T(1,128)}, u32[]{:S(2)}) copy-start(s32[1,3]{1,0:T(1,128)} %param.21) | copy-start | bytes 40
  70.1 8.6 %copy-start.2 = (bf16[512,256]{1,0:T(8,128)(2,1)S(1)}, bf16[512,256]{1,0:T(8,128)(2,1)}, u32[]{:S(2)}) copy-start(bf16[512,256]{1,0:T(8,128)(2,1)} %param.16) | copy-start | bytes 786436
  70.2 8.8 %copy-start.5 = (f32[256]{0:T(256)S(1)}, f32[256]{0:T(256)}, u32[]{:S(2)}) copy-start(f32[256]{0:T(256)} %param.20) | copy-start | bytes 3076
  76.2 5.7 %copy-start.8 = (f32[256]{0:T(256)S(1)}, f32[256]{0:T(256)}, u32[]{:S(2)}) copy-start(f32[256]{0:T(256)} %param.19) | copy-start | bytes 3076
  76.2 4.4 %collective-permute-start = (bf16[2048,512]{1,0:T(8,128)(2,1)S(1)}, bf16[2048,512]{1,0:T(8,128)(2,1)}, u32[]{:S(2)}, u32[]{:S(2)}) collective-permute-start(bf16[2048,512]{1,0:T(8,128)(2,1)S(1)} %bitcast_select_fusion), channel_id=1, source_target_pairs={{0,1},{1,0},{2,3},{3,2},{4,5},{5,4},{6,7},{7,6},{8,9},{9,8},{10,11... | collective-permute-start | bytes 6291464 | tf_op jit(solution)/shard_map/prefix_gather/ppermute | solution.py:156
  106.0 9.5 %copy-start.1 = (bf16[512,2560]{1,0:T(8,128)(2,1)S(1)}, bf16[512,2560]{1,0:T(8,128)(2,1)}, u32[]{:S(2)}) copy-start(bf16[512,2560]{1,0:T(8,128)(2,1)} %param.24) | copy-start | bytes 7864324
  106.0 9.5 %copy-start.3 = (f32[2560]{0:T(1024)S(1)}, f32[2560]{0:T(1024)}, u32[]{:S(2)}) copy-start(f32[2560]{0:T(1024)} %param.26) | copy-start | bytes 30724
  115.5 3.5 %copy-start.7 = (f32[2560]{0:T(1024)S(1)}, f32[2560]{0:T(1024)}, u32[]{:S(2)}) copy-start(f32[2560]{0:T(1024)} %param.27) | copy-start | bytes 30724
  116.7 2.3 %copy-start = (f32[512,2560]{1,0:T(8,128)}, f32[512,2560]{1,0:T(8,128)S(1)}, u32[]{:S(2)}) copy-start(f32[512,2560]{1,0:T(8,128)S(1)} %get-tuple-element.10) | copy-start | bytes 15728644
  125.5 49.6 %copy-start.4 = (f32[2560]{0:T(1024)S(1)}, f32[2560]{0:T(1024)}, u32[]{:S(2)}) copy-start(f32[2560]{0:T(1024)} %param.28) | copy-start | bytes 30724
Sparse Core Ops, SparseCore 0:
  9.5 54.8 all-gather.2
  141.4 32.4 reduce-scatter.1

commit v5 on v4

--- a/solution.py
+++ b/solution.py
@@ -108,6 +108,93 @@
             flops=0, transcendentals=0, bytes_accessed=2 * tok_count * rows * cols * 2
         ),
     )(block)
+
+
+def scatter_tok_kernel(tok_count, part_ref, out_ref, chip_in, cross_out, cross_in, send_sem, recv_sem):
+    mesh_ids = pl.DeviceIdType.MESH
+    me = lax.axis_index("tok")
+    up = lax.rem(me + 2, tok_count)
+    down = lax.rem(me + tok_count - 2, tok_count)
+    far = lax.rem(me + 4, tok_count)
+    partner = me + 1 - 2 * lax.rem(me, 2)
+    share = out_ref.shape[0]
+
+    barrier = pltpu.get_barrier_semaphore()
+    for peer in (up, down, far, partner):
+        pl.semaphore_signal(barrier, inc=1, device_id={"tok": peer}, device_id_type=mesh_ids)
+    pl.semaphore_wait(barrier, 4)
+
+    def remote(src, dst, slot, peer):
+        return pltpu.make_async_remote_copy(
+            src_ref=src,
+            dst_ref=dst,
+            send_sem=send_sem.at[slot],
+            recv_sem=recv_sem.at[slot],
+            device_id={"tok": peer},
+            device_id_type=mesh_ids,
+        )
+
+    def family(base):
+        return (
+            base,
+            lax.rem(base + 2, tok_count),
+            lax.rem(base + tok_count - 2, tok_count),
+            lax.rem(base + 4, tok_count),
+        )
+
+    def rows_of(block):
+        return pl.ds(pl.multiple_of(block * share, share), share)
+
+    sends = []
+    for idx, block in enumerate(family(partner)):
+        copy = remote(part_ref.at[rows_of(block)], chip_in.at[idx], idx, partner)
+        copy.start()
+        sends.append(copy)
+    mine = family(me)
+    for idx in range(4):
+        remote(part_ref.at[rows_of(mine[idx])], chip_in.at[idx], idx, partner).wait_recv()
+
+    for idx in range(1, 4):
+        summed = part_ref[rows_of(mine[idx]), :] + chip_in[idx]
+        cross_out[idx - 1] = summed.astype(cross_out.dtype)
+    for src_idx, dst_idx, peer in ((0, 1, up), (1, 0, down), (2, 2, far)):
+        copy = remote(cross_out.at[src_idx], cross_in.at[dst_idx], 4 + dst_idx, peer)
+        copy.start()
+        sends.append(copy)
+    total = part_ref[rows_of(me), :] + chip_in[0]
+    for idx, peer in ((0, up), (1, down), (2, far)):
+        remote(cross_out.at[idx], cross_in.at[idx], 4 + idx, peer).wait_recv()
+    for idx in range(3):
+        total = total + cross_in[idx].astype(jnp.float32)
+    out_ref[...] = total
+    for copy in sends:
+        copy.wait_send()
+
+
+def scatter_over_tok(partial, tok_count, collective_id):
+    assert tok_count == 8
+    rows, cols = partial.shape
+    share = rows // tok_count
+    vmem = pltpu.MemorySpace.VMEM
+    return pl.pallas_call(
+        lambda *refs: scatter_tok_kernel(tok_count, *refs),
+        out_shape=jax.ShapeDtypeStruct((share, cols), jnp.float32),
+        in_specs=[pl.BlockSpec(memory_space=vmem)],
+        out_specs=pl.BlockSpec(memory_space=vmem),
+        scratch_shapes=[
+            pltpu.VMEM((4, share, cols), jnp.float32),
+            pltpu.VMEM((3, share, cols), jnp.bfloat16),
+            pltpu.VMEM((3, share, cols), jnp.bfloat16),
+            pltpu.SemaphoreType.DMA((7,)),
+            pltpu.SemaphoreType.DMA((7,)),
+        ],
+        compiler_params=pltpu.CompilerParams(
+            collective_id=collective_id, has_side_effects=True, vmem_limit_bytes=48 * 1024 * 1024
+        ),
+        cost_estimate=pl.CostEstimate(
+            flops=8 * share * cols, transcendentals=0, bytes_accessed=rows * cols * 4 * 2
+        ),
+    )(partial)
 
 
 def local(
@@ -199,11 +286,8 @@
         gate = jnp.dot(normed, w_gate, preferred_element_type=jnp.float32)
         upward = jnp.dot(normed, w_up, preferred_element_type=jnp.float32)
         hidden = (jax.nn.gelu(gate, approximate=True) * upward).astype(jnp.bfloat16)
-        down_share = lax.psum_scatter(
-            jnp.dot(hidden, w_down, preferred_element_type=jnp.float32).astype(jnp.bfloat16),
-            "tok",
-            scatter_dimension=0,
-            tiled=True,
+        down_share = scatter_over_tok(
+            jnp.dot(hidden, w_down, preferred_element_type=jnp.float32), tok_count, 2
         )
     return (mixed_share + rms_scale(down_share.astype(jnp.float32), ffn_out_gain)).astype(
         jnp.bfloat16

time: 187 us -> 177 us (0.947); the launches traced: 184 us -> 177 us
  waiting for transfers between devices: 33 us -> 0.36 us
  Pallas kernels: 77.2 us -> 100 us
  local copies, waits for them, and re-layouts: 10 us -> 12.5 us
    reduce_scatter x1 -> x0, waiting for transfers between devices: 32.7 us -> none  [local(): lax.psum_scatter(jnp.dot(hidden, w_down, preferred_element_type=jnp.float...]
    pallas_call x0 -> x1, Pallas kernels: none -> 23.3 us  [scatter_over_tok(): pl.pallas_call(lambda *refs: scatter_tok_kernel(tok_count, *refs), out_sh...]
    unnamed x20 -> x22, local copies, waits for them, and re-layouts: 2.36 us -> 4.84 us
  transfers between devices with their start and end apart: 3 -> 2, of which waited for: 2 -> 1; matrix products, arithmetic and copies ran while one was open for 3% -> 3% of each run, Pallas kernels for 32% -> 34%
where the time goes in v5:
time: 177 us
  Pallas kernels  100 us (56%)
  matrix products  37.5 us (21%)
  between operations  14.3 us (8%)
  local copies, waits for them, and re-layouts  12.5 us (7%)
  other arithmetic  11.5 us (6%)
    pallas_call x2, Pallas kernels, gather_over_tok(): pl.pallas_call(lambda *refs: gather_tok_kernel(tok_count, *refs), out_sha...  77.2 us
    pallas_call x1, Pallas kernels, scatter_over_tok(): pl.pallas_call(lambda *refs: scatter_tok_kernel(tok_count, *refs), out_sh...  23.3 us
    dot_general x1, matrix products, local(): jnp.dot(hidden, w_down, preferred_element_type=jnp.float32)  16.6 us
    dot_general x1, matrix products, local(): jnp.einsum('srd,sdc->rc', attention_all, w_out_all, preferred_element_typ...  9.5 us
    dot_general x1, matrix products, local(): gate = jnp.dot(normed, w_gate, preferred_element_type=jnp.float32)  6.5 us
    unnamed x22, local copies, waits for them, and re-layouts  4.84 us
    gather x1, local copies, waits for them, and re-layouts, local(): picked = jnp.take(gathered, owner_ids, axis=0).reshape(-1, 2 * HD)  4.24 us
  transfers between devices with their start and end apart: 2, of which 1 were waited for; matrix products, arithmetic and copies ran while one was open for 3% of the time, Pallas kernels for 34%

profile of v5, /device:TPU:1, one launch (start us, length us, event | category | flops | bytes accessed | tf_op | source)
XLA Modules:
  0.0 176.8 jit_solution(5484037250363753837)
XLA Ops:
  6.5 1.1 constant_dynamic-slice_fusion.1
  7.6 0.7 fusion.42
  8.4 1.3 dynamic_slice.24
  10.3 59.5 %prefix_gather.1 = bf16[8,256,2560]{2,1,0:T(8,128)(2,1)} custom-call(bf16[256,2560]{1,0:T(8,128)(2,1)} %refs_0_.1), custom_call_target="tpu_custom_call" | custom-call | bytes 20971520 | tf_op jit(solution)/shard_map/prefix_gather/pallas_call | solution.py:96
  69.9 0.1 compare_and_fusion
  69.9 0.1 broadcast_in_dim.20
  70.0 0.0 all-gather.3.cloned.1.call-done
  70.1 4.2 %gather_fusion = bf16[8,256,512]{2,1,0:T(8,128)(2,1)} fusion(bf16[16,256,512]{2,1,0:T(8,128)(2,1)} %bitcast.21, s32[1024]{0:T(1024)S(1)} %pad_clamp_fusion), kind=kCustom, calls=%fused_computation | custom fusion | bytes 4194336 | tf_op jit(solution)/shard_map/prefix_gather/jit(_take)/gather | solution.py:241
  74.4 1.8 bitcast_select_fusion
  76.1 0.2 collective-permute-start
  76.3 0.2 reduce-window.8
  76.5 1.1 fusion.39
  77.6 0.1 convert_reduce_fusion
  77.7 1.0 constant_dynamic-slice_fusion
  78.7 0.1 fusion.36
  78.9 1.1 fusion.41
  80.0 0.2 fusion.24
  80.2 0.3 collective-permute-done
  80.5 1.4 fusion.23
  81.9 1.6 fusion.54
  83.5 1.4 fusion
  84.9 3.4 %fusion.30.refs_0_ = bf16[512,256]{1,0:T(8,128)(2,1)} fusion(bf16[2048,512]{1,0:T(8,128)(2,1)} %collective-permute-done, bf16[2048,512]{1,0:T(8,128)(2,1)S(1)} %bitcast_select_fusion, bf16[512,256]{1,0:T(8,128)(2,1)S(1)} %constant_dynamic-slice_fusion, f32[512,4608]{1,0:T(8,128)S(1)} %get-tuple-element.16, f32[512]{0:T(512)S(1)} %get-tuple-element.15, ...), kind=kOutput, calls=%fused_computation.38 | convolution fusion | flops 1220018176 | bytes 14159872 | tf_op jit(solution)/shard_map/attention/dot_general | solution.py:269
  88.2 17.6 %out_projection.1 = bf16[8,512,256]{2,1,0:T(8,128)(2,1)} custom-call(bf16[512,256]{1,0:T(8,128)(2,1)} %fusion.30.refs_0_), custom_call_target="tpu_custom_call" | custom-call | bytes 4194304 | tf_op jit(solution)/shard_map/out_projection/pallas_call | solution.py:96
  105.9 9.5 %fusion.2 = (f32[512]{0:T(512)S(1)}, f32[512,2560,1]{1,0,2:T(8,128)S(1)}) fusion(bf16[8,512,256]{2,1,0:T(8,128)(2,1)} %out_projection.1, bf16[8,256,2560]{2,1,0:T(8,128)(2,1)} %prefix_gather.1), kind=kOutput, calls=%fused_computation.7 | convolution fusion | flops 5371330048 | bytes 17827840 | tf_op jit(solution)/shard_map/out_projection/srd,sdc->rc/dot_general | solution.py:279
  115.5 1.2 multiply_reduce_fusion
  116.7 2.3 %copy-done.1 = f32[512,2560]{1,0:T(8,128)} copy-done((f32[512,2560]{1,0:T(8,128)}, f32[512,2560]{1,0:T(8,128)S(1)}, u32[]{:S(2)}) %copy-start.1) | copy-done | bytes 5242904
  119.0 6.5 %fusion.52 = f32[512,1280]{1,0:T(8,128)S(1)} fusion(bf16[2560,1280]{1,0:T(8,128)(2,1)} %param.29, f32[512,2560]{1,0:T(8,128)S(1)} %get-tuple-element.10, f32[2560]{0:T(1024)S(1)} %copy-done.8, f32[512]{0:T(512)S(1)} %add_rsqrt_fusion), kind=kOutput, calls=%fused_computation.76 | convolution fusion | flops 3359375360 | bytes 14430208 | tf_op jit(solution)/shard_map/feed_forward/dot_general | solution.py:286
  125.5 16.6 %fusion.35.refs_0_ = f32[512,2560]{1,0:T(8,128)} fusion(bf16[1280,2560]{1,0:T(8,128)(2,1)} %param.31, bf16[2560,1280]{1,0:T(8,128)(2,1)} %param.30, f32[512,1280]{1,0:T(8,128)S(1)} %fusion.52, f32[512,2560]{1,0:T(8,128)} %copy-done.1, f32[2560]{0:T(1024)S(1)} %copy-done.8, f32[512]{0:T(512)S(1)} %add_rsqrt_fusion), kind=kOutput, calls=%fused_computation.39 | convolution fusion | flops 6721372160 | bytes 26226688 | tf_op jit(solution)/shard_map/feed_forward/dot_general | solution.py:290
  142.0 2.5 %copy-done = f32[512,2560]{1,0:T(8,128)S(1)} copy-done((f32[512,2560]{1,0:T(8,128)S(1)}, f32[512,2560]{1,0:T(8,128)}, u32[]{:S(2)}) %copy-start) | copy-done | bytes 5242904
  144.5 23.3 %feed_forward.1 = f32[64,2560]{1,0:T(8,128)S(1)} custom-call(f32[512,2560]{1,0:T(8,128)S(1)} %copy-done), custom_call_target="tpu_custom_call" | custom-call | flops 1310720 | bytes 10485760 | tf_op jit(solution)/shard_map/feed_forward/pallas_call | solution.py:179
  167.8 0.1 multiply_reduce_fusion.1
  167.9 2.0 %add_convert_fusion = bf16[64,2560]{1,0:T(8,128)(2,1)} fusion(f32[64,2560]{1,0:T(8,128)S(1)} %feed_forward.1, f32[512,2560]{1,0:T(8,128)} %copy-done.1, s32[]{:T(128)S(6)} %select_n.55, f32[2560]{0:T(1024)S(1)} %copy-done.5, f32[64]{0:T(128)S(1)} %add_rsqrt_fusion.4), kind=kLoop, calls=%fused_computation.44 | loop fusion | flops 655360 | bytes 1648900 | tf_op jit(solution)/shard_map/convert_element_type | solution.py:292
  (29 shorter events, 0.1 us)
Async XLA Ops:
  6.5 63.5 %all-gather.3.cloned.1.call-start = ((), (), s32[]{:S(2)}) async-start(), calls=%async_computation | async-start | bytes 4456448 | tf_op jit(solution)/shard_map/prefix_gather/all_gather | solution.py:236
  10.3 59.5 %copy-start.7 = (s32[16]{0:T(128)S(1)}, s32[16]{0:T(128)}, u32[]{:S(2)}) copy-start(s32[16]{0:T(128)} %param.23) | copy-start | bytes 196
  70.1 6.3 %copy-start.10 = (s32[1,3]{1,0:T(1,128)S(1)}, s32[1,3]{1,0:T(1,128)}, u32[]{:S(2)}) copy-start(s32[1,3]{1,0:T(1,128)} %param.21) | copy-start | bytes 40
  70.1 8.6 %copy-start.3 = (bf16[512,256]{1,0:T(8,128)(2,1)S(1)}, bf16[512,256]{1,0:T(8,128)(2,1)}, u32[]{:S(2)}) copy-start(bf16[512,256]{1,0:T(8,128)(2,1)} %param.16) | copy-start | bytes 786436
  70.1 8.8 %copy-start.6 = (f32[256]{0:T(256)S(1)}, f32[256]{0:T(256)}, u32[]{:S(2)}) copy-start(f32[256]{0:T(256)} %param.20) | copy-start | bytes 3076
  76.1 5.7 %copy-start.9 = (f32[256]{0:T(256)S(1)}, f32[256]{0:T(256)}, u32[]{:S(2)}) copy-start(f32[256]{0:T(256)} %param.19) | copy-start | bytes 3076
  76.1 4.4 %collective-permute-start = (bf16[2048,512]{1,0:T(8,128)(2,1)S(1)}, bf16[2048,512]{1,0:T(8,128)(2,1)}, u32[]{:S(2)}, u32[]{:S(2)}) collective-permute-start(bf16[2048,512]{1,0:T(8,128)(2,1)S(1)} %bitcast_select_fusion), channel_id=1, source_target_pairs={{0,1},{1,0},{2,3},{3,2},{4,5},{5,4},{6,7},{7,6},{8,9},{9,8},{10,11... | collective-permute-start | bytes 6291464 | tf_op jit(solution)/shard_map/prefix_gather/ppermute | solution.py:243
  105.9 9.5 %copy-start.2 = (bf16[512,2560]{1,0:T(8,128)(2,1)S(1)}, bf16[512,2560]{1,0:T(8,128)(2,1)}, u32[]{:S(2)}) copy-start(bf16[512,2560]{1,0:T(8,128)(2,1)} %param.24) | copy-start | bytes 7864324
  105.9 9.5 %copy-start.4 = (f32[2560]{0:T(1024)S(1)}, f32[2560]{0:T(1024)}, u32[]{:S(2)}) copy-start(f32[2560]{0:T(1024)} %param.26) | copy-start | bytes 30724
  115.5 3.5 %copy-start.8 = (f32[2560]{0:T(1024)S(1)}, f32[2560]{0:T(1024)}, u32[]{:S(2)}) copy-start(f32[2560]{0:T(1024)} %param.27) | copy-start | bytes 30724
  116.6 2.3 %copy-start.1 = (f32[512,2560]{1,0:T(8,128)}, f32[512,2560]{1,0:T(8,128)S(1)}, u32[]{:S(2)}) copy-start(f32[512,2560]{1,0:T(8,128)S(1)} %get-tuple-element.10) | copy-start | bytes 15728644
  142.0 2.5 %copy-start = (f32[512,2560]{1,0:T(8,128)S(1)}, f32[512,2560]{1,0:T(8,128)}, u32[]{:S(2)}) copy-start(f32[512,2560]{1,0:T(8,128)} %fusion.35.refs_0_) | copy-start | bytes 15728644
  144.5 23.4 %copy-start.5 = (f32[2560]{0:T(1024)S(1)}, f32[2560]{0:T(1024)}, u32[]{:S(2)}) copy-start(f32[2560]{0:T(1024)} %param.28) | copy-start | bytes 30724
Sparse Core Ops, SparseCore 0:
  9.5 54.8 all-gather.2

commit v6 on v5

--- a/solution.py
+++ b/solution.py
@@ -88,6 +88,103 @@
         remote(out_ref.at[slot], out_ref.at[slot], 4 + idx, partner).wait_recv()
     for copy in [to_up, to_down, fwd_up, fwd_down] + to_partner:
         copy.wait_send()
+
+
+def gather_req_kernel(line, block_ref, out_ref, send_sem, recv_sem, local_sem):
+    mesh_ids = pl.DeviceIdType.MESH
+    me = lax.axis_index("req")
+    core = lax.rem(lax.axis_index("tok"), 2)
+    first_stride = 1 + (line - 1) * core
+    second_stride = line - (line - 1) * core
+    half = block_ref.shape[0] // 2
+    top = pl.ds(0, half)
+    bottom = pl.ds(half, half)
+
+    def step(index, stride, offset):
+        pos = lax.rem(index // stride, line)
+        return index + (lax.rem(pos + offset + line, line) - pos) * stride
+
+    plus1, minus1, far1 = (step(me, first_stride, d) for d in (1, -1, 2))
+    plus2, minus2, far2 = (step(me, second_stride, d) for d in (1, -1, 2))
+
+    barrier = pltpu.get_barrier_semaphore()
+    for peer in (plus1, minus1, plus2, minus2):
+        pl.semaphore_signal(barrier, inc=1, device_id={"req": peer}, device_id_type=mesh_ids)
+    pl.semaphore_wait(barrier, 4)
+
+    def remote(src, dst, slot, peer):
+        return pltpu.make_async_remote_copy(
+            src_ref=src,
+            dst_ref=dst,
+            send_sem=send_sem.at[slot],
+            recv_sem=recv_sem.at[slot],
+            device_id={"req": peer},
+            device_id_type=mesh_ids,
+        )
+
+    sends = []
+
+    def send(src, dst, slot, peer):
+        copy = remote(src, dst, slot, peer)
+        copy.start()
+        sends.append(copy)
+
+    local = pltpu.make_async_copy(block_ref, out_ref.at[me], local_sem.at[0])
+    local.start()
+    send(block_ref, out_ref.at[me], 0, plus1)
+    send(block_ref, out_ref.at[me], 1, minus1)
+    remote(block_ref, out_ref.at[minus1], 0, minus1).wait_recv()
+    remote(block_ref, out_ref.at[plus1], 1, plus1).wait_recv()
+    send(out_ref.at[minus1, top], out_ref.at[minus1, top], 2, plus1)
+    send(out_ref.at[plus1, bottom], out_ref.at[plus1, bottom], 3, minus1)
+    remote(out_ref.at[far1, top], out_ref.at[far1, top], 2, minus1).wait_recv()
+    remote(out_ref.at[far1, bottom], out_ref.at[far1, bottom], 3, plus1).wait_recv()
+    local.wait()
+
+    offsets = (0, 1, -1, 2)
+
+    def line_of(index):
+        return [step(index, first_stride, d) for d in offsets]
+
+    for idx, slot in enumerate(line_of(me)):
+        send(out_ref.at[slot], out_ref.at[slot], 4 + idx, plus2)
+        send(out_ref.at[slot], out_ref.at[slot], 8 + idx, minus2)
+    from_minus = line_of(minus2)
+    from_plus = line_of(plus2)
+    for idx in range(len(offsets)):
+        remote(out_ref.at[from_minus[idx]], out_ref.at[from_minus[idx]], 4 + idx, minus2).wait_recv()
+        remote(out_ref.at[from_plus[idx]], out_ref.at[from_plus[idx]], 8 + idx, plus2).wait_recv()
+    for idx in range(len(offsets)):
+        send(out_ref.at[from_minus[idx], top], out_ref.at[from_minus[idx], top], 12 + idx, plus2)
+        send(out_ref.at[from_plus[idx], bottom], out_ref.at[from_plus[idx], bottom], 16 + idx, minus2)
+    from_far = line_of(far2)
+    for idx in range(len(offsets)):
+        slot = from_far[idx]
+        remote(out_ref.at[slot, top], out_ref.at[slot, top], 12 + idx, minus2).wait_recv()
+        remote(out_ref.at[slot, bottom], out_ref.at[slot, bottom], 16 + idx, plus2).wait_recv()
+    for copy in sends:
+        copy.wait_send()
+
+
+def gather_over_req(block, req_count, collective_id):
+    line = 4
+    assert req_count == line * line
+    rows, cols = block.shape
+    return pl.pallas_call(
+        lambda *refs: gather_req_kernel(line, *refs),
+        out_shape=jax.ShapeDtypeStruct((req_count, rows, cols), block.dtype),
+        in_specs=[pl.BlockSpec(memory_space=pl.ANY)],
+        out_specs=pl.BlockSpec(memory_space=pl.ANY),
+        scratch_shapes=[
+            pltpu.SemaphoreType.DMA((20,)),
+            pltpu.SemaphoreType.DMA((20,)),
+            pltpu.SemaphoreType.DMA((1,)),
+        ],
+        compiler_params=pltpu.CompilerParams(collective_id=collective_id, has_side_effects=True),
+        cost_estimate=pl.CostEstimate(
+            flops=0, transcendentals=0, bytes_accessed=2 * req_count * rows * cols * 2
+        ),
+    )(block)
 
 
 def gather_over_tok(block, tok_count, collective_id):
@@ -233,9 +330,7 @@
         half_rows = pref_kv.shape[0] // 2
         core = tok_index % 2
         my_half = lax.dynamic_slice_in_dim(pref_kv, core * half_rows, half_rows, 0)
-        gathered = lax.all_gather(my_half, "req", axis=0, tiled=False)
-        w_out_all = gather_over_tok(w_out, tok_count, 0)
-        gathered, w_out_all = lax.optimization_barrier((gathered, w_out_all))
+        gathered = gather_over_req(my_half, req_count, 0)
         own_group = group_of[req_index]
         owner_ids = lax.dynamic_slice_in_dim(owner_order, own_group * own_count, own_count)
         picked = jnp.take(gathered, owner_ids, axis=0).reshape(-1, 2 * HD)
@@ -275,13 +370,13 @@
     share = row_count // tok_count
     first_row = tok_index * share
     with jax.named_scope("out_projection"):
-        attention_all = gather_over_tok(attention, tok_count, 1)
-        projected = jnp.einsum(
-            "srd,sdc->rc", attention_all, w_out_all, preferred_element_type=jnp.float32
-        )
-        mixed_rows = residual.astype(jnp.float32) + rms_scale(projected, attn_gain)
-        normed = rms_scale(mixed_rows, ffn_in_gain).astype(jnp.bfloat16)
-        mixed_share = lax.dynamic_slice_in_dim(mixed_rows, first_row, share, 0)
+        projected = scatter_over_tok(
+            jnp.dot(attention, w_out, preferred_element_type=jnp.float32), tok_count, 3
+        )
+        residual_share = lax.dynamic_slice_in_dim(residual, first_row, share, 0)
+        mixed_share = residual_share.astype(jnp.float32) + rms_scale(projected, attn_gain)
+        normed_share = rms_scale(mixed_share, ffn_in_gain).astype(jnp.bfloat16)
+        normed = gather_over_tok(normed_share, tok_count, 1).reshape(row_count, -1)
     with jax.named_scope("feed_forward"):
         gate = jnp.dot(normed, w_gate, preferred_element_type=jnp.float32)
         upward = jnp.dot(normed, w_up, preferred_element_type=jnp.float32)

time: 177 us -> 180 us (1.017)
  between operations: 14.3 us -> 0.9 us
  Pallas kernels: 100 us -> 105 us
  local copies, waits for them, and re-layouts: 12.5 us -> 17 us
  other arithmetic: 11.5 us -> 15.3 us
  starting transfers between devices: 0.21 us -> 3.77 us
    pallas_call x2 -> x1, Pallas kernels: 77.2 us -> 20.4 us  [gather_over_tok(): pl.pallas_call(lambda *refs: gather_tok_kernel(tok_count, *refs), out_sha...]
    pallas_call x0 -> x1, Pallas kernels: none -> 37.6 us  [gather_over_req(): pl.pallas_call(lambda *refs: gather_req_kernel(line, *refs), out_shape=ja...]
    pallas_call x1 -> x2, Pallas kernels: 23.3 us -> 47.3 us  [scatter_over_tok(): pl.pallas_call(lambda *refs: scatter_tok_kernel(tok_count, *refs), out_sh...]
    unnamed x22 -> x24, local copies, waits for them, and re-layouts: 4.84 us -> 8.64 us
    ppermute x1, starting transfers between devices: 0.2 us -> 3.77 us  [local(): swapped = lax.ppermute(picked, 'tok', perm=partner)]
    dot_general x2 -> x1, matrix products: 12.9 us -> 9.81 us  [local(): jnp.dot(attention, w_out, preferred_element_type=jnp.float32)]
    dot_general x1, matrix products: 6.5 us -> 8.77 us  [local(): gate = jnp.dot(normed, w_gate, preferred_element_type=jnp.float32)]
    convert_element_type x0 -> x1, other arithmetic: none -> 1.93 us  [local(): normed_share = rms_scale(mixed_share, ffn_in_gain).astype(jnp.bfloat16)]
  transfers between devices with their start and end apart: 2 -> 1, of which waited for: 1 -> 0; matrix products, arithmetic and copies ran while one was open for 3% -> 3% of each run, Pallas kernels for 34% -> 0%
where the time goes in v6:
time: 180 us; the launch traced here: 179 us
  Pallas kernels  105 us (58%)
  matrix products  36.8 us (20%)
  local copies, waits for them, and re-layouts  17 us (9%)
  other arithmetic  15.3 us (8%)
  starting transfers between devices  3.77 us (2%)
    pallas_call x2, Pallas kernels, scatter_over_tok(): pl.pallas_call(lambda *refs: scatter_tok_kernel(tok_count, *refs), out_sh...  47.3 us
    pallas_call x1, Pallas kernels, gather_over_req(): pl.pallas_call(lambda *refs: gather_req_kernel(line, *refs), out_shape=ja...  37.6 us
    pallas_call x1, Pallas kernels, gather_over_tok(): pl.pallas_call(lambda *refs: gather_tok_kernel(tok_count, *refs), out_sha...  20.4 us
    dot_general x1, matrix products, local(): jnp.dot(hidden, w_down, preferred_element_type=jnp.float32)  16.6 us
    dot_general x1, matrix products, local(): jnp.dot(attention, w_out, preferred_element_type=jnp.float32)  9.81 us
    dot_general x1, matrix products, local(): gate = jnp.dot(normed, w_gate, preferred_element_type=jnp.float32)  8.77 us
    unnamed x24, local copies, waits for them, and re-layouts  8.64 us
    gather x1, local copies, waits for them, and re-layouts, local(): picked = jnp.take(gathered, owner_ids, axis=0).reshape(-1, 2 * HD)  4.2 us
  transfers between devices with their start and end apart: 1, of which 0 were waited for; matrix products, arithmetic and copies ran while one was open for 3% of the time, Pallas kernels for 0%

profile of v6, /device:TPU:1, one launch (start us, length us, event | category | flops | bytes accessed | tf_op | source)
XLA Modules:
  0.0 179.1 jit_solution(13063756279945385150)
XLA Ops:
  0.0 1.3 dynamic_slice.25
  2.0 0.7 compare_and_fusion
  2.9 1.1 constant_dynamic-slice_fusion.1
  4.0 0.7 fusion.44.refs_0_
  4.7 37.6 %prefix_gather.1 = bf16[16,256,512]{2,1,0:T(8,128)(2,1)} custom-call(bf16[256,512]{1,0:T(8,128)(2,1)} %fusion.44.refs_0_), custom_call_target="tpu_custom_call" | custom-call | bytes 8388608 | tf_op jit(solution)/shard_map/prefix_gather/pallas_call | solution.py:173
  42.3 4.2 %gather_fusion = bf16[8,256,512]{2,1,0:T(8,128)(2,1)} fusion(bf16[16,256,512]{2,1,0:T(8,128)(2,1)} %prefix_gather.1, s32[1024]{0:T(1024)S(1)} %pad_clamp_fusion), kind=kCustom, calls=%fused_computation | custom fusion | bytes 4194336 | tf_op jit(solution)/shard_map/prefix_gather/jit(_take)/gather | solution.py:336
  46.5 1.8 %bitcast_select_fusion = bf16[2048,512]{1,0:T(8,128)(2,1)S(1)} fusion(bf16[8,256,512]{2,1,0:T(8,128)(2,1)} %gather_fusion, pred[2048]{0:T(1024)(128)(4,1)S(1)} %broadcast_in_dim.21), kind=kLoop, calls=%fused_computation.27 | loop fusion | flops 1048576 | bytes 4196352 | tf_op jit(solution)/shard_map/prefix_gather/jit(_take)/select_n | solution.py:336
  48.3 3.8 %collective-permute-start = (bf16[2048,512]{1,0:T(8,128)(2,1)S(1)}, bf16[2048,512]{1,0:T(8,128)(2,1)}, u32[]{:S(2)}, u32[]{:S(2)}) collective-permute-start(bf16[2048,512]{1,0:T(8,128)(2,1)S(1)} %bitcast_select_fusion), channel_id=1, source_target_pairs={{0,1},{1,0},{2,3},{3,2},{4,5},{5,4},{6,7},{7,6},{8,9},{9,8},{10,11... | collective-permute-start | bytes 6291464 | tf_op jit(solution)/shard_map/prefix_gather/ppermute | solution.py:338
  52.1 0.2 reduce-window.8
  52.3 1.1 fusion.41
  53.4 0.1 convert_reduce_fusion
  53.4 1.7 constant_dynamic-slice_fusion
  55.1 1.1 fusion.38
  56.2 1.1 fusion.43
  57.3 0.2 fusion.21
  57.6 1.4 fusion.20
  59.0 1.6 fusion.56
  60.6 3.6 %copy-done.4 = f32[512,4608]{1,0:T(8,128)} copy-done((f32[512,4608]{1,0:T(8,128)}, f32[512,4608]{1,0:T(8,128)S(1)}, u32[]{:S(2)}) %copy-start.4) | copy-done | bytes 9437208
  64.2 1.4 fusion
  65.6 9.8 %fusion.34.refs_0_ = f32[512,2560]{1,0:T(8,128)} fusion(bf16[256,2560]{1,0:T(8,128)(2,1)S(1)} %copy-done, bf16[2048,512]{1,0:T(8,128)(2,1)} %collective-permute-done, bf16[2048,512]{1,0:T(8,128)(2,1)S(1)} %bitcast_select_fusion, bf16[512,256]{1,0:T(8,128)(2,1)} %constant_dynamic-slice_fusion, f32[512,4608]{1,0:T(8,128)} %copy-done.4, ...), kind=kOutput, calls=%fused_computation.32 | convolution fusion | flops 1891106816 | bytes 20451328 | tf_op jit(solution)/shard_map/out_projection/dot_general | solution.py:374
  75.4 2.5 %copy-done.2 = f32[512,2560]{1,0:T(8,128)S(1)} copy-done((f32[512,2560]{1,0:T(8,128)S(1)}, f32[512,2560]{1,0:T(8,128)}, u32[]{:S(2)}) %copy-start.2) | copy-done | bytes 5242904
  77.9 24.0 %out_projection.2 = f32[64,2560]{1,0:T(8,128)S(1)} custom-call(f32[512,2560]{1,0:T(8,128)S(1)} %copy-done.2), custom_call_target="tpu_custom_call" | custom-call | flops 1310720 | bytes 10485760 | tf_op jit(solution)/shard_map/out_projection/pallas_call | solution.py:276
  102.0 0.1 multiply_reduce_fusion.2
  102.1 1.3 multiply_reduce_fusion.1
  103.4 1.9 %multiply_convert_fusion.refs_0_ = bf16[64,2560]{1,0:T(8,128)(2,1)} fusion(f32[2560]{0:T(1024)S(1)} %copy-done.7, f32[64]{0:T(128)S(1)} %add_rsqrt_fusion.3, f32[2560]{0:T(1024)S(1)} %copy-done.6, f32[64,2560]{1,0:T(8,128)S(1)} %out_projection.2, f32[64]{0:T(128)S(1)} %add_rsqrt_fusion.4, bf16[512,2560]{1,0:T(8,128)(2,1)} %param.24, s32[]{:T(128)S(6)} %select_n.45), kind=kLoop, calls=%fused_computation.40 | loop fusion | flops 1146880 | bytes 1331716 | tf_op jit(solution)/shard_map/out_projection/convert_element_type | solution.py:378
  105.4 20.4 %out_projection.3 = bf16[8,64,2560]{2,1,0:T(8,128)(2,1)} custom-call(bf16[64,2560]{1,0:T(8,128)(2,1)} %multiply_convert_fusion.refs_0_), custom_call_target="tpu_custom_call" | custom-call | bytes 5242880 | tf_op jit(solution)/shard_map/out_projection/pallas_call | solution.py:193
  125.8 8.8 %fusion.57 = f32[512,1280]{1,0:T(8,128)} fusion(bf16[512,2560]{1,0:T(8,128)(2,1)} %bitcast.12, bf16[2560,1280]{1,0:T(8,128)(2,1)} %param.29), kind=kOutput, calls=%fused_computation.76 | convolution fusion | flops 3355443200 | bytes 11796480 | tf_op jit(solution)/shard_map/feed_forward/dot_general | solution.py:381
  134.5 16.6 %fusion.37.refs_0_ = f32[512,2560]{1,0:T(8,128)} fusion(bf16[1280,2560]{1,0:T(8,128)(2,1)} %param.31, bf16[512,2560]{1,0:T(8,128)(2,1)} %bitcast.13, bf16[2560,1280]{1,0:T(8,128)(2,1)} %param.30, f32[512,1280]{1,0:T(8,128)} %fusion.57), kind=kOutput, calls=%fused_computation.33 | convolution fusion | flops 6717440000 | bytes 23592960 | tf_op jit(solution)/shard_map/feed_forward/dot_general | solution.py:385
  151.2 2.5 %copy-done.3 = f32[512,2560]{1,0:T(8,128)S(1)} copy-done((f32[512,2560]{1,0:T(8,128)S(1)}, f32[512,2560]{1,0:T(8,128)}, u32[]{:S(2)}) %copy-start.3) | copy-done | bytes 5242904
  153.7 23.3 %feed_forward.1 = f32[64,2560]{1,0:T(8,128)S(1)} custom-call(f32[512,2560]{1,0:T(8,128)S(1)} %copy-done.3), custom_call_target="tpu_custom_call" | custom-call | flops 1310720 | bytes 10485760 | tf_op jit(solution)/shard_map/feed_forward/pallas_call | solution.py:276
  176.9 0.1 multiply_reduce_fusion
  177.1 2.0 %add_convert_fusion = bf16[64,2560]{1,0:T(8,128)(2,1)} fusion(f32[64,2560]{1,0:T(8,128)S(1)} %feed_forward.1, f32[2560]{0:T(1024)S(1)} %copy-done.8, f32[64]{0:T(128)S(1)} %add_rsqrt_fusion.2, f32[2560]{0:T(1024)S(1)} %copy-done.6, f32[64,2560]{1,0:T(8,128)S(1)} %out_projection.2, f32[64]{0:T(128)S(1)} %add_rsqrt_fusion.4, bf16[512,2560]{1,0:T(8,128)(2,1)} %param.24, ...), kind=kLoop, calls=%fused_computation.38 | loop fusion | flops 1310720 | bytes 1987076 | tf_op jit(solution)/shard_map/convert_element_type | solution.py:387
  (30 shorter events, 0.2 us)
Async XLA Ops:
  0.0 65.6 %copy-start = (bf16[256,2560]{1,0:T(8,128)(2,1)S(1)}, bf16[256,2560]{1,0:T(8,128)(2,1)}, u32[]{:S(2)}) copy-start(bf16[256,2560]{1,0:T(8,128)(2,1)} %param.25) | copy-start | bytes 3932164
  46.5 5.6 %copy-start.11 = (s32[1,3]{1,0:T(1,128)S(1)}, s32[1,3]{1,0:T(1,128)}, u32[]{:S(2)}) copy-start(s32[1,3]{1,0:T(1,128)} %param.21) | copy-start | bytes 40
  46.5 9.7 %copy-start.9 = (f32[256]{0:T(256)S(1)}, f32[256]{0:T(256)}, u32[]{:S(2)}) copy-start(f32[256]{0:T(256)} %param.20) | copy-start | bytes 3076
  48.3 9.3 %collective-permute-start = (bf16[2048,512]{1,0:T(8,128)(2,1)S(1)}, bf16[2048,512]{1,0:T(8,128)(2,1)}, u32[]{:S(2)}, u32[]{:S(2)}) collective-permute-start(bf16[2048,512]{1,0:T(8,128)(2,1)S(1)} %bitcast_select_fusion), channel_id=1, source_target_pairs={{0,1},{1,0},{2,3},{3,2},{4,5},{5,4},{6,7},{7,6},{8,9},{9,8},{10,11... | collective-permute-start | bytes 6291464 | tf_op jit(solution)/shard_map/prefix_gather/ppermute | solution.py:338
  57.6 1.4 copy-start.5
  57.6 1.4 copy-start.10
  60.6 3.6 %copy-start.4 = (f32[512,4608]{1,0:T(8,128)}, f32[512,4608]{1,0:T(8,128)S(1)}, u32[]{:S(2)}) copy-start(f32[512,4608]{1,0:T(8,128)S(1)} %get-tuple-element.10) | copy-start | bytes 28311556
  75.4 2.5 %copy-start.2 = (f32[512,2560]{1,0:T(8,128)S(1)}, f32[512,2560]{1,0:T(8,128)}, u32[]{:S(2)}) copy-start(f32[512,2560]{1,0:T(8,128)} %fusion.34.refs_0_) | copy-start | bytes 15728644
  77.9 24.2 %copy-start.6 = (f32[2560]{0:T(1024)S(1)}, f32[2560]{0:T(1024)}, u32[]{:S(2)}) copy-start(f32[2560]{0:T(1024)} %param.26) | copy-start | bytes 30724
  77.9 25.5 %copy-start.7 = (f32[2560]{0:T(1024)S(1)}, f32[2560]{0:T(1024)}, u32[]{:S(2)}) copy-start(f32[2560]{0:T(1024)} %param.27) | copy-start | bytes 30724
  151.2 2.5 %copy-start.3 = (f32[512,2560]{1,0:T(8,128)S(1)}, f32[512,2560]{1,0:T(8,128)}, u32[]{:S(2)}) copy-start(f32[512,2560]{1,0:T(8,128)} %fusion.37.refs_0_) | copy-start | bytes 15728644
  153.7 23.4 %copy-start.8 = (f32[2560]{0:T(1024)S(1)}, f32[2560]{0:T(1024)}, u32[]{:S(2)}) copy-start(f32[2560]{0:T(1024)} %param.28) | copy-start | bytes 30724
  153.7 25.4 %copy-start.1 = (bf16[256,2560]{1,0:T(8,128)(2,1)S(1)}, bf16[256,2560]{1,0:T(8,128)(2,1)}, u32[]{:S(2)}) copy-start(bf16[256,2560]{1,0:T(8,128)(2,1)} %param.25) | copy-start | bytes 3932164

commit v7 on v5

--- a/solution.py
+++ b/solution.py
@@ -29,7 +29,87 @@
     return rms_scale(shaped, gain_vec).astype(jnp.bfloat16).reshape(row_count, head_count * HD)
 
 
-def gather_tok_kernel(tok_count, w_ref, out_ref, send_sem, recv_sem, local_sem):
+def req_ring(line, block_ref, out_ref, send_sem, recv_sem, local_sem, sends):
+    mesh_ids = pl.DeviceIdType.MESH
+    me = lax.axis_index("req")
+    core = lax.rem(lax.axis_index("tok"), 2)
+    first_stride = 1 + (line - 1) * core
+    second_stride = line - (line - 1) * core
+    half = block_ref.shape[0] // 2
+    top = pl.ds(0, half)
+    bottom = pl.ds(half, half)
+
+    def step(index, stride, offset):
+        pos = lax.rem(index // stride, line)
+        return index + (lax.rem(pos + offset + line, line) - pos) * stride
+
+    plus1, minus1, far1 = (step(me, first_stride, d) for d in (1, -1, 2))
+    plus2, minus2, far2 = (step(me, second_stride, d) for d in (1, -1, 2))
+
+    def remote(src, dst, slot, peer):
+        return pltpu.make_async_remote_copy(
+            src_ref=src,
+            dst_ref=dst,
+            send_sem=send_sem.at[slot],
+            recv_sem=recv_sem.at[slot],
+            device_id={"req": peer},
+            device_id_type=mesh_ids,
+        )
+
+    def send(src, dst, slot, peer):
+        copy = remote(src, dst, slot, peer)
+        copy.start()
+        sends.append(copy)
+
+    local = pltpu.make_async_copy(block_ref, out_ref.at[me], local_sem.at[0])
+    local.start()
+    send(block_ref, out_ref.at[me], 0, plus1)
+    send(block_ref, out_ref.at[me], 1, minus1)
+    yield
+    remote(block_ref, out_ref.at[minus1], 0, minus1).wait_recv()
+    remote(block_ref, out_ref.at[plus1], 1, plus1).wait_recv()
+    send(out_ref.at[minus1, top], out_ref.at[minus1, top], 2, plus1)
+    send(out_ref.at[plus1, bottom], out_ref.at[plus1, bottom], 3, minus1)
+    remote(out_ref.at[far1, top], out_ref.at[far1, top], 2, minus1).wait_recv()
+    remote(out_ref.at[far1, bottom], out_ref.at[far1, bottom], 3, plus1).wait_recv()
+    yield
+    local.wait()
+
+    offsets = (0, 1, -1, 2)
+
+    def line_of(index):
+        return [step(index, first_stride, d) for d in offsets]
+
+    for idx, slot in enumerate(line_of(me)):
+        send(out_ref.at[slot], out_ref.at[slot], 4 + idx, plus2)
+        send(out_ref.at[slot], out_ref.at[slot], 8 + idx, minus2)
+    from_minus = line_of(minus2)
+    from_plus = line_of(plus2)
+    yield
+    for idx in range(len(offsets)):
+        remote(out_ref.at[from_minus[idx]], out_ref.at[from_minus[idx]], 4 + idx, minus2).wait_recv()
+        remote(out_ref.at[from_plus[idx]], out_ref.at[from_plus[idx]], 8 + idx, plus2).wait_recv()
+    for idx in range(len(offsets)):
+        send(out_ref.at[from_minus[idx], top], out_ref.at[from_minus[idx], top], 12 + idx, plus2)
+        send(out_ref.at[from_plus[idx], bottom], out_ref.at[from_plus[idx], bottom], 16 + idx, minus2)
+    yield
+    from_far = line_of(far2)
+    for idx in range(len(offsets)):
+        slot = from_far[idx]
+        remote(out_ref.at[slot, top], out_ref.at[slot, top], 12 + idx, minus2).wait_recv()
+        remote(out_ref.at[slot, bottom], out_ref.at[slot, bottom], 16 + idx, plus2).wait_recv()
+    yield
+
+
+def tok_peers(tok_count):
+    me = lax.axis_index("tok")
+    up = lax.rem(me + 2, tok_count)
+    down = lax.rem(me + tok_count - 2, tok_count)
+    partner = me + 1 - 2 * lax.rem(me, 2)
+    return up, down, partner
+
+
+def tok_ring(tok_count, w_ref, out_ref, send_sem, recv_sem, local_sem, sends):
     mesh_ids = pl.DeviceIdType.MESH
     me = lax.axis_index("tok")
     up = lax.rem(me + 2, tok_count)
@@ -37,11 +117,6 @@
     far = lax.rem(me + 4, tok_count)
     partner = me + 1 - 2 * lax.rem(me, 2)
     half = w_ref.shape[0] // 2
-
-    barrier = pltpu.get_barrier_semaphore()
-    for peer in (up, down, partner):
-        pl.semaphore_signal(barrier, inc=1, device_id={"tok": peer}, device_id_type=mesh_ids)
-    pl.semaphore_wait(barrier, 3)
 
     def remote(src, dst, slot, peer):
         return pltpu.make_async_remote_copy(
@@ -59,6 +134,7 @@
     to_down = remote(w_ref, out_ref.at[me], 1, down)
     to_up.start()
     to_down.start()
+    yield
     remote(w_ref, out_ref.at[down], 0, down).wait_recv()
     remote(w_ref, out_ref.at[up], 1, up).wait_recv()
 
@@ -68,6 +144,7 @@
     fwd_down = remote(out_ref.at[up, second], out_ref.at[up, second], 3, down)
     fwd_up.start()
     fwd_down.start()
+    yield
     remote(out_ref.at[far, first], out_ref.at[far, first], 2, down).wait_recv()
     remote(out_ref.at[far, second], out_ref.at[far, second], 3, up).wait_recv()
     local.wait()
@@ -84,10 +161,82 @@
         copy = remote(out_ref.at[slot], out_ref.at[slot], 4 + idx, partner)
         copy.start()
         to_partner.append(copy)
+    yield
     for idx, slot in enumerate(theirs):
         remote(out_ref.at[slot], out_ref.at[slot], 4 + idx, partner).wait_recv()
-    for copy in [to_up, to_down, fwd_up, fwd_down] + to_partner:
+    sends.extend([to_up, to_down, fwd_up, fwd_down] + to_partner)
+    yield
+
+
+def gather_tok_kernel(tok_count, w_ref, out_ref, send_sem, recv_sem, local_sem):
+    mesh_ids = pl.DeviceIdType.MESH
+    barrier = pltpu.get_barrier_semaphore()
+    for peer in tok_peers(tok_count):
+        pl.semaphore_signal(barrier, inc=1, device_id={"tok": peer}, device_id_type=mesh_ids)
+    pl.semaphore_wait(barrier, 3)
+    sends = []
+    for _ in tok_ring(tok_count, w_ref, out_ref, send_sem, recv_sem, local_sem, sends):
+        pass
+    for copy in sends:
         copy.wait_send()
+
+
+def prefetch_kernel(
+    line, tok_count, w_ref, kv_ref, w_all, kv_all, w_send, w_recv, w_local, kv_send, kv_recv, kv_local
+):
+    mesh_ids = pl.DeviceIdType.MESH
+    me = lax.axis_index("req")
+    core = lax.rem(lax.axis_index("tok"), 2)
+    barrier = pltpu.get_barrier_semaphore()
+    for peer in tok_peers(tok_count):
+        pl.semaphore_signal(barrier, inc=1, device_id={"tok": peer}, device_id_type=mesh_ids)
+    for stride in (1 + (line - 1) * core, line - (line - 1) * core):
+        pos = lax.rem(me // stride, line)
+        for offset in (1, line - 1):
+            peer = me + (lax.rem(pos + offset, line) - pos) * stride
+            pl.semaphore_signal(barrier, inc=1, device_id={"req": peer}, device_id_type=mesh_ids)
+    pl.semaphore_wait(barrier, 7)
+    sends = []
+    w_steps = tok_ring(tok_count, w_ref, w_all, w_send, w_recv, w_local, sends)
+    kv_steps = req_ring(line, kv_ref, kv_all, kv_send, kv_recv, kv_local, sends)
+    for steps in (w_steps, kv_steps, kv_steps, kv_steps, w_steps, kv_steps, w_steps, kv_steps, w_steps):
+        next(steps)
+    for steps in (w_steps, kv_steps):
+        for _ in steps:
+            pass
+    for copy in sends:
+        copy.wait_send()
+
+
+def prefetch(w_block, kv_block, tok_count, req_count, collective_id):
+    line = 4
+    assert tok_count == 8 and req_count == line * line
+    w_rows, w_cols = w_block.shape
+    kv_rows, kv_cols = kv_block.shape
+    any_space = pl.BlockSpec(memory_space=pl.ANY)
+    return pl.pallas_call(
+        lambda *refs: prefetch_kernel(line, tok_count, *refs),
+        out_shape=(
+            jax.ShapeDtypeStruct((tok_count, w_rows, w_cols), w_block.dtype),
+            jax.ShapeDtypeStruct((req_count, kv_rows, kv_cols), kv_block.dtype),
+        ),
+        in_specs=[any_space, any_space],
+        out_specs=(any_space, any_space),
+        scratch_shapes=[
+            pltpu.SemaphoreType.DMA((8,)),
+            pltpu.SemaphoreType.DMA((8,)),
+            pltpu.SemaphoreType.DMA((1,)),
+            pltpu.SemaphoreType.DMA((20,)),
+            pltpu.SemaphoreType.DMA((20,)),
+            pltpu.SemaphoreType.DMA((1,)),
+        ],
+        compiler_params=pltpu.CompilerParams(collective_id=collective_id, has_side_effects=True),
+        cost_estimate=pl.CostEstimate(
+            flops=0,
+            transcendentals=0,
+            bytes_accessed=2 * (tok_count * w_rows * w_cols + req_count * kv_rows * kv_cols) * 2,
+        ),
+    )(w_block, kv_block)
 
 
 def gather_over_tok(block, tok_count, collective_id):
@@ -233,9 +382,7 @@
         half_rows = pref_kv.shape[0] // 2
         core = tok_index % 2
         my_half = lax.dynamic_slice_in_dim(pref_kv, core * half_rows, half_rows, 0)
-        gathered = lax.all_gather(my_half, "req", axis=0, tiled=False)
-        w_out_all = gather_over_tok(w_out, tok_count, 0)
-        gathered, w_out_all = lax.optimization_barrier((gathered, w_out_all))
+        w_out_all, gathered = prefetch(w_out, my_half, tok_count, req_count, 0)
         own_group = group_of[req_index]
         owner_ids = lax.dynamic_slice_in_dim(owner_order, own_group * own_count, own_count)
         picked = jnp.take(gathered, owner_ids, axis=0).reshape(-1, 2 * HD)

time: 177 us -> 186 us (1.051)
  Pallas kernels: 100 us -> 122 us
  between operations: 14.3 us -> 0.93 us
    pallas_call x0 -> x1, Pallas kernels: none -> 81.1 us  [prefetch(): pl.pallas_call(lambda *refs: prefetch_kernel(line, tok_count, *refs), out...]
    pallas_call x2 -> x1, Pallas kernels: 77.2 us -> 17.6 us  [gather_over_tok(): pl.pallas_call(lambda *refs: gather_tok_kernel(tok_count, *refs), out_sha...]
    unnamed x22 -> x20, local copies, waits for them, and re-layouts: 4.84 us -> 4.83 us
  transfers between devices with their start and end apart: 2 -> 1, of which waited for: 1 -> 1; matrix products, arithmetic and copies ran while one was open for 3% -> 2% of each run, Pallas kernels for 34% -> 0%
where the time goes in v7:
time: 186 us; the launch traced here: 185 us
  Pallas kernels  122 us (66%)
  matrix products  37.5 us (20%)
  local copies, waits for them, and re-layouts  12.4 us (7%)
  other arithmetic  12.1 us (7%)
    pallas_call x1, Pallas kernels, prefetch(): pl.pallas_call(lambda *refs: prefetch_kernel(line, tok_count, *refs), out...  81.1 us
    pallas_call x1, Pallas kernels, scatter_over_tok(): pl.pallas_call(lambda *refs: scatter_tok_kernel(tok_count, *refs), out_sh...  23.3 us
    pallas_call x1, Pallas kernels, gather_over_tok(): pl.pallas_call(lambda *refs: gather_tok_kernel(tok_count, *refs), out_sha...  17.6 us
    dot_general x1, matrix products, local(): jnp.dot(hidden, w_down, preferred_element_type=jnp.float32)  16.6 us
    dot_general x1, matrix products, local(): jnp.einsum('srd,sdc->rc', attention_all, w_out_all, preferred_element_typ...  9.5 us
    dot_general x1, matrix products, local(): gate = jnp.dot(normed, w_gate, preferred_element_type=jnp.float32)  6.5 us
    unnamed x20, local copies, waits for them, and re-layouts  4.83 us
    gather x1, local copies, waits for them, and re-layouts, local(): picked = jnp.take(gathered, owner_ids, axis=0).reshape(-1, 2 * HD)  4.24 us
  transfers between devices with their start and end apart: 1, of which 1 were waited for; matrix products, arithmetic and copies ran while one was open for 2% of the time, Pallas kernels for 0%

profile of v7, /device:TPU:1, one launch (start us, length us, event | category | flops | bytes accessed | tf_op | source)
XLA Modules:
  0.0 185.5 jit_solution(10831843558595619699)
XLA Ops:
  0.0 1.2 dynamic_slice.24
  1.9 0.7 compare_and_fusion
  2.7 0.1 broadcast_in_dim.20
  2.8 1.1 constant_dynamic-slice_fusion.1
  3.9 0.7 fusion.42.refs_1_
  4.6 81.1 %prefix_gather.1 = (bf16[8,256,2560]{2,1,0:T(8,128)(2,1)}, bf16[16,256,512]{2,1,0:T(8,128)(2,1)}) custom-call(bf16[256,2560]{1,0:T(8,128)(2,1)} %refs_0_.1, bf16[256,512]{1,0:T(8,128)(2,1)} %fusion.42.refs_1_), custom_call_target="tpu_custom_call" | custom-call | bytes 29360128 | tf_op jit(solution)/shard_map/prefix_gather/pallas_call | solution.py:217
  85.7 0.0 copy-start.3
  85.8 4.2 %gather_fusion = bf16[8,256,512]{2,1,0:T(8,128)(2,1)} fusion(bf16[16,256,512]{2,1,0:T(8,128)(2,1)} %get-tuple-element.7, s32[1024]{0:T(1024)S(1)} %pad_clamp_fusion), kind=kCustom, calls=%fused_computation | custom fusion | bytes 4194336 | tf_op jit(solution)/shard_map/prefix_gather/jit(_take)/gather | solution.py:388
  90.0 1.8 bitcast_select_fusion
  91.8 0.2 collective-permute-start
  92.0 0.2 reduce-window.8
  92.1 1.1 fusion.39
  93.2 0.1 convert_reduce_fusion
  93.3 1.0 constant_dynamic-slice_fusion
  94.3 0.1 fusion.36
  94.5 1.1 fusion.41
  95.6 0.2 fusion.24
  95.8 0.4 collective-permute-done
  96.2 1.4 fusion.23
  97.5 1.6 fusion.54
  99.1 1.4 fusion
  100.5 3.4 %fusion.30.refs_0_ = bf16[512,256]{1,0:T(8,128)(2,1)} fusion(bf16[2048,512]{1,0:T(8,128)(2,1)} %collective-permute-done, bf16[2048,512]{1,0:T(8,128)(2,1)S(1)} %bitcast_select_fusion, bf16[512,256]{1,0:T(8,128)(2,1)S(1)} %constant_dynamic-slice_fusion, f32[512,4608]{1,0:T(8,128)S(1)} %get-tuple-element.16, f32[512]{0:T(512)S(1)} %get-tuple-element.15, ...), kind=kOutput, calls=%fused_computation.38 | convolution fusion | flops 1220018176 | bytes 14159872 | tf_op jit(solution)/shard_map/attention/dot_general | solution.py:416
  103.9 17.6 %out_projection.1 = bf16[8,512,256]{2,1,0:T(8,128)(2,1)} custom-call(bf16[512,256]{1,0:T(8,128)(2,1)} %fusion.30.refs_0_), custom_call_target="tpu_custom_call" | custom-call | bytes 4194304 | tf_op jit(solution)/shard_map/out_projection/pallas_call | solution.py:245
  121.5 9.5 %fusion.2 = (f32[512]{0:T(512)S(1)}, f32[512,2560,1]{1,0,2:T(8,128)S(1)}) fusion(bf16[8,512,256]{2,1,0:T(8,128)(2,1)} %out_projection.1, bf16[8,256,2560]{2,1,0:T(8,128)(2,1)} %get-tuple-element.8), kind=kOutput, calls=%fused_computation.7 | convolution fusion | flops 5371330048 | bytes 17827840 | tf_op jit(solution)/shard_map/out_projection/srd,sdc->rc/dot_general | solution.py:426
  131.0 1.2 multiply_reduce_fusion
  132.2 2.3 %copy-done.1 = f32[512,2560]{1,0:T(8,128)} copy-done((f32[512,2560]{1,0:T(8,128)}, f32[512,2560]{1,0:T(8,128)S(1)}, u32[]{:S(2)}) %copy-start.1) | copy-done | bytes 5242904
  134.5 6.5 %fusion.52 = f32[512,1280]{1,0:T(8,128)S(1)} fusion(bf16[2560,1280]{1,0:T(8,128)(2,1)} %param.29, f32[512,2560]{1,0:T(8,128)S(1)} %get-tuple-element.10, f32[2560]{0:T(1024)S(1)} %copy-done.7, f32[512]{0:T(512)S(1)} %add_rsqrt_fusion), kind=kOutput, calls=%fused_computation.76 | convolution fusion | flops 3359375360 | bytes 14430208 | tf_op jit(solution)/shard_map/feed_forward/dot_general | solution.py:433
  141.0 16.6 %fusion.35.refs_0_ = f32[512,2560]{1,0:T(8,128)} fusion(bf16[1280,2560]{1,0:T(8,128)(2,1)} %param.31, bf16[2560,1280]{1,0:T(8,128)(2,1)} %param.30, f32[512,1280]{1,0:T(8,128)S(1)} %fusion.52, f32[512,2560]{1,0:T(8,128)} %copy-done.1, f32[2560]{0:T(1024)S(1)} %copy-done.7, f32[512]{0:T(512)S(1)} %add_rsqrt_fusion), kind=kOutput, calls=%fused_computation.39 | convolution fusion | flops 6721372160 | bytes 26226688 | tf_op jit(solution)/shard_map/feed_forward/dot_general | solution.py:437
  157.6 2.5 %copy-done = f32[512,2560]{1,0:T(8,128)S(1)} copy-done((f32[512,2560]{1,0:T(8,128)S(1)}, f32[512,2560]{1,0:T(8,128)}, u32[]{:S(2)}) %copy-start) | copy-done | bytes 5242904
  160.1 23.3 %feed_forward.1 = f32[64,2560]{1,0:T(8,128)S(1)} custom-call(f32[512,2560]{1,0:T(8,128)S(1)} %copy-done), custom_call_target="tpu_custom_call" | custom-call | flops 1310720 | bytes 10485760 | tf_op jit(solution)/shard_map/feed_forward/pallas_call | solution.py:328
  183.4 0.1 multiply_reduce_fusion.1
  183.5 2.0 %add_convert_fusion = bf16[64,2560]{1,0:T(8,128)(2,1)} fusion(f32[64,2560]{1,0:T(8,128)S(1)} %feed_forward.1, f32[512,2560]{1,0:T(8,128)} %copy-done.1, s32[]{:T(128)S(6)} %select_n.55, f32[2560]{0:T(1024)S(1)} %copy-done.5, f32[64]{0:T(128)S(1)} %add_rsqrt_fusion.4), kind=kLoop, calls=%fused_computation.44 | loop fusion | flops 655360 | bytes 1648900 | tf_op jit(solution)/shard_map/convert_element_type | solution.py:439
  (24 shorter events, 0.1 us)
Async XLA Ops:
  85.7 6.2 %copy-start.9 = (s32[1,3]{1,0:T(1,128)S(1)}, s32[1,3]{1,0:T(1,128)}, u32[]{:S(2)}) copy-start(s32[1,3]{1,0:T(1,128)} %param.21) | copy-start | bytes 40
  85.7 8.6 %copy-start.3 = (bf16[512,256]{1,0:T(8,128)(2,1)S(1)}, bf16[512,256]{1,0:T(8,128)(2,1)}, u32[]{:S(2)}) copy-start(bf16[512,256]{1,0:T(8,128)(2,1)} %param.16) | copy-start | bytes 786436
  85.7 8.7 %copy-start.6 = (f32[256]{0:T(256)S(1)}, f32[256]{0:T(256)}, u32[]{:S(2)}) copy-start(f32[256]{0:T(256)} %param.20) | copy-start | bytes 3076
  91.8 5.7 %copy-start.8 = (f32[256]{0:T(256)S(1)}, f32[256]{0:T(256)}, u32[]{:S(2)}) copy-start(f32[256]{0:T(256)} %param.19) | copy-start | bytes 3076
  91.8 4.4 %collective-permute-start = (bf16[2048,512]{1,0:T(8,128)(2,1)S(1)}, bf16[2048,512]{1,0:T(8,128)(2,1)}, u32[]{:S(2)}, u32[]{:S(2)}) collective-permute-start(bf16[2048,512]{1,0:T(8,128)(2,1)S(1)} %bitcast_select_fusion), channel_id=1, source_target_pairs={{0,1},{1,0},{2,3},{3,2},{4,5},{5,4},{6,7},{7,6},{8,9},{9,8},{10,11... | collective-permute-start | bytes 6291464 | tf_op jit(solution)/shard_map/prefix_gather/ppermute | solution.py:390
  121.5 9.5 %copy-start.2 = (bf16[512,2560]{1,0:T(8,128)(2,1)S(1)}, bf16[512,2560]{1,0:T(8,128)(2,1)}, u32[]{:S(2)}) copy-start(bf16[512,2560]{1,0:T(8,128)(2,1)} %param.24) | copy-start | bytes 7864324
  121.5 9.5 %copy-start.4 = (f32[2560]{0:T(1024)S(1)}, f32[2560]{0:T(1024)}, u32[]{:S(2)}) copy-start(f32[2560]{0:T(1024)} %param.26) | copy-start | bytes 30724
  131.0 3.5 %copy-start.7 = (f32[2560]{0:T(1024)S(1)}, f32[2560]{0:T(1024)}, u32[]{:S(2)}) copy-start(f32[2560]{0:T(1024)} %param.27) | copy-start | bytes 30724
  132.2 2.3 %copy-start.1 = (f32[512,2560]{1,0:T(8,128)}, f32[512,2560]{1,0:T(8,128)S(1)}, u32[]{:S(2)}) copy-start(f32[512,2560]{1,0:T(8,128)S(1)} %get-tuple-element.10) | copy-start | bytes 15728644
  157.6 2.5 %copy-start = (f32[512,2560]{1,0:T(8,128)S(1)}, f32[512,2560]{1,0:T(8,128)}, u32[]{:S(2)}) copy-start(f32[512,2560]{1,0:T(8,128)} %fusion.35.refs_0_) | copy-start | bytes 15728644
  160.1 23.4 %copy-start.5 = (f32[2560]{0:T(1024)S(1)}, f32[2560]{0:T(1024)}, u32[]{:S(2)}) copy-start(f32[2560]{0:T(1024)} %param.28) | copy-start | bytes 30724

commit v8 on v5

--- a/solution.py
+++ b/solution.py
@@ -108,6 +108,125 @@
             flops=0, transcendentals=0, bytes_accessed=2 * tok_count * rows * cols * 2
         ),
     )(block)
+
+
+def project_tok_kernel(
+    tok_count, att_ref, w_hbm, out_ref, att_all, w_buf, send_sem, recv_sem, load_sem
+):
+    mesh_ids = pl.DeviceIdType.MESH
+    me = lax.axis_index("tok")
+    up = lax.rem(me + 2, tok_count)
+    down = lax.rem(me + tok_count - 2, tok_count)
+    far = lax.rem(me + 4, tok_count)
+    partner = me + 1 - 2 * lax.rem(me, 2)
+    half = att_ref.shape[0] // 2
+    cols = out_ref.shape[1]
+    tile = 512
+    tiles = cols // tile
+
+    barrier = pltpu.get_barrier_semaphore()
+    for peer in (up, down, partner):
+        pl.semaphore_signal(barrier, inc=1, device_id={"tok": peer}, device_id_type=mesh_ids)
+    pl.semaphore_wait(barrier, 3)
+
+    def remote(src, dst, slot, peer):
+        return pltpu.make_async_remote_copy(
+            src_ref=src,
+            dst_ref=dst,
+            send_sem=send_sem.at[slot],
+            recv_sem=recv_sem.at[slot],
+            device_id={"tok": peer},
+            device_id_type=mesh_ids,
+        )
+
+    theirs = (
+        partner,
+        lax.rem(partner + 2, tok_count),
+        lax.rem(partner + tok_count - 2, tok_count),
+        lax.rem(partner + 4, tok_count),
+    )
+    order = (me, down, up, far) + theirs
+
+    def load(idx):
+        return pltpu.make_async_copy(w_hbm.at[order[idx]], w_buf.at[idx % 2], load_sem.at[idx % 2])
+
+    def accumulate(idx, source, first):
+        load(idx).wait()
+        if idx + 1 < len(order):
+            load(idx + 1).start()
+        weights = w_buf.at[idx % 2]
+
+        def one_tile(col):
+            span = pl.ds(pl.multiple_of(col * tile, tile), tile)
+            term = jnp.dot(source[...], weights[:, span], preferred_element_type=jnp.float32)
+            if first:
+                out_ref[:, span] = term
+            else:
+                out_ref[:, span] = out_ref[:, span] + term
+
+        pl.loop(0, tiles)(one_tile)
+
+    load(0).start()
+    sends = []
+    to_up = remote(att_ref, att_all.at[me], 0, up)
+    to_down = remote(att_ref, att_all.at[me], 1, down)
+    to_up.start()
+    to_down.start()
+    sends += [to_up, to_down]
+    accumulate(0, att_ref, True)
+    remote(att_ref, att_all.at[down], 0, down).wait_recv()
+    remote(att_ref, att_all.at[up], 1, up).wait_recv()
+    first = pl.ds(0, half)
+    second = pl.ds(half, half)
+    fwd_up = remote(att_all.at[down, first], att_all.at[down, first], 2, up)
+    fwd_down = remote(att_all.at[up, second], att_all.at[up, second], 3, down)
+    fwd_up.start()
+    fwd_down.start()
+    sends += [fwd_up, fwd_down]
+    accumulate(1, att_all.at[down], False)
+    accumulate(2, att_all.at[up], False)
+    remote(att_all.at[far, first], att_all.at[far, first], 2, down).wait_recv()
+    remote(att_all.at[far, second], att_all.at[far, second], 3, up).wait_recv()
+    for idx, (src, slot) in enumerate(
+        ((att_ref, me), (att_all.at[up], up), (att_all.at[down], down), (att_all.at[far], far))
+    ):
+        copy = remote(src, att_all.at[slot], 4 + idx, partner)
+        copy.start()
+        sends.append(copy)
+    accumulate(3, att_all.at[far], False)
+    for idx, slot in enumerate(theirs):
+        remote(att_all.at[slot], att_all.at[slot], 4 + idx, partner).wait_recv()
+        accumulate(4 + idx, att_all.at[slot], False)
+    for copy in sends:
+        copy.wait_send()
+
+
+def project_over_tok(attention, w_all, tok_count, collective_id):
+    assert tok_count == 8
+    rows, width = attention.shape
+    cols = w_all.shape[2]
+    vmem = pltpu.MemorySpace.VMEM
+    return pl.pallas_call(
+        lambda *refs: project_tok_kernel(tok_count, *refs),
+        out_shape=jax.ShapeDtypeStruct((rows, cols), jnp.float32),
+        in_specs=[pl.BlockSpec(memory_space=vmem), pl.BlockSpec(memory_space=pl.ANY)],
+        out_specs=pl.BlockSpec(memory_space=vmem),
+        scratch_shapes=[
+            pltpu.VMEM((tok_count, rows, width), attention.dtype),
+            pltpu.VMEM((2, width, cols), w_all.dtype),
+            pltpu.SemaphoreType.DMA((8,)),
+            pltpu.SemaphoreType.DMA((8,)),
+            pltpu.SemaphoreType.DMA((2,)),
+        ],
+        compiler_params=pltpu.CompilerParams(
+            collective_id=collective_id, has_side_effects=True, vmem_limit_bytes=48 * 1024 * 1024
+        ),
+        cost_estimate=pl.CostEstimate(
+            flops=2 * rows * width * tok_count * cols,
+            transcendentals=0,
+            bytes_accessed=tok_count * width * cols * 2 + rows * cols * 4,
+        ),
+    )(attention, w_all)
 
 
 def scatter_tok_kernel(tok_count, part_ref, out_ref, chip_in, cross_out, cross_in, send_sem, recv_sem):
@@ -275,10 +394,7 @@
     share = row_count // tok_count
     first_row = tok_index * share
     with jax.named_scope("out_projection"):
-        attention_all = gather_over_tok(attention, tok_count, 1)
-        projected = jnp.einsum(
-            "srd,sdc->rc", attention_all, w_out_all, preferred_element_type=jnp.float32
-        )
+        projected = project_over_tok(attention, w_out_all, tok_count, 1)
         mixed_rows = residual.astype(jnp.float32) + rms_scale(projected, attn_gain)
         normed = rms_scale(mixed_rows, ffn_in_gain).astype(jnp.bfloat16)
         mixed_share = lax.dynamic_slice_in_dim(mixed_rows, first_row, share, 0)

time: 177 us -> 170 us (0.960)
  matrix products: 37.5 us -> 24.5 us
  Pallas kernels: 100 us -> 105 us
    pallas_call x0 -> x1, Pallas kernels: none -> 21.6 us  [project_over_tok(): pl.pallas_call(lambda *refs: project_tok_kernel(tok_count, *refs), out_sh...]
    pallas_call x2 -> x1, Pallas kernels: 77.2 us -> 59.5 us  [gather_over_tok(): pl.pallas_call(lambda *refs: gather_tok_kernel(tok_count, *refs), out_sha...]
    dot_general x1 -> x0, matrix products: 9.5 us -> none  [local(): jnp.einsum('srd,sdc->rc', attention_all, w_out_all, preferred_element_typ...]
    dot_general x1, matrix products: 6.5 us -> 3.65 us  [local(): gate = jnp.dot(normed, w_gate, preferred_element_type=jnp.float32)]
    unnamed x22 -> x26, local copies, waits for them, and re-layouts: 4.84 us -> 6.12 us
  transfers between devices with their start and end apart: 2 -> 2, of which waited for: 1 -> 1; matrix products, arithmetic and copies ran while one was open for 3% -> 3% of each run, Pallas kernels for 34% -> 35%
where the time goes in v8:
time: 170 us
  Pallas kernels  105 us (62%)
  matrix products  24.5 us (14%)
  between operations  14.3 us (8%)
  local copies, waits for them, and re-layouts  13.8 us (8%)
  other arithmetic  12 us (7%)
    pallas_call x1, Pallas kernels, gather_over_tok(): pl.pallas_call(lambda *refs: gather_tok_kernel(tok_count, *refs), out_sha...  59.5 us
    pallas_call x1, Pallas kernels, scatter_over_tok(): pl.pallas_call(lambda *refs: scatter_tok_kernel(tok_count, *refs), out_sh...  23.7 us
    pallas_call x1, Pallas kernels, project_over_tok(): pl.pallas_call(lambda *refs: project_tok_kernel(tok_count, *refs), out_sh...  21.6 us
    dot_general x1, matrix products, local(): jnp.dot(hidden, w_down, preferred_element_type=jnp.float32)  16.6 us
    unnamed x26, local copies, waits for them, and re-layouts  6.12 us
    gather x1, local copies, waits for them, and re-layouts, local(): picked = jnp.take(gathered, owner_ids, axis=0).reshape(-1, 2 * HD)  4.24 us
    dot_general x1, matrix products, local(): gate = jnp.dot(normed, w_gate, preferred_element_type=jnp.float32)  3.65 us
  transfers between devices with their start and end apart: 2, of which 1 were waited for; matrix products, arithmetic and copies ran while one was open for 3% of the time, Pallas kernels for 35%

profile of v8, /device:TPU:1, one launch (start us, length us, event | category | flops | bytes accessed | tf_op | source)
XLA Modules:
  0.0 169.9 jit_solution(8808316189512105804)
XLA Ops:
  6.5 1.1 constant_dynamic-slice_fusion.1
  7.6 0.7 fusion.39
  8.4 1.3 dynamic_slice.24
  10.3 59.5 %prefix_gather.1.refs_1_ = bf16[8,256,2560]{2,1,0:T(8,128)(2,1)} custom-call(bf16[256,2560]{1,0:T(8,128)(2,1)} %refs_0_.1), custom_call_target="tpu_custom_call" | custom-call | bytes 20971520 | tf_op jit(solution)/shard_map/prefix_gather/pallas_call | solution.py:96
  69.9 0.1 compare_and_fusion
  69.9 0.1 broadcast_in_dim.20
  70.1 4.2 %gather_fusion = bf16[8,256,512]{2,1,0:T(8,128)(2,1)} fusion(bf16[16,256,512]{2,1,0:T(8,128)(2,1)} %bitcast.9, s32[1024]{0:T(1024)S(1)} %pad_clamp_fusion), kind=kCustom, calls=%fused_computation | custom fusion | bytes 4194336 | tf_op jit(solution)/shard_map/prefix_gather/jit(_take)/gather | solution.py:360
  74.4 1.8 %bitcast_select_fusion = bf16[2048,512]{1,0:T(8,128)(2,1)S(1)} fusion(bf16[8,256,512]{2,1,0:T(8,128)(2,1)} %gather_fusion, pred[2048]{0:T(1024)(128)(4,1)S(1)} %broadcast_in_dim.21), kind=kLoop, calls=%fused_computation.31 | loop fusion | flops 1048576 | bytes 4196352 | tf_op jit(solution)/shard_map/prefix_gather/jit(_take)/select_n | solution.py:360
  76.1 0.2 collective-permute-start
  76.3 0.2 reduce-window.8
  76.5 1.1 fusion.36
  77.6 0.1 convert_reduce_fusion
  77.7 1.0 constant_dynamic-slice_fusion
  78.7 0.1 fusion.33
  78.9 1.1 fusion.38
  80.0 0.2 fusion.21
  80.2 0.3 collective-permute-done
  80.5 1.4 fusion.20
  81.9 1.6 fusion.50
  83.5 1.4 fusion
  84.9 2.7 %fusion.27.refs_0_ = bf16[512,256]{1,0:T(8,128)(2,1)S(1)} fusion(bf16[2048,512]{1,0:T(8,128)(2,1)} %collective-permute-done, bf16[2048,512]{1,0:T(8,128)(2,1)S(1)} %bitcast_select_fusion, bf16[512,256]{1,0:T(8,128)(2,1)S(1)} %constant_dynamic-slice_fusion, f32[512,4608]{1,0:T(8,128)S(1)} %get-tuple-element.16, f32[512]{0:T(512)S(1)} %get-tuple-element.15, ...), kind=kOutput, calls=%fused_computation.35 | convolution fusion | flops 1220018176 | bytes 14159872 | tf_op jit(solution)/shard_map/attention/dot_general | solution.py:388
  87.5 21.6 %out_projection.1 = f32[512,2560]{1,0:T(8,128)S(1)} custom-call(bf16[512,256]{1,0:T(8,128)(2,1)S(1)} %fusion.27.refs_0_, bf16[8,256,2560]{2,1,0:T(8,128)(2,1)} %prefix_gather.1.refs_1_), custom_call_target="tpu_custom_call" | custom-call | flops 5368709120 | bytes 15728640 | tf_op jit(solution)/shard_map/out_projection/pallas_call | solution.py:209
  109.2 0.4 multiply_reduce_fusion.1
  109.6 1.3 copy-done.2
  110.9 1.2 multiply_reduce_fusion
  112.2 2.3 %copy-done.1 = f32[512,2560]{1,0:T(8,128)} copy-done((f32[512,2560]{1,0:T(8,128)}, f32[512,2560]{1,0:T(8,128)S(1)}, u32[]{:S(2)}) %copy-start.1) | copy-done | bytes 5242904
  114.5 3.6 %fusion.49 = f32[512,1280]{1,0:T(8,128)S(1)} fusion(bf16[2560,1280]{1,0:T(8,128)(2,1)S(1)} %bitcast.12, f32[512,2560]{1,0:T(8,128)S(1)} %get-tuple-element.10, f32[2560]{0:T(1024)S(1)} %copy-done.8, f32[512]{0:T(512)S(1)} %add_rsqrt_fusion), kind=kOutput, calls=%fused_computation.73 | convolution fusion | flops 3359375360 | bytes 14430208 | tf_op jit(solution)/shard_map/feed_forward/dot_general | solution.py:402
  118.1 16.6 %fusion.32.refs_0_ = f32[512,2560]{1,0:T(8,128)} fusion(bf16[1280,2560]{1,0:T(8,128)(2,1)} %param.31, bf16[2560,1280]{1,0:T(8,128)(2,1)} %param.30, f32[512,1280]{1,0:T(8,128)S(1)} %fusion.49, f32[512,2560]{1,0:T(8,128)} %copy-done.1, f32[2560]{0:T(1024)S(1)} %copy-done.8, f32[512]{0:T(512)S(1)} %add_rsqrt_fusion), kind=kOutput, calls=%fused_computation.36 | convolution fusion | flops 6721372160 | bytes 26226688 | tf_op jit(solution)/shard_map/feed_forward/dot_general | solution.py:406
  134.7 2.5 %copy-done = f32[512,2560]{1,0:T(8,128)S(1)} copy-done((f32[512,2560]{1,0:T(8,128)S(1)}, f32[512,2560]{1,0:T(8,128)}, u32[]{:S(2)}) %copy-start) | copy-done | bytes 5242904
  137.2 23.7 %feed_forward.1 = f32[64,2560]{1,0:T(8,128)S(1)} custom-call(f32[512,2560]{1,0:T(8,128)S(1)} %copy-done), custom_call_target="tpu_custom_call" | custom-call | flops 1310720 | bytes 10485760 | tf_op jit(solution)/shard_map/feed_forward/pallas_call | solution.py:298
  160.9 0.1 multiply_reduce_fusion.2
  161.1 2.0 %add_convert_fusion = bf16[64,2560]{1,0:T(8,128)(2,1)} fusion(f32[64,2560]{1,0:T(8,128)S(1)} %feed_forward.1, f32[512,2560]{1,0:T(8,128)} %copy-done.1, s32[]{:T(128)S(6)} %select_n.55, f32[2560]{0:T(1024)S(1)} %copy-done.5, f32[64]{0:T(128)S(1)} %add_rsqrt_fusion.4), kind=kLoop, calls=%fused_computation.41 | loop fusion | flops 655360 | bytes 1648900 | tf_op jit(solution)/shard_map/convert_element_type | solution.py:408
  (34 shorter events, 0.2 us)
Async XLA Ops:
  6.5 63.5 %all-gather.3.cloned.1.call-start = ((), (), s32[]{:S(2)}) async-start(), calls=%async_computation | async-start | bytes 4456448 | tf_op jit(solution)/shard_map/prefix_gather/all_gather | solution.py:355
  10.3 59.5 %copy-start.7 = (s32[16]{0:T(128)S(1)}, s32[16]{0:T(128)}, u32[]{:S(2)}) copy-start(s32[16]{0:T(128)} %param.23) | copy-start | bytes 196
  70.1 6.3 %copy-start.10 = (s32[1,3]{1,0:T(1,128)S(1)}, s32[1,3]{1,0:T(1,128)}, u32[]{:S(2)}) copy-start(s32[1,3]{1,0:T(1,128)} %param.21) | copy-start | bytes 40
  70.1 8.6 %copy-start.3 = (bf16[512,256]{1,0:T(8,128)(2,1)S(1)}, bf16[512,256]{1,0:T(8,128)(2,1)}, u32[]{:S(2)}) copy-start(bf16[512,256]{1,0:T(8,128)(2,1)} %param.16) | copy-start | bytes 786436
  70.1 8.8 %copy-start.6 = (f32[256]{0:T(256)S(1)}, f32[256]{0:T(256)}, u32[]{:S(2)}) copy-start(f32[256]{0:T(256)} %param.20) | copy-start | bytes 3076
  76.1 5.7 %copy-start.9 = (f32[256]{0:T(256)S(1)}, f32[256]{0:T(256)}, u32[]{:S(2)}) copy-start(f32[256]{0:T(256)} %param.19) | copy-start | bytes 3076
  76.1 4.4 %collective-permute-start = (bf16[2048,512]{1,0:T(8,128)(2,1)S(1)}, bf16[2048,512]{1,0:T(8,128)(2,1)}, u32[]{:S(2)}, u32[]{:S(2)}) collective-permute-start(bf16[2048,512]{1,0:T(8,128)(2,1)S(1)} %bitcast_select_fusion), channel_id=1, source_target_pairs={{0,1},{1,0},{2,3},{3,2},{4,5},{5,4},{6,7},{7,6},{8,9},{9,8},{10,11... | collective-permute-start | bytes 6291464 | tf_op jit(solution)/shard_map/prefix_gather/ppermute | solution.py:362
  109.2 1.7 %copy-start.2 = (bf16[512,2560]{1,0:T(8,128)(2,1)S(1)}, bf16[512,2560]{1,0:T(8,128)(2,1)}, u32[]{:S(2)}) copy-start(bf16[512,2560]{1,0:T(8,128)(2,1)} %param.24) | copy-start | bytes 7864324
  109.2 1.7 %copy-start.4 = (f32[2560]{0:T(1024)S(1)}, f32[2560]{0:T(1024)}, u32[]{:S(2)}) copy-start(f32[2560]{0:T(1024)} %param.26) | copy-start | bytes 30724
  109.2 5.3 %slice-start = ((s8[6553600]{0:T(1024)(128)(4,1)}), s8[4194304]{0:T(1024)(128)(4,1)S(1)}, s32[]{:S(2)}) async-start(s8[6553600]{0:T(1024)(128)(4,1)} %bitcast.11), calls=%async_computation.1 | async-start | bytes 8388608
  110.9 3.6 %slice-start.1 = ((s8[6553600]{0:T(1024)(128)(4,1)}), s8[2359296]{0:T(1024)(128)(4,1)S(1)}, s32[]{:S(2)}) async-start(s8[6553600]{0:T(1024)(128)(4,1)} %bitcast.11), calls=%async_computation.2 | async-start | bytes 4718592
  110.9 3.6 %copy-start.8 = (f32[2560]{0:T(1024)S(1)}, f32[2560]{0:T(1024)}, u32[]{:S(2)}) copy-start(f32[2560]{0:T(1024)} %param.27) | copy-start | bytes 30724
  112.2 2.3 %copy-start.1 = (f32[512,2560]{1,0:T(8,128)}, f32[512,2560]{1,0:T(8,128)S(1)}, u32[]{:S(2)}) copy-start(f32[512,2560]{1,0:T(8,128)S(1)} %get-tuple-element.10) | copy-start | bytes 15728644
  134.7 2.5 %copy-start = (f32[512,2560]{1,0:T(8,128)S(1)}, f32[512,2560]{1,0:T(8,128)}, u32[]{:S(2)}) copy-start(f32[512,2560]{1,0:T(8,128)} %fusion.32.refs_0_) | copy-start | bytes 15728644
  137.2 23.9 %copy-start.5 = (f32[2560]{0:T(1024)S(1)}, f32[2560]{0:T(1024)}, u32[]{:S(2)}) copy-start(f32[2560]{0:T(1024)} %param.28) | copy-start | bytes 30724
Sparse Core Ops, SparseCore 0:
  9.5 54.8 all-gather.2

commit v9 on v8

--- a/solution.py
+++ b/solution.py
@@ -229,6 +229,69 @@
     )(attention, w_all)
 
 
+def cross_tok_kernel(tok_count, sums_ref, out_ref, cross_out, cross_in, send_sem, recv_sem):
+    mesh_ids = pl.DeviceIdType.MESH
+    me = lax.axis_index("tok")
+    up = lax.rem(me + 2, tok_count)
+    down = lax.rem(me + tok_count - 2, tok_count)
+    far = lax.rem(me + 4, tok_count)
+    lines = tok_count // 2
+
+    barrier = pltpu.get_barrier_semaphore()
+    for peer in (up, down, far):
+        pl.semaphore_signal(barrier, inc=1, device_id={"tok": peer}, device_id_type=mesh_ids)
+    pl.semaphore_wait(barrier, 3)
+
+    def remote(src, dst, slot, peer):
+        return pltpu.make_async_remote_copy(
+            src_ref=src,
+            dst_ref=dst,
+            send_sem=send_sem.at[slot],
+            recv_sem=recv_sem.at[slot],
+            device_id={"tok": peer},
+            device_id_type=mesh_ids,
+        )
+
+    sends = []
+    for src_idx, peer, dst_idx in ((0, up, 1), (1, down, 0), (2, far, 2)):
+        cross_out[src_idx] = sums_ref[lax.rem(peer // 2, lines)].astype(cross_out.dtype)
+        copy = remote(cross_out.at[src_idx], cross_in.at[dst_idx], dst_idx, peer)
+        copy.start()
+        sends.append(copy)
+    total = sums_ref[me // 2]
+    for idx, peer in ((0, up), (1, down), (2, far)):
+        remote(cross_out.at[idx], cross_in.at[idx], idx, peer).wait_recv()
+    for idx in range(3):
+        total = total + cross_in[idx].astype(jnp.float32)
+    out_ref[...] = total
+    for copy in sends:
+        copy.wait_send()
+
+
+def cross_over_tok(sums, tok_count, collective_id):
+    assert tok_count == 8
+    lines, share, cols = sums.shape
+    vmem = pltpu.MemorySpace.VMEM
+    return pl.pallas_call(
+        lambda *refs: cross_tok_kernel(tok_count, *refs),
+        out_shape=jax.ShapeDtypeStruct((share, cols), jnp.float32),
+        in_specs=[pl.BlockSpec(memory_space=vmem)],
+        out_specs=pl.BlockSpec(memory_space=vmem),
+        scratch_shapes=[
+            pltpu.VMEM((3, share, cols), jnp.bfloat16),
+            pltpu.VMEM((3, share, cols), jnp.bfloat16),
+            pltpu.SemaphoreType.DMA((3,)),
+            pltpu.SemaphoreType.DMA((3,)),
+        ],
+        compiler_params=pltpu.CompilerParams(
+            collective_id=collective_id, has_side_effects=True, vmem_limit_bytes=32 * 1024 * 1024
+        ),
+        cost_estimate=pl.CostEstimate(
+            flops=4 * share * cols, transcendentals=0, bytes_accessed=lines * share * cols * 4 * 2
+        ),
+    )(sums)
+
+
 def scatter_tok_kernel(tok_count, part_ref, out_ref, chip_in, cross_out, cross_in, send_sem, recv_sem):
     mesh_ids = pl.DeviceIdType.MESH
     me = lax.axis_index("tok")
@@ -398,13 +461,23 @@
         mixed_rows = residual.astype(jnp.float32) + rms_scale(projected, attn_gain)
         normed = rms_scale(mixed_rows, ffn_in_gain).astype(jnp.bfloat16)
         mixed_share = lax.dynamic_slice_in_dim(mixed_rows, first_row, share, 0)
+    def feed_forward(rows_in):
+        gate = jnp.dot(rows_in, w_gate, preferred_element_type=jnp.float32)
+        upward = jnp.dot(rows_in, w_up, preferred_element_type=jnp.float32)
+        hidden = (jax.nn.gelu(gate, approximate=True) * upward).astype(jnp.bfloat16)
+        return jnp.dot(hidden, w_down, preferred_element_type=jnp.float32)
+
     with jax.named_scope("feed_forward"):
-        gate = jnp.dot(normed, w_gate, preferred_element_type=jnp.float32)
-        upward = jnp.dot(normed, w_up, preferred_element_type=jnp.float32)
-        hidden = (jax.nn.gelu(gate, approximate=True) * upward).astype(jnp.bfloat16)
-        down_share = scatter_over_tok(
-            jnp.dot(hidden, w_down, preferred_element_type=jnp.float32), tok_count, 2
-        )
+        core = tok_index % 2
+        by_parity = normed.reshape(tok_count // 2, 2, share, normed.shape[1])
+        theirs = lax.dynamic_index_in_dim(by_parity, 1 - core, axis=1, keepdims=False)
+        mine = lax.dynamic_index_in_dim(by_parity, core, axis=1, keepdims=False)
+        cols = normed.shape[1]
+        partner = [(t, t ^ 1) for t in range(tok_count)]
+        for_partner = feed_forward(theirs.reshape(-1, cols))
+        from_partner = lax.ppermute(for_partner, "tok", perm=partner)
+        chip_sums = feed_forward(mine.reshape(-1, cols)) + from_partner
+        down_share = cross_over_tok(chip_sums.reshape(tok_count // 2, share, cols), tok_count, 2)
     return (mixed_share + rms_scale(down_share.astype(jnp.float32), ffn_out_gain)).astype(
         jnp.bfloat16
     )

time: 170 us -> 174 us (1.024)
  matrix products: 24.5 us -> 34 us
  Pallas kernels: 105 us -> 99.3 us
  local copies, waits for them, and re-layouts: 13.8 us -> 12 us
    dot_general x2 -> x4, matrix products: 20.2 us -> 29.8 us  [the longest x2 20.9 us: feed_forward(): return jnp.dot(hidden, w_down, preferred_element_type=jnp.float32)]
    pallas_call x1, Pallas kernels: 23.7 us -> 18.2 us  [cross_over_tok(): pl.pallas_call(lambda *refs: cross_tok_kernel(tok_count, *refs), out_shap...]
    unnamed x26, local copies, waits for them, and re-layouts: 6.12 us -> 4.23 us
  transfers between devices with their start and end apart: 2 -> 3, of which waited for: 1 -> 1; matrix products, arithmetic and copies ran while one was open for 3% -> 6% of each run, Pallas kernels for 35% -> 34%
where the time goes in v9:
time: 174 us; the launch traced here: 173 us
  Pallas kernels  99.3 us (57%)
  matrix products  34 us (20%)
  between operations  14.3 us (8%)
  other arithmetic  12.5 us (7%)
  local copies, waits for them, and re-layouts  12 us (7%)
    pallas_call x1, Pallas kernels, gather_over_tok(): pl.pallas_call(lambda *refs: gather_tok_kernel(tok_count, *refs), out_sha...  59.5 us
    pallas_call x1, Pallas kernels, project_over_tok(): pl.pallas_call(lambda *refs: project_tok_kernel(tok_count, *refs), out_sh...  21.6 us
    dot_general x2, matrix products, feed_forward(): return jnp.dot(hidden, w_down, preferred_element_type=jnp.float32)  20.9 us
    pallas_call x1, Pallas kernels, cross_over_tok(): pl.pallas_call(lambda *refs: cross_tok_kernel(tok_count, *refs), out_shap...  18.2 us
    dot_general x2, matrix products, feed_forward(): gate = jnp.dot(rows_in, w_gate, preferred_element_type=jnp.float32)  8.84 us
    unnamed x26, local copies, waits for them, and re-layouts  4.23 us
    gather x1, local copies, waits for them, and re-layouts, local(): picked = jnp.take(gathered, owner_ids, axis=0).reshape(-1, 2 * HD)  4.2 us
  transfers between devices with their start and end apart: 3, of which 1 were waited for; matrix products, arithmetic and copies ran while one was open for 6% of the time, Pallas kernels for 34%

profile of v9, /device:TPU:1, one launch (start us, length us, event | category | flops | bytes accessed | tf_op | source)
XLA Modules:
  0.0 173.2 jit_solution(8352912774711524612)
XLA Ops:
  6.5 1.1 constant_dynamic-slice_fusion.3
  7.6 0.7 fusion.47
  8.4 1.3 dynamic_slice.31
  10.3 59.5 %prefix_gather.1.refs_1_ = bf16[8,256,2560]{2,1,0:T(8,128)(2,1)} custom-call(bf16[256,2560]{1,0:T(8,128)(2,1)} %refs_0_.1), custom_call_target="tpu_custom_call" | custom-call | bytes 20971520 | tf_op jit(solution)/shard_map/prefix_gather/pallas_call | solution.py:96
  70.1 4.2 %gather_fusion = bf16[8,256,512]{2,1,0:T(8,128)(2,1)} fusion(bf16[16,256,512]{2,1,0:T(8,128)(2,1)} %bitcast.26, s32[1024]{0:T(1024)S(1)} %pad_clamp_fusion), kind=kCustom, calls=%fused_computation | custom fusion | bytes 4194336 | tf_op jit(solution)/shard_map/prefix_gather/jit(_take)/gather | solution.py:423
  74.3 1.8 %bitcast_select_fusion = bf16[2048,512]{1,0:T(8,128)(2,1)S(1)} fusion(bf16[8,256,512]{2,1,0:T(8,128)(2,1)} %gather_fusion, pred[2048]{0:T(1024)(128)(4,1)S(1)} %broadcast_in_dim.21), kind=kLoop, calls=%fused_computation.26 | loop fusion | flops 1048576 | bytes 4196352 | tf_op jit(solution)/shard_map/prefix_gather/jit(_take)/select_n | solution.py:423
  76.1 0.2 collective-permute-start
  76.3 0.2 reduce-window.8
  76.5 1.1 fusion.44
  77.7 1.0 constant_dynamic-slice_fusion.2
  78.8 1.1 fusion.46
  79.9 0.2 fusion.29
  80.2 0.3 collective-permute-done
  80.5 1.4 fusion.14
  81.8 1.6 fusion.61
  83.4 1.4 fusion
  84.8 2.7 %fusion.35.refs_0_ = bf16[512,256]{1,0:T(8,128)(2,1)S(1)} fusion(bf16[2048,512]{1,0:T(8,128)(2,1)} %collective-permute-done, bf16[2048,512]{1,0:T(8,128)(2,1)S(1)} %bitcast_select_fusion, bf16[512,256]{1,0:T(8,128)(2,1)S(1)} %constant_dynamic-slice_fusion.2, f32[512,4608]{1,0:T(8,128)S(1)} %get-tuple-element.18, f32[512]{0:T(512)S(1)} %get-tuple-element.17, ...), kind=kOutput, calls=%fused_computation.46 | convolution fusion | flops 1220018176 | bytes 14159872 | tf_op jit(solution)/shard_map/attention/dot_general | solution.py:451
  87.5 21.6 %out_projection.1 = f32[512,2560]{1,0:T(8,128)S(1)} custom-call(bf16[512,256]{1,0:T(8,128)(2,1)S(1)} %fusion.35.refs_0_, bf16[8,256,2560]{2,1,0:T(8,128)(2,1)} %prefix_gather.1.refs_1_), custom_call_target="tpu_custom_call" | custom-call | flops 5368709120 | bytes 15728640 | tf_op jit(solution)/shard_map/out_projection/pallas_call | solution.py:209
  109.2 0.4 multiply_reduce_fusion.1
  109.6 1.3 copy-done.1
  110.9 1.2 multiply_reduce_fusion
  112.2 0.5 multiply_convert_fusion
  112.7 2.0 %copy-done = f32[512,2560]{1,0:T(8,128)} copy-done((f32[512,2560]{1,0:T(8,128)}, f32[512,2560]{1,0:T(8,128)S(1)}, u32[]{:S(2)}) %copy-start) | copy-done | bytes 5242904
  114.7 0.2 constant_dynamic-slice_fusion.1
  114.9 0.9 slice-done.1
  115.8 3.0 %fusion.63 = f32[256,1280]{1,0:T(8,128)} fusion(bf16[256,2560]{1,0:T(8,128)(2,1)S(1)} %bitcast.24, bf16[2560,1280]{1,0:T(8,128)(2,1)S(1)} %bitcast.29), kind=kOutput, calls=%fused_computation.92 | convolution fusion | flops 1677721600 | bytes 9175040 | tf_op jit(solution)/shard_map/feed_forward/dot_general | solution.py:465
  118.8 10.7 %fusion.40 = f32[256,2560]{1,0:T(8,128)} fusion(bf16[1280,2560]{1,0:T(8,128)(2,1)} %param.31, bf16[256,2560]{1,0:T(8,128)(2,1)S(1)} %bitcast.25, bf16[2560,1280]{1,0:T(8,128)(2,1)} %param.30, f32[256,1280]{1,0:T(8,128)} %fusion.63), kind=kOutput, calls=%fused_computation.53 | convolution fusion | flops 3358720000 | bytes 18350080 | tf_op jit(solution)/shard_map/feed_forward/dot_general | solution.py:468
  129.5 0.5 collective-permute-start.1
  130.0 5.8 %fusion.62 = f32[256,1280]{1,0:T(8,128)} fusion(bf16[256,2560]{1,0:T(8,128)(2,1)S(1)} %bitcast.22, bf16[2560,1280]{1,0:T(8,128)(2,1)} %param.29), kind=kOutput, calls=%fused_computation.91 | convolution fusion | flops 1677721600 | bytes 9175040 | tf_op jit(solution)/shard_map/feed_forward/dot_general | solution.py:465
  135.8 10.3 %convolution_add_fusion = f32[256,2560]{1,0:T(8,128)S(1)} fusion(f32[256,2560]{1,0:T(8,128)} %collective-permute-done.1, bf16[1280,2560]{1,0:T(8,128)(2,1)} %param.31, bf16[256,2560]{1,0:T(8,128)(2,1)} %bitcast.23, bf16[2560,1280]{1,0:T(8,128)(2,1)} %param.30, f32[256,1280]{1,0:T(8,128)} %fusion.62), kind=kOutput, calls=%fused_computation.13 | convolution fusion | flops 3359375360 | bytes 20971520 | tf_op jit(solution)/shard_map/feed_forward/dot_general | solution.py:468
  146.1 18.2 %feed_forward.1 = f32[64,2560]{1,0:T(8,128)S(1)} custom-call(f32[4,64,2560]{2,1,0:T(8,128)S(1)} %bitcast.20), custom_call_target="tpu_custom_call" | custom-call | flops 655360 | bytes 5242880 | tf_op jit(solution)/shard_map/feed_forward/pallas_call | solution.py:275
  164.4 2.0 %add_convert_fusion = bf16[64,2560]{1,0:T(8,128)(2,1)} fusion(f32[64,2560]{1,0:T(8,128)S(1)} %feed_forward.1, f32[512,2560]{1,0:T(8,128)} %copy-done, s32[]{:T(128)S(6)} %select_n.64, f32[2560]{0:T(1024)S(1)} %copy-done.6, f32[64]{0:T(128)S(1)} %add_rsqrt_fusion.4), kind=kLoop, calls=%fused_computation.51 | loop fusion | flops 655360 | bytes 1648900 | tf_op jit(solution)/shard_map/convert_element_type | solution.py:481
  (40 shorter events, 0.7 us)
Async XLA Ops:
  6.5 63.5 %all-gather.3.cloned.1.call-start = ((), (), s32[]{:S(2)}) async-start(), calls=%async_computation | async-start | bytes 4456448 | tf_op jit(solution)/shard_map/prefix_gather/all_gather | solution.py:418
  10.3 59.5 %copy-start.8 = (s32[16]{0:T(128)S(1)}, s32[16]{0:T(128)}, u32[]{:S(2)}) copy-start(s32[16]{0:T(128)} %param.23) | copy-start | bytes 196
  74.3 2.0 %copy-start.10 = (s32[1,3]{1,0:T(1,128)S(1)}, s32[1,3]{1,0:T(1,128)}, u32[]{:S(2)}) copy-start(s32[1,3]{1,0:T(1,128)} %param.21) | copy-start | bytes 40
  74.3 4.4 %copy-start.3 = (bf16[512,256]{1,0:T(8,128)(2,1)S(1)}, bf16[512,256]{1,0:T(8,128)(2,1)}, u32[]{:S(2)}) copy-start(bf16[512,256]{1,0:T(8,128)(2,1)} %param.16) | copy-start | bytes 786436
  74.3 4.6 %copy-start.7 = (f32[256]{0:T(256)S(1)}, f32[256]{0:T(256)}, u32[]{:S(2)}) copy-start(f32[256]{0:T(256)} %param.20) | copy-start | bytes 3076
  76.1 4.4 %collective-permute-start = (bf16[2048,512]{1,0:T(8,128)(2,1)S(1)}, bf16[2048,512]{1,0:T(8,128)(2,1)}, u32[]{:S(2)}, u32[]{:S(2)}) collective-permute-start(bf16[2048,512]{1,0:T(8,128)(2,1)S(1)} %bitcast_select_fusion), channel_id=1, source_target_pairs={{0,1},{1,0},{2,3},{3,2},{4,5},{5,4},{6,7},{7,6},{8,9},{9,8},{10,11... | collective-permute-start | bytes 6291464 | tf_op jit(solution)/shard_map/prefix_gather/ppermute | solution.py:425
  80.1 1.7 copy-start.9
  109.2 1.7 %copy-start.1 = (bf16[512,2560]{1,0:T(8,128)(2,1)S(1)}, bf16[512,2560]{1,0:T(8,128)(2,1)}, u32[]{:S(2)}) copy-start(bf16[512,2560]{1,0:T(8,128)(2,1)} %param.24) | copy-start | bytes 7864324
  109.2 1.7 %copy-start.4 = (f32[2560]{0:T(1024)S(1)}, f32[2560]{0:T(1024)}, u32[]{:S(2)}) copy-start(f32[2560]{0:T(1024)} %param.26) | copy-start | bytes 30724
  110.9 1.3 copy-start.5
  110.9 4.0 %slice-start = ((s8[6553600]{0:T(1024)(128)(4,1)}), s8[4194304]{0:T(1024)(128)(4,1)S(1)}, s32[]{:S(2)}) async-start(s8[6553600]{0:T(1024)(128)(4,1)} %bitcast.28), calls=%async_computation.1 | async-start | bytes 8388608
  112.1 2.6 %copy-start = (f32[512,2560]{1,0:T(8,128)}, f32[512,2560]{1,0:T(8,128)S(1)}, u32[]{:S(2)}) copy-start(f32[512,2560]{1,0:T(8,128)S(1)} %get-tuple-element.10) | copy-start | bytes 15728644
  112.2 3.6 %slice-start.1 = ((s8[6553600]{0:T(1024)(128)(4,1)}), s8[2359296]{0:T(1024)(128)(4,1)S(1)}, s32[]{:S(2)}) async-start(s8[6553600]{0:T(1024)(128)(4,1)} %bitcast.28), calls=%async_computation.2 | async-start | bytes 4718592
  114.9 15.0 %copy-start.2 = (bf16[4,1,64,2560]{3,2,1,0:T(8,128)(2,1)}, bf16[4,1,64,2560]{3,2,1,0:T(8,128)(2,1)S(1)}, u32[]{:S(2)}) copy-start(bf16[4,1,64,2560]{3,2,1,0:T(8,128)(2,1)S(1)} %get-tuple-element.13) | copy-start | bytes 3932164
  129.5 6.3 %collective-permute-start.1 = (f32[256,2560]{1,0:T(8,128)}, f32[256,2560]{1,0:T(8,128)}, u32[]{:S(2)}, u32[]{:S(2)}) collective-permute-start(f32[256,2560]{1,0:T(8,128)} %fusion.40), channel_id=1, source_target_pairs={{0,1},{1,0},{2,3},{3,2},{4,5},{5,4},{6,7},{7,6},{8,9},{9,8},{10,11... | collective-permute-start | bytes 7864328 | tf_op jit(solution)/shard_map/feed_forward/ppermute | solution.py:478
  146.0 18.3 %copy-start.6 = (f32[2560]{0:T(1024)S(1)}, f32[2560]{0:T(1024)}, u32[]{:S(2)}) copy-start(f32[2560]{0:T(1024)} %param.28) | copy-start | bytes 30724
Sparse Core Ops, SparseCore 0:
  9.5 54.8 all-gather.2

commit v10 on v8

--- a/solution.py
+++ b/solution.py
@@ -229,7 +229,9 @@
     )(attention, w_all)
 
 
-def scatter_tok_kernel(tok_count, part_ref, out_ref, chip_in, cross_out, cross_in, send_sem, recv_sem):
+def scatter_tok_kernel(
+    tok_count, part_hbm, out_ref, mine, chip_in, cross_out, cross_in, load_sem, send_sem, recv_sem
+):
     mesh_ids = pl.DeviceIdType.MESH
     me = lax.axis_index("tok")
     up = lax.rem(me + 2, tok_count)
@@ -264,23 +266,31 @@
     def rows_of(block):
         return pl.ds(pl.multiple_of(block * share, share), share)
 
+    order = (3, 1, 2, 0)
     sends = []
-    for idx, block in enumerate(family(partner)):
-        copy = remote(part_ref.at[rows_of(block)], chip_in.at[idx], idx, partner)
+    theirs = family(partner)
+    for idx in order:
+        copy = remote(part_hbm.at[rows_of(theirs[idx])], chip_in.at[idx], idx, partner)
         copy.start()
         sends.append(copy)
-    mine = family(me)
-    for idx in range(4):
-        remote(part_ref.at[rows_of(mine[idx])], chip_in.at[idx], idx, partner).wait_recv()
-
-    for idx in range(1, 4):
-        summed = part_ref[rows_of(mine[idx]), :] + chip_in[idx]
-        cross_out[idx - 1] = summed.astype(cross_out.dtype)
-    for src_idx, dst_idx, peer in ((0, 1, up), (1, 0, down), (2, 2, far)):
-        copy = remote(cross_out.at[src_idx], cross_in.at[dst_idx], 4 + dst_idx, peer)
+    own = family(me)
+    loads = []
+    for idx in order:
+        load = pltpu.make_async_copy(part_hbm.at[rows_of(own[idx])], mine.at[idx], load_sem.at[idx])
+        load.start()
+        loads.append(load)
+    targets = {1: (up, 1), 2: (down, 0), 3: (far, 2)}
+    for pos, idx in enumerate(order[:3]):
+        loads[pos].wait()
+        remote(part_hbm.at[rows_of(own[idx])], chip_in.at[idx], idx, partner).wait_recv()
+        cross_out[idx - 1] = (mine[idx] + chip_in[idx]).astype(cross_out.dtype)
+        peer, dst_idx = targets[idx]
+        copy = remote(cross_out.at[idx - 1], cross_in.at[dst_idx], 4 + dst_idx, peer)
         copy.start()
         sends.append(copy)
-    total = part_ref[rows_of(me), :] + chip_in[0]
+    loads[3].wait()
+    remote(part_hbm.at[rows_of(own[0])], chip_in.at[0], 0, partner).wait_recv()
+    total = mine[0] + chip_in[0]
     for idx, peer in ((0, up), (1, down), (2, far)):
         remote(cross_out.at[idx], cross_in.at[idx], 4 + idx, peer).wait_recv()
     for idx in range(3):
@@ -298,12 +308,14 @@
     return pl.pallas_call(
         lambda *refs: scatter_tok_kernel(tok_count, *refs),
         out_shape=jax.ShapeDtypeStruct((share, cols), jnp.float32),
-        in_specs=[pl.BlockSpec(memory_space=vmem)],
+        in_specs=[pl.BlockSpec(memory_space=pl.ANY)],
         out_specs=pl.BlockSpec(memory_space=vmem),
         scratch_shapes=[
             pltpu.VMEM((4, share, cols), jnp.float32),
+            pltpu.VMEM((4, share, cols), jnp.float32),
             pltpu.VMEM((3, share, cols), jnp.bfloat16),
             pltpu.VMEM((3, share, cols), jnp.bfloat16),
+            pltpu.SemaphoreType.DMA((4,)),
             pltpu.SemaphoreType.DMA((7,)),
             pltpu.SemaphoreType.DMA((7,)),
         ],

time: 170 us -> 168 us (0.988)
  Pallas kernels: 105 us -> 102 us
    pallas_call x1, Pallas kernels: 23.7 us -> 20.9 us  [scatter_over_tok(): pl.pallas_call(lambda *refs: scatter_tok_kernel(tok_count, *refs), out_sh...]
  transfers between devices with their start and end apart: 2 -> 2, of which waited for: 1 -> 1; matrix products, arithmetic and copies ran while one was open for 3% -> 3% of each run, Pallas kernels for 35% -> 36%
where the time goes in v10:
time: 168 us; the launch traced here: 167 us
  Pallas kernels  102 us (61%)
  matrix products  24.5 us (15%)
  between operations  14.3 us (9%)
  local copies, waits for them, and re-layouts  13.8 us (8%)
  other arithmetic  12 us (7%)
    pallas_call x1, Pallas kernels, gather_over_tok(): pl.pallas_call(lambda *refs: gather_tok_kernel(tok_count, *refs), out_sha...  59.5 us
    pallas_call x1, Pallas kernels, project_over_tok(): pl.pallas_call(lambda *refs: project_tok_kernel(tok_count, *refs), out_sh...  21.6 us
    pallas_call x1, Pallas kernels, scatter_over_tok(): pl.pallas_call(lambda *refs: scatter_tok_kernel(tok_count, *refs), out_sh...  20.9 us
    dot_general x1, matrix products, local(): jnp.dot(hidden, w_down, preferred_element_type=jnp.float32)  16.6 us
    unnamed x26, local copies, waits for them, and re-layouts  6.12 us
    gather x1, local copies, waits for them, and re-layouts, local(): picked = jnp.take(gathered, owner_ids, axis=0).reshape(-1, 2 * HD)  4.24 us
    dot_general x1, matrix products, local(): gate = jnp.dot(normed, w_gate, preferred_element_type=jnp.float32)  3.65 us
  transfers between devices with their start and end apart: 2, of which 1 were waited for; matrix products, arithmetic and copies ran while one was open for 3% of the time, Pallas kernels for 36%

profile of v10, /device:TPU:1, one launch (start us, length us, event | category | flops | bytes accessed | tf_op | source)
XLA Modules:
  0.0 167.1 jit_solution(6911862666897715840)
XLA Ops:
  6.5 1.1 constant_dynamic-slice_fusion.1
  7.6 0.7 fusion.39
  8.4 1.3 dynamic_slice.24
  10.3 59.5 %prefix_gather.1.refs_1_ = bf16[8,256,2560]{2,1,0:T(8,128)(2,1)} custom-call(bf16[256,2560]{1,0:T(8,128)(2,1)} %refs_0_.1), custom_call_target="tpu_custom_call" | custom-call | bytes 20971520 | tf_op jit(solution)/shard_map/prefix_gather/pallas_call | solution.py:96
  69.9 0.1 compare_and_fusion
  69.9 0.1 broadcast_in_dim.20
  70.1 4.2 %gather_fusion = bf16[8,256,512]{2,1,0:T(8,128)(2,1)} fusion(bf16[16,256,512]{2,1,0:T(8,128)(2,1)} %bitcast.9, s32[1024]{0:T(1024)S(1)} %pad_clamp_fusion), kind=kCustom, calls=%fused_computation | custom fusion | bytes 4194336 | tf_op jit(solution)/shard_map/prefix_gather/jit(_take)/gather | solution.py:372
  74.4 1.8 %bitcast_select_fusion = bf16[2048,512]{1,0:T(8,128)(2,1)S(1)} fusion(bf16[8,256,512]{2,1,0:T(8,128)(2,1)} %gather_fusion, pred[2048]{0:T(1024)(128)(4,1)S(1)} %broadcast_in_dim.21), kind=kLoop, calls=%fused_computation.31 | loop fusion | flops 1048576 | bytes 4196352 | tf_op jit(solution)/shard_map/prefix_gather/jit(_take)/select_n | solution.py:372
  76.1 0.2 collective-permute-start
  76.3 0.2 reduce-window.8
  76.5 1.1 fusion.36
  77.6 0.1 convert_reduce_fusion
  77.7 1.0 constant_dynamic-slice_fusion
  78.7 0.1 fusion.33
  78.9 1.1 fusion.38
  80.0 0.2 fusion.21
  80.2 0.3 collective-permute-done
  80.5 1.4 fusion.20
  81.9 1.6 fusion.50
  83.5 1.4 fusion
  84.9 2.7 %fusion.27.refs_0_ = bf16[512,256]{1,0:T(8,128)(2,1)S(1)} fusion(bf16[2048,512]{1,0:T(8,128)(2,1)} %collective-permute-done, bf16[2048,512]{1,0:T(8,128)(2,1)S(1)} %bitcast_select_fusion, bf16[512,256]{1,0:T(8,128)(2,1)S(1)} %constant_dynamic-slice_fusion, f32[512,4608]{1,0:T(8,128)S(1)} %get-tuple-element.16, f32[512]{0:T(512)S(1)} %get-tuple-element.15, ...), kind=kOutput, calls=%fused_computation.35 | convolution fusion | flops 1220018176 | bytes 14159872 | tf_op jit(solution)/shard_map/attention/dot_general | solution.py:400
  87.5 21.6 %out_projection.1 = f32[512,2560]{1,0:T(8,128)S(1)} custom-call(bf16[512,256]{1,0:T(8,128)(2,1)S(1)} %fusion.27.refs_0_, bf16[8,256,2560]{2,1,0:T(8,128)(2,1)} %prefix_gather.1.refs_1_), custom_call_target="tpu_custom_call" | custom-call | flops 5368709120 | bytes 15728640 | tf_op jit(solution)/shard_map/out_projection/pallas_call | solution.py:209
  109.2 0.4 multiply_reduce_fusion.1
  109.6 1.3 copy-done.2
  110.9 1.2 multiply_reduce_fusion
  112.2 2.3 %copy-done.1 = f32[512,2560]{1,0:T(8,128)} copy-done((f32[512,2560]{1,0:T(8,128)}, f32[512,2560]{1,0:T(8,128)S(1)}, u32[]{:S(2)}) %copy-start.1) | copy-done | bytes 5242904
  114.5 3.6 %fusion.49 = f32[512,1280]{1,0:T(8,128)S(1)} fusion(bf16[2560,1280]{1,0:T(8,128)(2,1)S(1)} %bitcast.12, f32[512,2560]{1,0:T(8,128)S(1)} %get-tuple-element.10, f32[2560]{0:T(1024)S(1)} %copy-done.8, f32[512]{0:T(512)S(1)} %add_rsqrt_fusion), kind=kOutput, calls=%fused_computation.73 | convolution fusion | flops 3359375360 | bytes 14430208 | tf_op jit(solution)/shard_map/feed_forward/dot_general | solution.py:414
  118.1 16.6 %fusion.32.refs_0_ = f32[512,2560]{1,0:T(8,128)} fusion(bf16[1280,2560]{1,0:T(8,128)(2,1)} %param.31, bf16[2560,1280]{1,0:T(8,128)(2,1)} %param.30, f32[512,1280]{1,0:T(8,128)S(1)} %fusion.49, f32[512,2560]{1,0:T(8,128)} %copy-done.1, f32[2560]{0:T(1024)S(1)} %copy-done.8, f32[512]{0:T(512)S(1)} %add_rsqrt_fusion), kind=kOutput, calls=%fused_computation.36 | convolution fusion | flops 6721372160 | bytes 26226688 | tf_op jit(solution)/shard_map/feed_forward/dot_general | solution.py:418
  134.7 2.5 %copy-done = f32[512,2560]{1,0:T(8,128)S(1)} copy-done((f32[512,2560]{1,0:T(8,128)S(1)}, f32[512,2560]{1,0:T(8,128)}, u32[]{:S(2)}) %copy-start) | copy-done | bytes 5242904
  137.2 20.9 %feed_forward.1 = f32[64,2560]{1,0:T(8,128)S(1)} custom-call(f32[512,2560]{1,0:T(8,128)S(1)} %copy-done), custom_call_target="tpu_custom_call" | custom-call | flops 1310720 | bytes 10485760 | tf_op jit(solution)/shard_map/feed_forward/pallas_call | solution.py:308
  158.1 0.1 multiply_reduce_fusion.2
  158.3 2.0 %add_convert_fusion = bf16[64,2560]{1,0:T(8,128)(2,1)} fusion(f32[64,2560]{1,0:T(8,128)S(1)} %feed_forward.1, f32[512,2560]{1,0:T(8,128)} %copy-done.1, s32[]{:T(128)S(6)} %select_n.55, f32[2560]{0:T(1024)S(1)} %copy-done.5, f32[64]{0:T(128)S(1)} %add_rsqrt_fusion.4), kind=kLoop, calls=%fused_computation.41 | loop fusion | flops 655360 | bytes 1648900 | tf_op jit(solution)/shard_map/convert_element_type | solution.py:420
  (34 shorter events, 0.2 us)
Async XLA Ops:
  6.5 63.5 %all-gather.3.cloned.1.call-start = ((), (), s32[]{:S(2)}) async-start(), calls=%async_computation | async-start | bytes 4456448 | tf_op jit(solution)/shard_map/prefix_gather/all_gather | solution.py:367
  10.3 59.5 %copy-start.7 = (s32[16]{0:T(128)S(1)}, s32[16]{0:T(128)}, u32[]{:S(2)}) copy-start(s32[16]{0:T(128)} %param.23) | copy-start | bytes 196
  70.1 6.3 %copy-start.10 = (s32[1,3]{1,0:T(1,128)S(1)}, s32[1,3]{1,0:T(1,128)}, u32[]{:S(2)}) copy-start(s32[1,3]{1,0:T(1,128)} %param.21) | copy-start | bytes 40
  70.1 8.6 %copy-start.3 = (bf16[512,256]{1,0:T(8,128)(2,1)S(1)}, bf16[512,256]{1,0:T(8,128)(2,1)}, u32[]{:S(2)}) copy-start(bf16[512,256]{1,0:T(8,128)(2,1)} %param.16) | copy-start | bytes 786436
  70.1 8.8 %copy-start.6 = (f32[256]{0:T(256)S(1)}, f32[256]{0:T(256)}, u32[]{:S(2)}) copy-start(f32[256]{0:T(256)} %param.20) | copy-start | bytes 3076
  76.1 5.7 %copy-start.9 = (f32[256]{0:T(256)S(1)}, f32[256]{0:T(256)}, u32[]{:S(2)}) copy-start(f32[256]{0:T(256)} %param.19) | copy-start | bytes 3076
  76.1 4.4 %collective-permute-start = (bf16[2048,512]{1,0:T(8,128)(2,1)S(1)}, bf16[2048,512]{1,0:T(8,128)(2,1)}, u32[]{:S(2)}, u32[]{:S(2)}) collective-permute-start(bf16[2048,512]{1,0:T(8,128)(2,1)S(1)} %bitcast_select_fusion), channel_id=1, source_target_pairs={{0,1},{1,0},{2,3},{3,2},{4,5},{5,4},{6,7},{7,6},{8,9},{9,8},{10,11... | collective-permute-start | bytes 6291464 | tf_op jit(solution)/shard_map/prefix_gather/ppermute | solution.py:374
  109.2 1.7 %copy-start.2 = (bf16[512,2560]{1,0:T(8,128)(2,1)S(1)}, bf16[512,2560]{1,0:T(8,128)(2,1)}, u32[]{:S(2)}) copy-start(bf16[512,2560]{1,0:T(8,128)(2,1)} %param.24) | copy-start | bytes 7864324
  109.2 1.7 %copy-start.4 = (f32[2560]{0:T(1024)S(1)}, f32[2560]{0:T(1024)}, u32[]{:S(2)}) copy-start(f32[2560]{0:T(1024)} %param.26) | copy-start | bytes 30724
  109.2 5.3 %slice-start = ((s8[6553600]{0:T(1024)(128)(4,1)}), s8[4194304]{0:T(1024)(128)(4,1)S(1)}, s32[]{:S(2)}) async-start(s8[6553600]{0:T(1024)(128)(4,1)} %bitcast.11), calls=%async_computation.1 | async-start | bytes 8388608
  110.9 3.6 %slice-start.1 = ((s8[6553600]{0:T(1024)(128)(4,1)}), s8[2359296]{0:T(1024)(128)(4,1)S(1)}, s32[]{:S(2)}) async-start(s8[6553600]{0:T(1024)(128)(4,1)} %bitcast.11), calls=%async_computation.2 | async-start | bytes 4718592
  110.9 3.6 %copy-start.8 = (f32[2560]{0:T(1024)S(1)}, f32[2560]{0:T(1024)}, u32[]{:S(2)}) copy-start(f32[2560]{0:T(1024)} %param.27) | copy-start | bytes 30724
  112.2 2.3 %copy-start.1 = (f32[512,2560]{1,0:T(8,128)}, f32[512,2560]{1,0:T(8,128)S(1)}, u32[]{:S(2)}) copy-start(f32[512,2560]{1,0:T(8,128)S(1)} %get-tuple-element.10) | copy-start | bytes 15728644
  134.7 2.5 %copy-start = (f32[512,2560]{1,0:T(8,128)S(1)}, f32[512,2560]{1,0:T(8,128)}, u32[]{:S(2)}) copy-start(f32[512,2560]{1,0:T(8,128)} %fusion.32.refs_0_) | copy-start | bytes 15728644
  137.2 21.1 %copy-start.5 = (f32[2560]{0:T(1024)S(1)}, f32[2560]{0:T(1024)}, u32[]{:S(2)}) copy-start(f32[2560]{0:T(1024)} %param.28) | copy-start | bytes 30724
Sparse Core Ops, SparseCore 0:
  9.5 54.8 all-gather.2

commit v11 on v10

--- a/solution.py
+++ b/solution.py
@@ -308,7 +308,7 @@
     return pl.pallas_call(
         lambda *refs: scatter_tok_kernel(tok_count, *refs),
         out_shape=jax.ShapeDtypeStruct((share, cols), jnp.float32),
-        in_specs=[pl.BlockSpec(memory_space=pl.ANY)],
+        in_specs=[pl.BlockSpec(memory_space=pltpu.MemorySpace.HBM)],
         out_specs=pl.BlockSpec(memory_space=vmem),
         scratch_shapes=[
             pltpu.VMEM((4, share, cols), jnp.float32),
@@ -411,9 +411,11 @@
         normed = rms_scale(mixed_rows, ffn_in_gain).astype(jnp.bfloat16)
         mixed_share = lax.dynamic_slice_in_dim(mixed_rows, first_row, share, 0)
     with jax.named_scope("feed_forward"):
+        normed = lax.optimization_barrier(normed)
         gate = jnp.dot(normed, w_gate, preferred_element_type=jnp.float32)
         upward = jnp.dot(normed, w_up, preferred_element_type=jnp.float32)
         hidden = (jax.nn.gelu(gate, approximate=True) * upward).astype(jnp.bfloat16)
+        hidden = lax.optimization_barrier(hidden)
         down_share = scatter_over_tok(
             jnp.dot(hidden, w_down, preferred_element_type=jnp.float32), tok_count, 2
         )

time: 168 us -> 155 us (0.923)
  matrix products: 24.5 us -> 17.3 us
  local copies, waits for them, and re-layouts: 13.8 us -> 9.4 us
    dot_general x1, matrix products: 16.6 us -> 5.7 us  [local(): jnp.dot(hidden, w_down, preferred_element_type=jnp.float32)]
    unnamed x26, local copies, waits for them, and re-layouts: 6.12 us -> 1.77 us
    dot_general x0 -> x1, matrix products: none -> 3.83 us  [local(): upward = jnp.dot(normed, w_up, preferred_element_type=jnp.float32)]
  transfers between devices with their start and end apart: 2 -> 2, of which waited for: 1 -> 1; matrix products, arithmetic and copies ran while one was open for 3% -> 3% of each run, Pallas kernels for 36% -> 38%
where the time goes in v11:
time: 155 us
  Pallas kernels  102 us (66%)
  matrix products  17.3 us (11%)
  between operations  14.3 us (9%)
  other arithmetic  11.4 us (7%)
  local copies, waits for them, and re-layouts  9.4 us (6%)
    pallas_call x1, Pallas kernels, gather_over_tok(): pl.pallas_call(lambda *refs: gather_tok_kernel(tok_count, *refs), out_sha...  59.5 us
    pallas_call x1, Pallas kernels, project_over_tok(): pl.pallas_call(lambda *refs: project_tok_kernel(tok_count, *refs), out_sh...  21.6 us
    pallas_call x1, Pallas kernels, scatter_over_tok(): pl.pallas_call(lambda *refs: scatter_tok_kernel(tok_count, *refs), out_sh...  21 us
    dot_general x1, matrix products, local(): jnp.dot(hidden, w_down, preferred_element_type=jnp.float32)  5.7 us
    gather x1, local copies, waits for them, and re-layouts, local(): picked = jnp.take(gathered, owner_ids, axis=0).reshape(-1, 2 * HD)  4.2 us
    dot_general x1, matrix products, local(): upward = jnp.dot(normed, w_up, preferred_element_type=jnp.float32)  3.83 us
    dot_general x1, matrix products, local(): gate = jnp.dot(normed, w_gate, preferred_element_type=jnp.float32)  3.54 us
  transfers between devices with their start and end apart: 2, of which 1 were waited for; matrix products, arithmetic and copies ran while one was open for 3% of the time, Pallas kernels for 38%

profile of v11, /device:TPU:1, one launch (start us, length us, event | category | flops | bytes accessed | tf_op | source)
XLA Modules:
  0.0 155.1 jit_solution(9059214792872378041)
XLA Ops:
  6.5 1.1 constant_dynamic-slice_fusion.1
  7.6 0.7 fusion.38
  8.4 1.3 dynamic_slice.24
  10.3 59.5 %prefix_gather.1.refs_1_ = bf16[8,256,2560]{2,1,0:T(8,128)(2,1)} custom-call(bf16[256,2560]{1,0:T(8,128)(2,1)} %refs_0_.1), custom_call_target="tpu_custom_call" | custom-call | bytes 20971520 | tf_op jit(solution)/shard_map/prefix_gather/pallas_call | solution.py:96
  69.9 0.1 compare_and_fusion
  70.1 4.2 %gather_fusion = bf16[8,256,512]{2,1,0:T(8,128)(2,1)} fusion(bf16[16,256,512]{2,1,0:T(8,128)(2,1)} %bitcast.12, s32[1024]{0:T(1024)S(1)} %pad_clamp_fusion), kind=kCustom, calls=%fused_computation | custom fusion | bytes 4194336 | tf_op jit(solution)/shard_map/prefix_gather/jit(_take)/gather | solution.py:372
  74.3 1.8 %bitcast_select_fusion = bf16[2048,512]{1,0:T(8,128)(2,1)S(1)} fusion(bf16[8,256,512]{2,1,0:T(8,128)(2,1)} %gather_fusion, pred[2048]{0:T(1024)(128)(4,1)S(1)} %broadcast_in_dim.21), kind=kLoop, calls=%fused_computation.31 | loop fusion | flops 1048576 | bytes 4196352 | tf_op jit(solution)/shard_map/prefix_gather/jit(_take)/select_n | solution.py:372
  76.1 0.2 collective-permute-start
  76.3 0.2 reduce-window.8
  76.5 1.1 fusion.35
  77.6 0.1 convert_reduce_fusion
  77.7 1.0 constant_dynamic-slice_fusion
  78.7 0.1 fusion.32
  78.8 1.1 fusion.37
  79.9 0.2 fusion.21
  80.2 0.3 collective-permute-done
  80.5 1.4 fusion.20
  81.9 1.6 %fusion.44 = (f32[512]{0:T(512)S(1)}, f32[512,4608]{1,0:T(8,128)S(1)}) fusion(bf16[512,256]{1,0:T(8,128)(2,1)S(1)} %fusion.37, bf16[4096,256]{1,0:T(8,128)(2,1)S(1)} %fusion.20, bf16[512,256]{1,0:T(8,128)(2,1)S(1)} %copy-done.1, f32[256]{0:T(256)S(1)} %copy-done.7, f32[512]{0:T(512)S(1)} %add_rsqrt_fusion.3, pred[512,512]{1,0:T(32,128)(4,1)S(1)} %fusion.21), kind=kOutput, calls=%fused_computation.68 | convolution fusion | flops 1220279808 | bytes 12325888 | tf_op jit(solution)/shard_map/attention/dot_general | solution.py:395
  83.4 1.4 fusion
  84.8 2.7 %fusion.27.refs_0_ = bf16[512,256]{1,0:T(8,128)(2,1)S(1)} fusion(bf16[2048,512]{1,0:T(8,128)(2,1)} %collective-permute-done, bf16[2048,512]{1,0:T(8,128)(2,1)S(1)} %bitcast_select_fusion, bf16[512,256]{1,0:T(8,128)(2,1)S(1)} %constant_dynamic-slice_fusion, f32[512,4608]{1,0:T(8,128)S(1)} %get-tuple-element.16, f32[512]{0:T(512)S(1)} %get-tuple-element.15, ...), kind=kOutput, calls=%fused_computation.35 | convolution fusion | flops 1220018176 | bytes 14159872 | tf_op jit(solution)/shard_map/attention/dot_general | solution.py:400
  87.5 21.6 %out_projection.1 = f32[512,2560]{1,0:T(8,128)S(1)} custom-call(bf16[512,256]{1,0:T(8,128)(2,1)S(1)} %fusion.27.refs_0_, bf16[8,256,2560]{2,1,0:T(8,128)(2,1)} %prefix_gather.1.refs_1_), custom_call_target="tpu_custom_call" | custom-call | flops 5368709120 | bytes 15728640 | tf_op jit(solution)/shard_map/out_projection/pallas_call | solution.py:209
  109.2 0.4 multiply_reduce_fusion.1
  109.6 1.3 copy-done
  110.9 1.2 multiply_reduce_fusion
  112.1 0.5 multiply_convert_fusion
  112.6 0.4 slice-done.1
  113.1 3.5 %fusion.45 = f32[512,1280]{1,0:T(8,128)S(1)} fusion(bf16[512,2560]{1,0:T(8,128)(2,1)S(1)} %multiply_convert_fusion, bf16[2560,1280]{1,0:T(8,128)(2,1)S(1)} %bitcast.15), kind=kOutput, calls=%fused_computation.69 | convolution fusion | flops 3355443200 | bytes 11796480 | tf_op jit(solution)/shard_map/feed_forward/dot_general | solution.py:415
  116.6 3.8 %fusion.5 = bf16[512,1280]{1,0:T(8,128)(2,1)S(1)} fusion(bf16[512,2560]{1,0:T(8,128)(2,1)S(1)} %multiply_convert_fusion, bf16[2560,1280]{1,0:T(8,128)(2,1)S(1)} %bitcast.17, f32[512,1280]{1,0:T(8,128)S(1)} %fusion.45), kind=kOutput, calls=%fused_computation.15 | convolution fusion | flops 3361996800 | bytes 13107200 | tf_op jit(solution)/shard_map/feed_forward/dot_general | solution.py:416
  120.5 5.7 %fusion.46.refs_0_ = f32[512,2560]{1,0:T(8,128)S(1)} fusion(bf16[512,1280]{1,0:T(8,128)(2,1)S(1)} %fusion.5, bf16[1280,2560]{1,0:T(8,128)(2,1)} %param.31), kind=kOutput, calls=%fused_computation.70 | convolution fusion | flops 3355443200 | bytes 13107200 | tf_op jit(solution)/shard_map/feed_forward/dot_general | solution.py:420
  126.2 21.0 %feed_forward.1 = f32[64,2560]{1,0:T(8,128)S(1)} custom-call(f32[512,2560]{1,0:T(8,128)S(1)} %fusion.46.refs_0_), custom_call_target="tpu_custom_call" | custom-call | flops 1310720 | bytes 10485760 | tf_op jit(solution)/shard_map/feed_forward/pallas_call | solution.py:308
  147.2 0.1 multiply_reduce_fusion.2
  147.4 0.9 add_convert_fusion
  (37 shorter events, 0.2 us)
Async XLA Ops:
  6.5 63.5 %all-gather.3.cloned.1.call-start = ((), (), s32[]{:S(2)}) async-start(), calls=%async_computation | async-start | bytes 4456448 | tf_op jit(solution)/shard_map/prefix_gather/all_gather | solution.py:367
  10.3 59.5 %copy-start.6 = (s32[16]{0:T(128)S(1)}, s32[16]{0:T(128)}, u32[]{:S(2)}) copy-start(s32[16]{0:T(128)} %param.23) | copy-start | bytes 196
  74.3 2.0 %copy-start.8 = (s32[1,3]{1,0:T(1,128)S(1)}, s32[1,3]{1,0:T(1,128)}, u32[]{:S(2)}) copy-start(s32[1,3]{1,0:T(1,128)} %param.21) | copy-start | bytes 40
  74.3 4.4 %copy-start.1 = (bf16[512,256]{1,0:T(8,128)(2,1)S(1)}, bf16[512,256]{1,0:T(8,128)(2,1)}, u32[]{:S(2)}) copy-start(bf16[512,256]{1,0:T(8,128)(2,1)} %param.16) | copy-start | bytes 786436
  74.3 4.6 %copy-start.5 = (f32[256]{0:T(256)S(1)}, f32[256]{0:T(256)}, u32[]{:S(2)}) copy-start(f32[256]{0:T(256)} %param.20) | copy-start | bytes 3076
  76.1 4.4 %collective-permute-start = (bf16[2048,512]{1,0:T(8,128)(2,1)S(1)}, bf16[2048,512]{1,0:T(8,128)(2,1)}, u32[]{:S(2)}, u32[]{:S(2)}) collective-permute-start(bf16[2048,512]{1,0:T(8,128)(2,1)S(1)} %bitcast_select_fusion), channel_id=1, source_target_pairs={{0,1},{1,0},{2,3},{3,2},{4,5},{5,4},{6,7},{7,6},{8,9},{9,8},{10,11... | collective-permute-start | bytes 6291464 | tf_op jit(solution)/shard_map/prefix_gather/ppermute | solution.py:374
  80.1 1.7 %copy-start.7 = (f32[256]{0:T(256)S(1)}, f32[256]{0:T(256)}, u32[]{:S(2)}) copy-start(f32[256]{0:T(256)} %param.19) | copy-start | bytes 3076
  109.2 1.7 %copy-start = (bf16[512,2560]{1,0:T(8,128)(2,1)S(1)}, bf16[512,2560]{1,0:T(8,128)(2,1)}, u32[]{:S(2)}) copy-start(bf16[512,2560]{1,0:T(8,128)(2,1)} %param.24) | copy-start | bytes 7864324
  109.2 1.7 %copy-start.2 = (f32[2560]{0:T(1024)S(1)}, f32[2560]{0:T(1024)}, u32[]{:S(2)}) copy-start(f32[2560]{0:T(1024)} %param.26) | copy-start | bytes 30724
  109.2 3.4 %slice-start = ((s8[6553600]{0:T(1024)(128)(4,1)}), s8[4194304]{0:T(1024)(128)(4,1)S(1)}, s32[]{:S(2)}) async-start(s8[6553600]{0:T(1024)(128)(4,1)} %bitcast.14), calls=%async_computation.1 | async-start | bytes 8388608
  110.9 1.2 copy-start.3
  110.9 2.2 %slice-start.1 = ((s8[6553600]{0:T(1024)(128)(4,1)}), s8[2359296]{0:T(1024)(128)(4,1)S(1)}, s32[]{:S(2)}) async-start(s8[6553600]{0:T(1024)(128)(4,1)} %bitcast.14), calls=%async_computation.2 | async-start | bytes 4718592
  112.1 4.5 %slice-start.2 = ((s8[6553600]{0:T(1024)(128)(4,1)}), s8[4194304]{0:T(1024)(128)(4,1)S(1)}, s32[]{:S(2)}) async-start(s8[6553600]{0:T(1024)(128)(4,1)} %bitcast.16), calls=%async_computation.3 | async-start | bytes 8388608
  113.1 3.6 %slice-start.3 = ((s8[6553600]{0:T(1024)(128)(4,1)}), s8[2359296]{0:T(1024)(128)(4,1)S(1)}, s32[]{:S(2)}) async-start(s8[6553600]{0:T(1024)(128)(4,1)} %bitcast.16), calls=%async_computation.4 | async-start | bytes 4718592
  126.2 21.2 %copy-start.4 = (f32[2560]{0:T(1024)S(1)}, f32[2560]{0:T(1024)}, u32[]{:S(2)}) copy-start(f32[2560]{0:T(1024)} %param.28) | copy-start | bytes 30724
Sparse Core Ops, SparseCore 0:
  9.5 54.8 all-gather.2

commit v12 on v11

--- a/solution.py
+++ b/solution.py
@@ -369,10 +369,12 @@
         gathered, w_out_all = lax.optimization_barrier((gathered, w_out_all))
         own_group = group_of[req_index]
         owner_ids = lax.dynamic_slice_in_dim(owner_order, own_group * own_count, own_count)
-        picked = jnp.take(gathered, owner_ids, axis=0).reshape(-1, 2 * HD)
+        picked = jnp.concatenate(
+            [lax.dynamic_index_in_dim(gathered, owner_ids[j], 0, keepdims=False) for j in range(own_count)],
+            axis=0,
+        )
         partner = [(t, t ^ 1) for t in range(tok_count)]
         swapped = lax.ppermute(picked, "tok", perm=partner)
-        shared = jnp.concatenate([picked, swapped], axis=0)
 
     with jax.named_scope("attention"):
         query_normed = norm_heads(queries, q_gain, heads_here)
@@ -380,27 +382,36 @@
             lax.dynamic_slice_in_dim(suffix_kv, kv_first * HD, HD, 1), k_gain, 1
         )
         suf_vals = lax.dynamic_slice_in_dim(suffix_kv, kv_width + kv_first * HD, HD, 1)
-        all_keys = jnp.concatenate([shared[:, :HD], suf_keys], axis=0)
-        all_vals = jnp.concatenate([shared[:, HD:], suf_vals], axis=0)
         seg_ends = jnp.cumsum(lengths[0])
         positions = jnp.arange(row_count, dtype=jnp.int32)
         segment = jnp.sum((positions[:, None] >= seg_ends[None, :]).astype(jnp.int32), axis=1)
         causal = (segment[:, None] == segment[None, :]) & (positions[None, :] <= positions[:, None])
-        visible = jnp.concatenate(
-            [jnp.ones((row_count, shared.shape[0]), jnp.bool_), causal], axis=1
+        key_sets = (
+            (picked[:, :HD], picked[:, HD:], None),
+            (swapped[:, :HD], swapped[:, HD:], None),
+            (suf_keys, suf_vals, causal),
         )
         outputs = []
         for head_idx in range(heads_here):
             head_q = query_normed[:, head_idx * HD:(head_idx + 1) * HD]
-            scores = jnp.dot(head_q, all_keys.T, preferred_element_type=jnp.float32) * HD ** (-0.5)
-            scores = jnp.where(visible, scores, MASKED)
-            row_max = jnp.max(scores, axis=-1, keepdims=True)
-            weights = jnp.exp(scores - row_max)
-            row_sum = jnp.sum(weights, axis=-1, keepdims=True)
-            head_out = jnp.dot(
-                weights.astype(jnp.bfloat16), all_vals, preferred_element_type=jnp.float32
-            ) / row_sum
-            outputs.append(head_out)
+            parts = []
+            for keys, vals, mask in key_sets:
+                scores = jnp.dot(head_q, keys.T, preferred_element_type=jnp.float32) * HD ** (-0.5)
+                if mask is not None:
+                    scores = jnp.where(mask, scores, MASKED)
+                parts.append(scores)
+            row_max = parts[0].max(axis=-1, keepdims=True)
+            for scores in parts[1:]:
+                row_max = jnp.maximum(row_max, scores.max(axis=-1, keepdims=True))
+            row_sum = 0.0
+            head_out = 0.0
+            for scores, (keys, vals, mask) in zip(parts, key_sets):
+                weights = jnp.exp(scores - row_max)
+                row_sum = row_sum + jnp.sum(weights, axis=-1, keepdims=True)
+                head_out = head_out + jnp.dot(
+                    weights.astype(jnp.bfloat16), vals, preferred_element_type=jnp.float32
+                )
+            outputs.append(head_out / row_sum)
         attention = jnp.concatenate(outputs, axis=1).astype(jnp.bfloat16)
 
     share = row_count // tok_count

time: 155 us -> 176 us (1.14)
  between operations: 14.3 us -> 30.1 us
  matrix products: 17.3 us -> 21.7 us
  other arithmetic: 11.4 us -> 7.11 us
  local copies, waits for them, and re-layouts: 9.4 us -> 13.4 us
    unnamed x26 -> x31, local copies, waits for them, and re-layouts: 1.77 us -> 8.59 us
    dot_general x2 -> x6, matrix products: 4.24 us -> 8.62 us  [the longest x3 4.35 us: local(): jnp.dot(head_q, keys.T, preferred_element_type=jnp.float32) * HD ** (-0.5)]
    gather x1 -> x0, local copies, waits for them, and re-layouts: 4.2 us -> none  [local(): picked = jnp.take(gathered, owner_ids, axis=0).reshape(-1, 2 * HD)]
    select_n x1 -> x0, other arithmetic: 1.81 us -> none  [local(): picked = jnp.take(gathered, owner_ids, axis=0).reshape(-1, 2 * HD)]
  transfers between devices with their start and end apart: 2 -> 2, of which waited for: 1 -> 1; matrix products, arithmetic and copies ran while one was open for 3% -> 4% of each run, Pallas kernels for 38% -> 34%
where the time goes in v12:
time: 176 us; the launch traced here: 175 us
  Pallas kernels  102 us (58%)
  between operations  30.1 us (17%)
  matrix products  21.7 us (12%)
  local copies, waits for them, and re-layouts  13.4 us (8%)
  other arithmetic  7.11 us (4%)
    pallas_call x1, Pallas kernels, gather_over_tok(): pl.pallas_call(lambda *refs: gather_tok_kernel(tok_count, *refs), out_sha...  59.5 us
    pallas_call x1, Pallas kernels, project_over_tok(): pl.pallas_call(lambda *refs: project_tok_kernel(tok_count, *refs), out_sh...  21.7 us
    pallas_call x1, Pallas kernels, scatter_over_tok(): pl.pallas_call(lambda *refs: scatter_tok_kernel(tok_count, *refs), out_sh...  21 us
    unnamed x31, local copies, waits for them, and re-layouts  8.59 us
    dot_general x1, matrix products, local(): jnp.dot(hidden, w_down, preferred_element_type=jnp.float32)  5.7 us
    dot_general x3, matrix products, local(): jnp.dot(head_q, keys.T, preferred_element_type=jnp.float32) * HD ** (-0.5)  4.35 us
    dot_general x3, matrix products, local(): jnp.dot(weights.astype(jnp.bfloat16), vals, preferred_element_type=jnp.fl...  4.28 us
    dot_general x1, matrix products, local(): upward = jnp.dot(normed, w_up, preferred_element_type=jnp.float32)  3.83 us
  transfers between devices with their start and end apart: 2, of which 1 were waited for; matrix products, arithmetic and copies ran while one was open for 4% of the time, Pallas kernels for 34%

profile of v12, /device:TPU:1, one launch (start us, length us, event | category | flops | bytes accessed | tf_op | source)
XLA Modules:
  0.0 175.0 jit_solution(11685911128861984487)
XLA Ops:
  6.5 1.1 constant_dynamic-slice_fusion
  7.6 0.7 fusion.43
  8.4 1.3 dynamic_slice.52
  10.4 0.7 dynamic_slice.53
  11.1 0.7 fusion.56
  22.3 59.5 %prefix_gather.1.refs_1_ = bf16[8,256,2560]{2,1,0:T(8,128)(2,1)} custom-call(bf16[256,2560]{1,0:T(8,128)(2,1)} %refs_0_.1), custom_call_target="tpu_custom_call" | custom-call | bytes 20971520 | tf_op jit(solution)/shard_map/prefix_gather/pallas_call | solution.py:96
  87.2 1.0 bitcast_dynamic-update-slice_fusion.7
  88.2 1.0 bitcast_dynamic-update-slice_fusion.6
  89.1 1.0 bitcast_dynamic-update-slice_fusion.5
  90.1 1.0 bitcast_dynamic-update-slice_fusion.4
  91.1 1.0 bitcast_dynamic-update-slice_fusion.3
  92.1 1.0 bitcast_dynamic-update-slice_fusion.2
  93.0 1.0 bitcast_dynamic-update-slice_fusion.1
  94.0 1.0 bitcast_dynamic-update-slice_fusion
  95.4 1.1 fusion.38
  96.8 1.4 fusion.57
  98.2 0.9 multiply_reduce_fusion.3
  99.4 2.1 %multiply_reduce_fusion.2 = (f32[512]{0:T(512)S(1)}, f32[512,2048]{1,0:T(8,128)S(1)}) fusion(bf16[2048,512]{1,0:T(8,128)(2,1)} %collective-permute-done, bf16[512,256]{1,0:T(8,128)(2,1)S(1)} %copy-done.1, f32[256]{0:T(256)S(1)} %copy-done.5, f32[512]{0:T(512)S(1)} %add_rsqrt_fusion.3), kind=kOutput, calls=%fused_computation.6 | convolution fusion | flops 539491840 | bytes 5510144 | tf_op jit(solution)/shard_map/attention/dot_general | solution.py:399
  101.4 0.9 fusion.14
  102.3 1.5 fusion.2
  104.0 2.1 %fusion.22 = f32[512,256]{1,0:T(8,128)S(1)} fusion(f32[512,256]{1,0:T(8,128)S(1)} %fusion.14, f32[512,2048]{1,0:T(8,128)S(1)} %get-tuple-element.28, f32[512]{0:T(512)S(1)} %maximum_maximum_fusion, bf16[2048,512]{1,0:T(8,128)(2,1)} %collective-permute-done), kind=kOutput, calls=%fused_computation.32 | convolution fusion | flops 540147712 | bytes 6293504 | tf_op jit(solution)/shard_map/attention/dot_general | solution.py:411
  106.1 1.3 fusion.25.refs_0_
  107.5 21.7 %out_projection.1 = f32[512,2560]{1,0:T(8,128)S(1)} custom-call(bf16[512,256]{1,0:T(8,128)(2,1)S(1)} %fusion.25.refs_0_, bf16[8,256,2560]{2,1,0:T(8,128)(2,1)} %prefix_gather.1.refs_1_), custom_call_target="tpu_custom_call" | custom-call | flops 5368709120 | bytes 15728640 | tf_op jit(solution)/shard_map/out_projection/pallas_call | solution.py:209
  129.6 1.3 copy-done
  130.9 1.2 multiply_reduce_fusion
  132.1 0.5 multiply_convert_fusion
  132.6 0.4 slice-done.1
  133.0 3.5 %fusion.58 = f32[512,1280]{1,0:T(8,128)S(1)} fusion(bf16[512,2560]{1,0:T(8,128)(2,1)S(1)} %multiply_convert_fusion, bf16[2560,1280]{1,0:T(8,128)(2,1)S(1)} %bitcast.44), kind=kOutput, calls=%fused_computation.90 | convolution fusion | flops 3355443200 | bytes 11796480 | tf_op jit(solution)/shard_map/feed_forward/dot_general | solution.py:426
  136.6 3.8 %fusion.4 = bf16[512,1280]{1,0:T(8,128)(2,1)S(1)} fusion(bf16[512,2560]{1,0:T(8,128)(2,1)S(1)} %multiply_convert_fusion, bf16[2560,1280]{1,0:T(8,128)(2,1)S(1)} %bitcast.46, f32[512,1280]{1,0:T(8,128)S(1)} %fusion.58), kind=kOutput, calls=%fused_computation.14 | convolution fusion | flops 3361996800 | bytes 13107200 | tf_op jit(solution)/shard_map/feed_forward/dot_general | solution.py:427
  140.4 5.7 %fusion.59.refs_0_ = f32[512,2560]{1,0:T(8,128)S(1)} fusion(bf16[512,1280]{1,0:T(8,128)(2,1)S(1)} %fusion.4, bf16[1280,2560]{1,0:T(8,128)(2,1)} %param.31), kind=kOutput, calls=%fused_computation.91 | convolution fusion | flops 3355443200 | bytes 13107200 | tf_op jit(solution)/shard_map/feed_forward/dot_general | solution.py:431
  146.2 21.0 %feed_forward.1 = f32[64,2560]{1,0:T(8,128)S(1)} custom-call(f32[512,2560]{1,0:T(8,128)S(1)} %fusion.59.refs_0_), custom_call_target="tpu_custom_call" | custom-call | flops 1310720 | bytes 10485760 | tf_op jit(solution)/shard_map/feed_forward/pallas_call | solution.py:308
  167.3 0.9 add_convert_fusion
  (42 shorter events, 1.9 us)
Async XLA Ops:
  6.5 80.6 %all-gather.3.cloned.1.call-start = ((), (), s32[]{:S(2)}) async-start(), calls=%async_computation | async-start | bytes 4456448 | tf_op jit(solution)/shard_map/prefix_gather/all_gather | solution.py:367
  81.8 13.4 %copy-start.7 = (s32[1,3]{1,0:T(1,128)S(1)}, s32[1,3]{1,0:T(1,128)}, u32[]{:S(2)}) copy-start(s32[1,3]{1,0:T(1,128)} %param.21) | copy-start | bytes 40
  81.8 14.7 %copy-start.1 = (bf16[512,256]{1,0:T(8,128)(2,1)S(1)}, bf16[512,256]{1,0:T(8,128)(2,1)}, u32[]{:S(2)}) copy-start(bf16[512,256]{1,0:T(8,128)(2,1)} %param.16) | copy-start | bytes 786436
  81.8 14.9 %copy-start.5 = (f32[256]{0:T(256)S(1)}, f32[256]{0:T(256)}, u32[]{:S(2)}) copy-start(f32[256]{0:T(256)} %param.19) | copy-start | bytes 3076
  81.9 14.9 %copy-start.6 = (f32[256]{0:T(256)S(1)}, f32[256]{0:T(256)}, u32[]{:S(2)}) copy-start(f32[256]{0:T(256)} %param.20) | copy-start | bytes 3076
  95.0 4.4 %collective-permute-start = (bf16[2048,512]{1,0:T(8,128)(2,1)S(1)}, bf16[2048,512]{1,0:T(8,128)(2,1)}, u32[]{:S(2)}, u32[]{:S(2)}) collective-permute-start(bf16[2048,512]{1,0:T(8,128)(2,1)S(1)} %bitcast_dynamic-update-slice_fusion), channel_id=1, source_target_pairs={{0,1},{1,0},{2,3},{3,2},{4,5},{5,4},{6,7},{7,6},{8,9},{9,8},{10,11... | collective-permute-start | bytes 6291464 | tf_op jit(solution)/shard_map/prefix_gather/ppermute | solution.py:377
  129.1 1.7 copy-start
  129.1 1.7 copy-start.2
  129.1 3.4 %slice-start = ((s8[6553600]{0:T(1024)(128)(4,1)}), s8[4194304]{0:T(1024)(128)(4,1)S(1)}, s32[]{:S(2)}) async-start(s8[6553600]{0:T(1024)(128)(4,1)} %bitcast.43), calls=%async_computation.1 | async-start | bytes 8388608
  130.9 1.2 copy-start.3
  130.9 2.2 %slice-start.1 = ((s8[6553600]{0:T(1024)(128)(4,1)}), s8[2359296]{0:T(1024)(128)(4,1)S(1)}, s32[]{:S(2)}) async-start(s8[6553600]{0:T(1024)(128)(4,1)} %bitcast.43), calls=%async_computation.2 | async-start | bytes 4718592
  132.0 4.5 %slice-start.2 = ((s8[6553600]{0:T(1024)(128)(4,1)}), s8[4194304]{0:T(1024)(128)(4,1)S(1)}, s32[]{:S(2)}) async-start(s8[6553600]{0:T(1024)(128)(4,1)} %bitcast.45), calls=%async_computation.3 | async-start | bytes 8388608
  133.0 3.6 %slice-start.3 = ((s8[6553600]{0:T(1024)(128)(4,1)}), s8[2359296]{0:T(1024)(128)(4,1)S(1)}, s32[]{:S(2)}) async-start(s8[6553600]{0:T(1024)(128)(4,1)} %bitcast.45), calls=%async_computation.4 | async-start | bytes 4718592
  146.1 21.2 %copy-start.4 = (f32[2560]{0:T(1024)S(1)}, f32[2560]{0:T(1024)}, u32[]{:S(2)}) copy-start(f32[2560]{0:T(1024)} %param.28) | copy-start | bytes 30724
Sparse Core Ops, SparseCore 0:
  9.5 54.8 all-gather.2

commit v13 on v11

--- a/solution.py
+++ b/solution.py
@@ -145,7 +145,7 @@
         lax.rem(partner + tok_count - 2, tok_count),
         lax.rem(partner + 4, tok_count),
     )
-    order = (me, down, up, far) + theirs
+    order = (me, down, up, theirs[0], far) + theirs[1:]
 
     def load(idx):
         return pltpu.make_async_copy(w_hbm.at[order[idx]], w_buf.at[idx % 2], load_sem.at[idx % 2])
@@ -168,35 +168,41 @@
 
     load(0).start()
     sends = []
-    to_up = remote(att_ref, att_all.at[me], 0, up)
-    to_down = remote(att_ref, att_all.at[me], 1, down)
-    to_up.start()
-    to_down.start()
-    sends += [to_up, to_down]
-    accumulate(0, att_ref, True)
-    remote(att_ref, att_all.at[down], 0, down).wait_recv()
-    remote(att_ref, att_all.at[up], 1, up).wait_recv()
+
+    def send(src, slot, index, peer):
+        copy = remote(src, att_all.at[slot], index, peer)
+        copy.start()
+        sends.append(copy)
+
+    def arrived(slot, index, peer, rows=None):
+        dst = att_all.at[slot] if rows is None else att_all.at[slot, rows]
+        remote(dst, dst, index, peer).wait_recv()
+
     first = pl.ds(0, half)
     second = pl.ds(half, half)
-    fwd_up = remote(att_all.at[down, first], att_all.at[down, first], 2, up)
-    fwd_down = remote(att_all.at[up, second], att_all.at[up, second], 3, down)
-    fwd_up.start()
-    fwd_down.start()
-    sends += [fwd_up, fwd_down]
+    send(att_ref, me, 0, up)
+    send(att_ref, me, 1, down)
+    send(att_ref, me, 4, partner)
+    accumulate(0, att_ref, True)
+    arrived(down, 0, down)
+    arrived(up, 1, up)
+    for src, index, peer in ((att_all.at[down, first], 2, up), (att_all.at[up, second], 3, down)):
+        copy = remote(src, src, index, peer)
+        copy.start()
+        sends.append(copy)
+    send(att_all.at[up], up, 5, partner)
+    send(att_all.at[down], down, 6, partner)
     accumulate(1, att_all.at[down], False)
     accumulate(2, att_all.at[up], False)
-    remote(att_all.at[far, first], att_all.at[far, first], 2, down).wait_recv()
-    remote(att_all.at[far, second], att_all.at[far, second], 3, up).wait_recv()
-    for idx, (src, slot) in enumerate(
-        ((att_ref, me), (att_all.at[up], up), (att_all.at[down], down), (att_all.at[far], far))
-    ):
-        copy = remote(src, att_all.at[slot], 4 + idx, partner)
-        copy.start()
-        sends.append(copy)
-    accumulate(3, att_all.at[far], False)
-    for idx, slot in enumerate(theirs):
-        remote(att_all.at[slot], att_all.at[slot], 4 + idx, partner).wait_recv()
-        accumulate(4 + idx, att_all.at[slot], False)
+    arrived(theirs[0], 4, partner)
+    accumulate(3, att_all.at[theirs[0]], False)
+    arrived(far, 2, down, first)
+    arrived(far, 3, up, second)
+    send(att_all.at[far], far, 7, partner)
+    accumulate(4, att_all.at[far], False)
+    for idx in range(1, 4):
+        arrived(theirs[idx], 4 + idx, partner)
+        accumulate(4 + idx, att_all.at[theirs[idx]], False)
     for copy in sends:
         copy.wait_send()
 
@@ -369,7 +375,7 @@
         gathered, w_out_all = lax.optimization_barrier((gathered, w_out_all))
         own_group = group_of[req_index]
         owner_ids = lax.dynamic_slice_in_dim(owner_order, own_group * own_count, own_count)
-        picked = jnp.take(gathered, owner_ids, axis=0).reshape(-1, 2 * HD)
+        picked = jnp.take(gathered, owner_ids, axis=0, mode="clip").reshape(-1, 2 * HD)
         partner = [(t, t ^ 1) for t in range(tok_count)]
         swapped = lax.ppermute(picked, "tok", perm=partner)
         shared = jnp.concatenate([picked, swapped], axis=0)

time: 155 us -> 150 us (0.968)
  Pallas kernels: 102 us -> 100 us
  other arithmetic: 11.4 us -> 9.47 us
    pallas_call x1, Pallas kernels: 21.6 us -> 19.8 us  [project_over_tok(): pl.pallas_call(lambda *refs: project_tok_kernel(tok_count, *refs), out_sh...]
    select_n x1 -> x0, other arithmetic: 1.81 us -> none  [local(): picked = jnp.take(gathered, owner_ids, axis=0).reshape(-1, 2 * HD)]
  transfers between devices with their start and end apart: 2 -> 2, of which waited for: 1 -> 1; matrix products, arithmetic and copies ran while one was open for 3% -> 3% of each run, Pallas kernels for 38% -> 40%
where the time goes in v13:
time: 150 us
  Pallas kernels  100 us (67%)
  matrix products  17.3 us (12%)
  between operations  14.3 us (10%)
  other arithmetic  9.47 us (6%)
  local copies, waits for them, and re-layouts  8.07 us (5%)
    pallas_call x1, Pallas kernels, gather_over_tok(): pl.pallas_call(lambda *refs: gather_tok_kernel(tok_count, *refs), out_sha...  59.5 us
    pallas_call x1, Pallas kernels, scatter_over_tok(): pl.pallas_call(lambda *refs: scatter_tok_kernel(tok_count, *refs), out_sh...  20.9 us
    pallas_call x1, Pallas kernels, project_over_tok(): pl.pallas_call(lambda *refs: project_tok_kernel(tok_count, *refs), out_sh...  19.8 us
    dot_general x1, matrix products, local(): jnp.dot(hidden, w_down, preferred_element_type=jnp.float32)  5.7 us
    dot_general x1, matrix products, local(): upward = jnp.dot(normed, w_up, preferred_element_type=jnp.float32)  3.83 us
    dot_general x1, matrix products, local(): gate = jnp.dot(normed, w_gate, preferred_element_type=jnp.float32)  3.54 us
  transfers between devices with their start and end apart: 2, of which 1 were waited for; matrix products, arithmetic and copies ran while one was open for 3% of the time, Pallas kernels for 40%

profile of v13, /device:TPU:1, one launch (start us, length us, event | category | flops | bytes accessed | tf_op | source)
XLA Modules:
  0.0 149.9 jit_solution(16606248179527223376)
XLA Ops:
  6.5 1.1 constant_dynamic-slice_fusion.1
  7.6 0.7 fusion.38
  8.3 0.0 all-gather.3.cloned.1.call-update
  8.4 1.3 dynamic_slice.27
  10.3 59.5 %prefix_gather.1.refs_1_ = bf16[8,256,2560]{2,1,0:T(8,128)(2,1)} custom-call(bf16[256,2560]{1,0:T(8,128)(2,1)} %refs_0_.1), custom_call_target="tpu_custom_call" | custom-call | bytes 20971520 | tf_op jit(solution)/shard_map/prefix_gather/pallas_call | solution.py:96
  69.9 0.1 dynamic_slice.28
  70.0 2.9 %gather_fusion = bf16[8,256,512]{2,1,0:T(8,128)(2,1)S(1)} fusion(bf16[16,256,512]{2,1,0:T(8,128)(2,1)} %bitcast.14, s32[1024]{0:T(1024)S(1)} %pad_clamp_fusion), kind=kCustom, calls=%fused_computation | custom fusion | bytes 4194336 | tf_op jit(solution)/shard_map/prefix_gather/jit(_take)/gather | solution.py:378
  72.9 0.2 collective-permute-start
  73.1 0.2 reduce-window.8
  73.3 1.1 fusion.35
  74.4 0.1 convert_reduce_fusion
  74.4 1.0 constant_dynamic-slice_fusion
  75.4 0.1 fusion.32
  75.6 1.1 fusion.37
  76.7 0.2 fusion.21
  76.9 0.3 collective-permute-done
  77.2 1.4 fusion.20
  78.6 1.6 %fusion.44 = (f32[512]{0:T(512)S(1)}, f32[512,4608]{1,0:T(8,128)S(1)}) fusion(bf16[512,256]{1,0:T(8,128)(2,1)S(1)} %fusion.37, bf16[4096,256]{1,0:T(8,128)(2,1)S(1)} %fusion.20, bf16[512,256]{1,0:T(8,128)(2,1)S(1)} %copy-done.1, f32[256]{0:T(256)S(1)} %copy-done.6, f32[512]{0:T(512)S(1)} %add_rsqrt_fusion.3, pred[512,512]{1,0:T(32,128)(4,1)S(1)} %fusion.21), kind=kOutput, calls=%fused_computation.65 | convolution fusion | flops 1220279808 | bytes 12325888 | tf_op jit(solution)/shard_map/attention/dot_general | solution.py:401
  80.2 1.4 fusion
  81.6 2.7 %fusion.27.refs_0_ = bf16[512,256]{1,0:T(8,128)(2,1)S(1)} fusion(bf16[2048,512]{1,0:T(8,128)(2,1)} %collective-permute-done, bf16[2048,512]{1,0:T(8,128)(2,1)S(1)} %bitcast.13, bf16[512,256]{1,0:T(8,128)(2,1)S(1)} %constant_dynamic-slice_fusion, f32[512,4608]{1,0:T(8,128)S(1)} %get-tuple-element.14, f32[512]{0:T(512)S(1)} %get-tuple-element.13, f32[512]{0:T(512)S(1)} %fusion), kind=kOutput, calls=%fused_computation.34 | convolution fusion | flops 1220018176 | bytes 14159872 | tf_op jit(solution)/shard_map/attention/dot_general | solution.py:406
  84.3 19.8 %out_projection.1 = f32[512,2560]{1,0:T(8,128)S(1)} custom-call(bf16[512,256]{1,0:T(8,128)(2,1)S(1)} %fusion.27.refs_0_, bf16[8,256,2560]{2,1,0:T(8,128)(2,1)} %prefix_gather.1.refs_1_), custom_call_target="tpu_custom_call" | custom-call | flops 5368709120 | bytes 15728640 | tf_op jit(solution)/shard_map/out_projection/pallas_call | solution.py:215
  104.1 0.4 multiply_reduce_fusion.1
  104.5 1.3 copy-done
  105.8 1.2 multiply_reduce_fusion
  107.0 0.5 multiply_convert_fusion
  107.5 0.4 slice-done.1
  107.9 3.5 %fusion.45 = f32[512,1280]{1,0:T(8,128)S(1)} fusion(bf16[512,2560]{1,0:T(8,128)(2,1)S(1)} %multiply_convert_fusion, bf16[2560,1280]{1,0:T(8,128)(2,1)S(1)} %bitcast.17), kind=kOutput, calls=%fused_computation.66 | convolution fusion | flops 3355443200 | bytes 11796480 | tf_op jit(solution)/shard_map/feed_forward/dot_general | solution.py:421
  111.5 3.8 %fusion.5 = bf16[512,1280]{1,0:T(8,128)(2,1)S(1)} fusion(bf16[512,2560]{1,0:T(8,128)(2,1)S(1)} %multiply_convert_fusion, bf16[2560,1280]{1,0:T(8,128)(2,1)S(1)} %bitcast.19, f32[512,1280]{1,0:T(8,128)S(1)} %fusion.45), kind=kOutput, calls=%fused_computation.15 | convolution fusion | flops 3361996800 | bytes 13107200 | tf_op jit(solution)/shard_map/feed_forward/dot_general | solution.py:422
  115.3 5.7 %fusion.46.refs_0_ = f32[512,2560]{1,0:T(8,128)S(1)} fusion(bf16[512,1280]{1,0:T(8,128)(2,1)S(1)} %fusion.5, bf16[1280,2560]{1,0:T(8,128)(2,1)} %param.31), kind=kOutput, calls=%fused_computation.67 | convolution fusion | flops 3355443200 | bytes 13107200 | tf_op jit(solution)/shard_map/feed_forward/dot_general | solution.py:426
  121.1 20.9 %feed_forward.1 = f32[64,2560]{1,0:T(8,128)S(1)} custom-call(f32[512,2560]{1,0:T(8,128)S(1)} %fusion.46.refs_0_), custom_call_target="tpu_custom_call" | custom-call | flops 1310720 | bytes 10485760 | tf_op jit(solution)/shard_map/feed_forward/pallas_call | solution.py:314
  142.0 0.1 multiply_reduce_fusion.2
  142.2 0.9 add_convert_fusion
  (34 shorter events, 0.1 us)
Async XLA Ops:
  6.5 63.4 %all-gather.3.cloned.1.call-start = ((), (), s32[]{:S(2)}) async-start(), calls=%async_computation | async-start | bytes 4456448 | tf_op jit(solution)/shard_map/prefix_gather/all_gather | solution.py:373
  10.3 59.6 %copy-start.7 = (s32[16]{0:T(128)S(1)}, s32[16]{0:T(128)}, u32[]{:S(2)}) copy-start(s32[16]{0:T(128)} %param.23) | copy-start | bytes 196
  69.8 3.2 %copy-start.8 = (s32[1,3]{1,0:T(1,128)S(1)}, s32[1,3]{1,0:T(1,128)}, u32[]{:S(2)}) copy-start(s32[1,3]{1,0:T(1,128)} %param.21) | copy-start | bytes 40
  69.9 5.6 %copy-start.1 = (bf16[512,256]{1,0:T(8,128)(2,1)S(1)}, bf16[512,256]{1,0:T(8,128)(2,1)}, u32[]{:S(2)}) copy-start(bf16[512,256]{1,0:T(8,128)(2,1)} %param.16) | copy-start | bytes 786436
  70.0 5.6 %copy-start.5 = (f32[256]{0:T(256)S(1)}, f32[256]{0:T(256)}, u32[]{:S(2)}) copy-start(f32[256]{0:T(256)} %param.20) | copy-start | bytes 3076
  72.9 4.4 %collective-permute-start = (bf16[2048,512]{1,0:T(8,128)(2,1)S(1)}, bf16[2048,512]{1,0:T(8,128)(2,1)}, u32[]{:S(2)}, u32[]{:S(2)}) collective-permute-start(bf16[2048,512]{1,0:T(8,128)(2,1)S(1)} %bitcast.11), channel_id=1, source_target_pairs={{0,1},{1,0},{2,3},{3,2},{4,5},{5,4},{6,7},{7,6},{8,9},{9,8},{10,11... | collective-permute-start | bytes 6291464 | tf_op jit(solution)/shard_map/prefix_gather/ppermute | solution.py:380
  76.9 1.7 %copy-start.6 = (f32[256]{0:T(256)S(1)}, f32[256]{0:T(256)}, u32[]{:S(2)}) copy-start(f32[256]{0:T(256)} %param.19) | copy-start | bytes 3076
  104.0 1.7 %copy-start = (bf16[512,2560]{1,0:T(8,128)(2,1)S(1)}, bf16[512,2560]{1,0:T(8,128)(2,1)}, u32[]{:S(2)}) copy-start(bf16[512,2560]{1,0:T(8,128)(2,1)} %param.24) | copy-start | bytes 7864324
  104.0 1.7 %copy-start.2 = (f32[2560]{0:T(1024)S(1)}, f32[2560]{0:T(1024)}, u32[]{:S(2)}) copy-start(f32[2560]{0:T(1024)} %param.26) | copy-start | bytes 30724
  104.0 3.4 %slice-start = ((s8[6553600]{0:T(1024)(128)(4,1)}), s8[4194304]{0:T(1024)(128)(4,1)S(1)}, s32[]{:S(2)}) async-start(s8[6553600]{0:T(1024)(128)(4,1)} %bitcast.16), calls=%async_computation.1 | async-start | bytes 8388608
  105.8 1.2 copy-start.3
  105.8 2.2 %slice-start.1 = ((s8[6553600]{0:T(1024)(128)(4,1)}), s8[2359296]{0:T(1024)(128)(4,1)S(1)}, s32[]{:S(2)}) async-start(s8[6553600]{0:T(1024)(128)(4,1)} %bitcast.16), calls=%async_computation.2 | async-start | bytes 4718592
  107.0 4.5 %slice-start.2 = ((s8[6553600]{0:T(1024)(128)(4,1)}), s8[4194304]{0:T(1024)(128)(4,1)S(1)}, s32[]{:S(2)}) async-start(s8[6553600]{0:T(1024)(128)(4,1)} %bitcast.18), calls=%async_computation.3 | async-start | bytes 8388608
  107.9 3.6 %slice-start.3 = ((s8[6553600]{0:T(1024)(128)(4,1)}), s8[2359296]{0:T(1024)(128)(4,1)S(1)}, s32[]{:S(2)}) async-start(s8[6553600]{0:T(1024)(128)(4,1)} %bitcast.18), calls=%async_computation.4 | async-start | bytes 4718592
  121.1 21.1 %copy-start.4 = (f32[2560]{0:T(1024)S(1)}, f32[2560]{0:T(1024)}, u32[]{:S(2)}) copy-start(f32[2560]{0:T(1024)} %param.28) | copy-start | bytes 30724
Sparse Core Ops, SparseCore 0:
  9.5 54.8 all-gather.2

commit v14 on v13

--- a/solution.py
+++ b/solution.py
@@ -55,38 +55,39 @@
 
     local = pltpu.make_async_copy(w_ref, out_ref.at[me], local_sem.at[0])
     local.start()
-    to_up = remote(w_ref, out_ref.at[me], 0, up)
-    to_down = remote(w_ref, out_ref.at[me], 1, down)
-    to_up.start()
-    to_down.start()
+    sends = []
+
+    def send(src, dst, slot, peer):
+        copy = remote(src, dst, slot, peer)
+        copy.start()
+        sends.append(copy)
+
+    send(w_ref, out_ref.at[me], 0, up)
+    send(w_ref, out_ref.at[me], 1, down)
+    send(w_ref, out_ref.at[me], 4, partner)
     remote(w_ref, out_ref.at[down], 0, down).wait_recv()
     remote(w_ref, out_ref.at[up], 1, up).wait_recv()
 
     first = pl.ds(0, half)
     second = pl.ds(half, half)
-    fwd_up = remote(out_ref.at[down, first], out_ref.at[down, first], 2, up)
-    fwd_down = remote(out_ref.at[up, second], out_ref.at[up, second], 3, down)
-    fwd_up.start()
-    fwd_down.start()
+    send(out_ref.at[down, first], out_ref.at[down, first], 2, up)
+    send(out_ref.at[up, second], out_ref.at[up, second], 3, down)
+    send(out_ref.at[up], out_ref.at[up], 5, partner)
+    send(out_ref.at[down], out_ref.at[down], 6, partner)
     remote(out_ref.at[far, first], out_ref.at[far, first], 2, down).wait_recv()
     remote(out_ref.at[far, second], out_ref.at[far, second], 3, up).wait_recv()
+    send(out_ref.at[far], out_ref.at[far], 7, partner)
     local.wait()
 
-    mine = (me, up, down, far)
     theirs = (
         partner,
         lax.rem(partner + 2, tok_count),
         lax.rem(partner + tok_count - 2, tok_count),
         lax.rem(partner + 4, tok_count),
     )
-    to_partner = []
-    for idx, slot in enumerate(mine):
-        copy = remote(out_ref.at[slot], out_ref.at[slot], 4 + idx, partner)
-        copy.start()
-        to_partner.append(copy)
     for idx, slot in enumerate(theirs):
         remote(out_ref.at[slot], out_ref.at[slot], 4 + idx, partner).wait_recv()
-    for copy in [to_up, to_down, fwd_up, fwd_down] + to_partner:
+    for copy in sends:
         copy.wait_send()
 
 

time: 150 us -> 146 us (0.973)
  Pallas kernels: 100 us -> 95.7 us
    pallas_call x1, Pallas kernels: 59.5 us -> 53.9 us  [gather_over_tok(): pl.pallas_call(lambda *refs: gather_tok_kernel(tok_count, *refs), out_sha...]
  transfers between devices with their start and end apart: 2 -> 2, of which waited for: 1 -> 2; matrix products, arithmetic and copies ran while one was open for 3% -> 4% of each run, Pallas kernels for 40% -> 37%
where the time goes in v14:
time: 146 us
  Pallas kernels  95.7 us (66%)
  matrix products  17.3 us (12%)
  between operations  14.3 us (10%)
  other arithmetic  9.47 us (6%)
  local copies, waits for them, and re-layouts  8.07 us (6%)
    pallas_call x1, Pallas kernels, gather_over_tok(): pl.pallas_call(lambda *refs: gather_tok_kernel(tok_count, *refs), out_sha...  53.9 us
    pallas_call x1, Pallas kernels, scatter_over_tok(): pl.pallas_call(lambda *refs: scatter_tok_kernel(tok_count, *refs), out_sh...  22 us
    pallas_call x1, Pallas kernels, project_over_tok(): pl.pallas_call(lambda *refs: project_tok_kernel(tok_count, *refs), out_sh...  19.9 us
    dot_general x1, matrix products, local(): jnp.dot(hidden, w_down, preferred_element_type=jnp.float32)  5.7 us
    dot_general x1, matrix products, local(): upward = jnp.dot(normed, w_up, preferred_element_type=jnp.float32)  3.83 us
    dot_general x1, matrix products, local(): gate = jnp.dot(normed, w_gate, preferred_element_type=jnp.float32)  3.54 us
    reduce_sum x5, other arithmetic, rms_scale(): jnp.mean(values_in * values_in, axis=-1, keepdims=True) + EPSILON  2.98 us
  transfers between devices with their start and end apart: 2, of which 2 were waited for; matrix products, arithmetic and copies ran while one was open for 4% of the time, Pallas kernels for 37%

profile of v14, /device:TPU:1, one launch (start us, length us, event | category | flops | bytes accessed | tf_op | source)
XLA Modules:
  0.0 145.8 jit_solution(7937403262349837618)
XLA Ops:
  6.5 1.1 constant_dynamic-slice_fusion.1
  7.6 0.7 fusion.38
  8.4 1.3 dynamic_slice.27
  10.3 53.9 %prefix_gather.1.refs_1_ = bf16[8,256,2560]{2,1,0:T(8,128)(2,1)} custom-call(bf16[256,2560]{1,0:T(8,128)(2,1)} %refs_0_.1), custom_call_target="tpu_custom_call" | custom-call | bytes 20971520 | tf_op jit(solution)/shard_map/prefix_gather/pallas_call | solution.py:97
  64.3 0.1 dynamic_slice.28
  64.3 0.1 all-gather.3.cloned.1.call-done
  64.4 2.9 %gather_fusion = bf16[8,256,512]{2,1,0:T(8,128)(2,1)S(1)} fusion(bf16[16,256,512]{2,1,0:T(8,128)(2,1)} %bitcast.14, s32[1024]{0:T(1024)S(1)} %pad_clamp_fusion), kind=kCustom, calls=%fused_computation | custom fusion | bytes 4194336 | tf_op jit(solution)/shard_map/prefix_gather/jit(_take)/gather | solution.py:379
  67.3 0.8 collective-permute-start
  68.1 0.2 reduce-window.8
  68.2 1.1 fusion.35
  69.3 0.1 convert_reduce_fusion
  69.4 1.0 constant_dynamic-slice_fusion
  70.4 0.1 fusion.32
  70.6 1.1 fusion.37
  71.7 0.2 fusion.21
  71.9 0.1 collective-permute-done
  72.0 1.4 fusion.20
  73.3 1.6 %fusion.44 = (f32[512]{0:T(512)S(1)}, f32[512,4608]{1,0:T(8,128)S(1)}) fusion(bf16[512,256]{1,0:T(8,128)(2,1)S(1)} %fusion.37, bf16[4096,256]{1,0:T(8,128)(2,1)S(1)} %fusion.20, bf16[512,256]{1,0:T(8,128)(2,1)S(1)} %copy-done.1, f32[256]{0:T(256)S(1)} %copy-done.6, f32[512]{0:T(512)S(1)} %add_rsqrt_fusion.3, pred[512,512]{1,0:T(32,128)(4,1)S(1)} %fusion.21), kind=kOutput, calls=%fused_computation.65 | convolution fusion | flops 1220279808 | bytes 12325888 | tf_op jit(solution)/shard_map/attention/dot_general | solution.py:402
  74.9 1.4 fusion
  76.3 2.7 %fusion.27.refs_0_ = bf16[512,256]{1,0:T(8,128)(2,1)S(1)} fusion(bf16[2048,512]{1,0:T(8,128)(2,1)} %collective-permute-done, bf16[2048,512]{1,0:T(8,128)(2,1)S(1)} %bitcast.13, bf16[512,256]{1,0:T(8,128)(2,1)S(1)} %constant_dynamic-slice_fusion, f32[512,4608]{1,0:T(8,128)S(1)} %get-tuple-element.14, f32[512]{0:T(512)S(1)} %get-tuple-element.13, f32[512]{0:T(512)S(1)} %fusion), kind=kOutput, calls=%fused_computation.34 | convolution fusion | flops 1220018176 | bytes 14159872 | tf_op jit(solution)/shard_map/attention/dot_general | solution.py:407
  79.0 19.9 %out_projection.1 = f32[512,2560]{1,0:T(8,128)S(1)} custom-call(bf16[512,256]{1,0:T(8,128)(2,1)S(1)} %fusion.27.refs_0_, bf16[8,256,2560]{2,1,0:T(8,128)(2,1)} %prefix_gather.1.refs_1_), custom_call_target="tpu_custom_call" | custom-call | flops 5368709120 | bytes 15728640 | tf_op jit(solution)/shard_map/out_projection/pallas_call | solution.py:216
  98.9 0.4 multiply_reduce_fusion.1
  99.3 1.3 copy-done
  100.6 1.2 multiply_reduce_fusion
  101.8 0.5 multiply_convert_fusion
  102.3 0.4 slice-done.1
  102.8 3.5 %fusion.45 = f32[512,1280]{1,0:T(8,128)S(1)} fusion(bf16[512,2560]{1,0:T(8,128)(2,1)S(1)} %multiply_convert_fusion, bf16[2560,1280]{1,0:T(8,128)(2,1)S(1)} %bitcast.17), kind=kOutput, calls=%fused_computation.66 | convolution fusion | flops 3355443200 | bytes 11796480 | tf_op jit(solution)/shard_map/feed_forward/dot_general | solution.py:422
  106.3 3.8 %fusion.5 = bf16[512,1280]{1,0:T(8,128)(2,1)S(1)} fusion(bf16[512,2560]{1,0:T(8,128)(2,1)S(1)} %multiply_convert_fusion, bf16[2560,1280]{1,0:T(8,128)(2,1)S(1)} %bitcast.19, f32[512,1280]{1,0:T(8,128)S(1)} %fusion.45), kind=kOutput, calls=%fused_computation.15 | convolution fusion | flops 3361996800 | bytes 13107200 | tf_op jit(solution)/shard_map/feed_forward/dot_general | solution.py:423
  110.2 5.7 %fusion.46.refs_0_ = f32[512,2560]{1,0:T(8,128)S(1)} fusion(bf16[512,1280]{1,0:T(8,128)(2,1)S(1)} %fusion.5, bf16[1280,2560]{1,0:T(8,128)(2,1)} %param.31), kind=kOutput, calls=%fused_computation.67 | convolution fusion | flops 3355443200 | bytes 13107200 | tf_op jit(solution)/shard_map/feed_forward/dot_general | solution.py:427
  115.9 22.0 %feed_forward.1 = f32[64,2560]{1,0:T(8,128)S(1)} custom-call(f32[512,2560]{1,0:T(8,128)S(1)} %fusion.46.refs_0_), custom_call_target="tpu_custom_call" | custom-call | flops 1310720 | bytes 10485760 | tf_op jit(solution)/shard_map/feed_forward/pallas_call | solution.py:315
  137.9 0.1 multiply_reduce_fusion.2
  138.0 0.9 add_convert_fusion
  (34 shorter events, 0.1 us)
Async XLA Ops:
  6.5 57.9 %all-gather.3.cloned.1.call-start = ((), (), s32[]{:S(2)}) async-start(), calls=%async_computation | async-start | bytes 4456448 | tf_op jit(solution)/shard_map/prefix_gather/all_gather | solution.py:374
  10.3 53.9 %copy-start.7 = (s32[16]{0:T(128)S(1)}, s32[16]{0:T(128)}, u32[]{:S(2)}) copy-start(s32[16]{0:T(128)} %param.23) | copy-start | bytes 196
  64.2 3.8 %copy-start.8 = (s32[1,3]{1,0:T(1,128)S(1)}, s32[1,3]{1,0:T(1,128)}, u32[]{:S(2)}) copy-start(s32[1,3]{1,0:T(1,128)} %param.21) | copy-start | bytes 40
  64.2 6.2 %copy-start.1 = (bf16[512,256]{1,0:T(8,128)(2,1)S(1)}, bf16[512,256]{1,0:T(8,128)(2,1)}, u32[]{:S(2)}) copy-start(bf16[512,256]{1,0:T(8,128)(2,1)} %param.16) | copy-start | bytes 786436
  64.4 6.2 %copy-start.5 = (f32[256]{0:T(256)S(1)}, f32[256]{0:T(256)}, u32[]{:S(2)}) copy-start(f32[256]{0:T(256)} %param.20) | copy-start | bytes 3076
  67.3 4.7 %collective-permute-start = (bf16[2048,512]{1,0:T(8,128)(2,1)S(1)}, bf16[2048,512]{1,0:T(8,128)(2,1)}, u32[]{:S(2)}, u32[]{:S(2)}) collective-permute-start(bf16[2048,512]{1,0:T(8,128)(2,1)S(1)} %bitcast.11), channel_id=1, source_target_pairs={{0,1},{1,0},{2,3},{3,2},{4,5},{5,4},{6,7},{7,6},{8,9},{9,8},{10,11... | collective-permute-start | bytes 6291464 | tf_op jit(solution)/shard_map/prefix_gather/ppermute | solution.py:381
  71.9 1.4 copy-start.6
  98.9 1.7 %copy-start = (bf16[512,2560]{1,0:T(8,128)(2,1)S(1)}, bf16[512,2560]{1,0:T(8,128)(2,1)}, u32[]{:S(2)}) copy-start(bf16[512,2560]{1,0:T(8,128)(2,1)} %param.24) | copy-start | bytes 7864324
  98.9 1.7 %copy-start.2 = (f32[2560]{0:T(1024)S(1)}, f32[2560]{0:T(1024)}, u32[]{:S(2)}) copy-start(f32[2560]{0:T(1024)} %param.26) | copy-start | bytes 30724
  98.9 3.4 %slice-start = ((s8[6553600]{0:T(1024)(128)(4,1)}), s8[4194304]{0:T(1024)(128)(4,1)S(1)}, s32[]{:S(2)}) async-start(s8[6553600]{0:T(1024)(128)(4,1)} %bitcast.16), calls=%async_computation.1 | async-start | bytes 8388608
  100.6 1.2 copy-start.3
  100.6 2.2 %slice-start.1 = ((s8[6553600]{0:T(1024)(128)(4,1)}), s8[2359296]{0:T(1024)(128)(4,1)S(1)}, s32[]{:S(2)}) async-start(s8[6553600]{0:T(1024)(128)(4,1)} %bitcast.16), calls=%async_computation.2 | async-start | bytes 4718592
  101.8 4.5 %slice-start.2 = ((s8[6553600]{0:T(1024)(128)(4,1)}), s8[4194304]{0:T(1024)(128)(4,1)S(1)}, s32[]{:S(2)}) async-start(s8[6553600]{0:T(1024)(128)(4,1)} %bitcast.18), calls=%async_computation.3 | async-start | bytes 8388608
  102.8 3.6 %slice-start.3 = ((s8[6553600]{0:T(1024)(128)(4,1)}), s8[2359296]{0:T(1024)(128)(4,1)S(1)}, s32[]{:S(2)}) async-start(s8[6553600]{0:T(1024)(128)(4,1)} %bitcast.18), calls=%async_computation.4 | async-start | bytes 4718592
  115.9 22.1 %copy-start.4 = (f32[2560]{0:T(1024)S(1)}, f32[2560]{0:T(1024)}, u32[]{:S(2)}) copy-start(f32[2560]{0:T(1024)} %param.28) | copy-start | bytes 30724
Sparse Core Ops, SparseCore 0:
  9.5 54.8 all-gather.2

commit v15 on v14

--- a/solution.py
+++ b/solution.py
@@ -237,7 +237,7 @@
 
 
 def scatter_tok_kernel(
-    tok_count, part_hbm, out_ref, mine, chip_in, cross_out, cross_in, load_sem, send_sem, recv_sem
+    tok_count, part_hbm, out_ref, mine, theirs_buf, chip_in, cross_out, cross_in, load_sem, send_sem, recv_sem
 ):
     mesh_ids = pl.DeviceIdType.MESH
     me = lax.axis_index("tok")
@@ -276,11 +276,20 @@
     order = (3, 1, 2, 0)
     sends = []
     theirs = family(partner)
+    staged = []
     for idx in order:
-        copy = remote(part_hbm.at[rows_of(theirs[idx])], chip_in.at[idx], idx, partner)
+        load = pltpu.make_async_copy(
+            part_hbm.at[rows_of(theirs[idx])], theirs_buf.at[idx], load_sem.at[4 + idx]
+        )
+        load.start()
+        staged.append(load)
+    own = family(me)
+    for pos, idx in enumerate(order):
+        staged[pos].wait()
+        cross_out[3 + idx] = theirs_buf[idx].astype(cross_out.dtype)
+        copy = remote(cross_out.at[3 + idx], chip_in.at[idx], idx, partner)
         copy.start()
         sends.append(copy)
-    own = family(me)
     loads = []
     for idx in order:
         load = pltpu.make_async_copy(part_hbm.at[rows_of(own[idx])], mine.at[idx], load_sem.at[idx])
@@ -289,15 +298,15 @@
     targets = {1: (up, 1), 2: (down, 0), 3: (far, 2)}
     for pos, idx in enumerate(order[:3]):
         loads[pos].wait()
-        remote(part_hbm.at[rows_of(own[idx])], chip_in.at[idx], idx, partner).wait_recv()
-        cross_out[idx - 1] = (mine[idx] + chip_in[idx]).astype(cross_out.dtype)
+        remote(cross_out.at[3 + idx], chip_in.at[idx], idx, partner).wait_recv()
+        cross_out[idx - 1] = (mine[idx] + chip_in[idx].astype(jnp.float32)).astype(cross_out.dtype)
         peer, dst_idx = targets[idx]
         copy = remote(cross_out.at[idx - 1], cross_in.at[dst_idx], 4 + dst_idx, peer)
         copy.start()
         sends.append(copy)
     loads[3].wait()
-    remote(part_hbm.at[rows_of(own[0])], chip_in.at[0], 0, partner).wait_recv()
-    total = mine[0] + chip_in[0]
+    remote(cross_out.at[3], chip_in.at[0], 0, partner).wait_recv()
+    total = mine[0] + chip_in[0].astype(jnp.float32)
     for idx, peer in ((0, up), (1, down), (2, far)):
         remote(cross_out.at[idx], cross_in.at[idx], 4 + idx, peer).wait_recv()
     for idx in range(3):
@@ -320,9 +329,10 @@
         scratch_shapes=[
             pltpu.VMEM((4, share, cols), jnp.float32),
             pltpu.VMEM((4, share, cols), jnp.float32),
+            pltpu.VMEM((4, share, cols), jnp.bfloat16),
+            pltpu.VMEM((7, share, cols), jnp.bfloat16),
             pltpu.VMEM((3, share, cols), jnp.bfloat16),
-            pltpu.VMEM((3, share, cols), jnp.bfloat16),
-            pltpu.SemaphoreType.DMA((4,)),
+            pltpu.SemaphoreType.DMA((8,)),
             pltpu.SemaphoreType.DMA((7,)),
             pltpu.SemaphoreType.DMA((7,)),
         ],

time: 146 us -> 147 us (level)
  no operation moved by 1% of the time
where the time goes in v15:
time: 147 us; the launch traced here: 146 us
  Pallas kernels  96.3 us (66%)
  matrix products  17.3 us (12%)
  between operations  14.3 us (10%)
  other arithmetic  9.47 us (6%)
  local copies, waits for them, and re-layouts  8.07 us (5%)
    pallas_call x1, Pallas kernels, gather_over_tok(): pl.pallas_call(lambda *refs: gather_tok_kernel(tok_count, *refs), out_sha...  53.9 us
    pallas_call x1, Pallas kernels, scatter_over_tok(): pl.pallas_call(lambda *refs: scatter_tok_kernel(tok_count, *refs), out_sh...  22.5 us
    pallas_call x1, Pallas kernels, project_over_tok(): pl.pallas_call(lambda *refs: project_tok_kernel(tok_count, *refs), out_sh...  19.9 us
    dot_general x1, matrix products, local(): jnp.dot(hidden, w_down, preferred_element_type=jnp.float32)  5.7 us
    dot_general x1, matrix products, local(): upward = jnp.dot(normed, w_up, preferred_element_type=jnp.float32)  3.83 us
    dot_general x1, matrix products, local(): gate = jnp.dot(normed, w_gate, preferred_element_type=jnp.float32)  3.54 us
    reduce_sum x5, other arithmetic, rms_scale(): jnp.mean(values_in * values_in, axis=-1, keepdims=True) + EPSILON  2.98 us
  transfers between devices with their start and end apart: 2, of which 2 were waited for; matrix products, arithmetic and copies ran while one was open for 4% of the time, Pallas kernels for 37%

profile of v15, /device:TPU:1, one launch (start us, length us, event | category | flops | bytes accessed | tf_op | source)
XLA Modules:
  0.0 146.3 jit_solution(10630174424657472293)
XLA Ops:
  6.5 1.1 constant_dynamic-slice_fusion.1
  7.6 0.7 fusion.38
  8.4 1.3 dynamic_slice.27
  10.3 53.9 %prefix_gather.1.refs_1_ = bf16[8,256,2560]{2,1,0:T(8,128)(2,1)} custom-call(bf16[256,2560]{1,0:T(8,128)(2,1)} %refs_0_.1), custom_call_target="tpu_custom_call" | custom-call | bytes 20971520 | tf_op jit(solution)/shard_map/prefix_gather/pallas_call | solution.py:97
  64.3 0.1 dynamic_slice.28
  64.3 0.1 all-gather.3.cloned.1.call-done
  64.4 2.9 %gather_fusion = bf16[8,256,512]{2,1,0:T(8,128)(2,1)S(1)} fusion(bf16[16,256,512]{2,1,0:T(8,128)(2,1)} %bitcast.14, s32[1024]{0:T(1024)S(1)} %pad_clamp_fusion), kind=kCustom, calls=%fused_computation | custom fusion | bytes 4194336 | tf_op jit(solution)/shard_map/prefix_gather/jit(_take)/gather | solution.py:389
  67.3 0.8 collective-permute-start
  68.1 0.2 reduce-window.8
  68.2 1.1 fusion.35
  69.3 0.1 convert_reduce_fusion
  69.4 1.0 constant_dynamic-slice_fusion
  70.4 0.1 fusion.32
  70.6 1.1 fusion.37
  71.7 0.2 fusion.21
  71.9 0.1 collective-permute-done
  72.0 1.4 fusion.20
  73.3 1.6 %fusion.44 = (f32[512]{0:T(512)S(1)}, f32[512,4608]{1,0:T(8,128)S(1)}) fusion(bf16[512,256]{1,0:T(8,128)(2,1)S(1)} %fusion.37, bf16[4096,256]{1,0:T(8,128)(2,1)S(1)} %fusion.20, bf16[512,256]{1,0:T(8,128)(2,1)S(1)} %copy-done.1, f32[256]{0:T(256)S(1)} %copy-done.6, f32[512]{0:T(512)S(1)} %add_rsqrt_fusion.3, pred[512,512]{1,0:T(32,128)(4,1)S(1)} %fusion.21), kind=kOutput, calls=%fused_computation.65 | convolution fusion | flops 1220279808 | bytes 12325888 | tf_op jit(solution)/shard_map/attention/dot_general | solution.py:412
  74.9 1.4 fusion
  76.3 2.7 %fusion.27.refs_0_ = bf16[512,256]{1,0:T(8,128)(2,1)S(1)} fusion(bf16[2048,512]{1,0:T(8,128)(2,1)} %collective-permute-done, bf16[2048,512]{1,0:T(8,128)(2,1)S(1)} %bitcast.13, bf16[512,256]{1,0:T(8,128)(2,1)S(1)} %constant_dynamic-slice_fusion, f32[512,4608]{1,0:T(8,128)S(1)} %get-tuple-element.14, f32[512]{0:T(512)S(1)} %get-tuple-element.13, f32[512]{0:T(512)S(1)} %fusion), kind=kOutput, calls=%fused_computation.34 | convolution fusion | flops 1220018176 | bytes 14159872 | tf_op jit(solution)/shard_map/attention/dot_general | solution.py:417
  79.0 19.9 %out_projection.1 = f32[512,2560]{1,0:T(8,128)S(1)} custom-call(bf16[512,256]{1,0:T(8,128)(2,1)S(1)} %fusion.27.refs_0_, bf16[8,256,2560]{2,1,0:T(8,128)(2,1)} %prefix_gather.1.refs_1_), custom_call_target="tpu_custom_call" | custom-call | flops 5368709120 | bytes 15728640 | tf_op jit(solution)/shard_map/out_projection/pallas_call | solution.py:216
  98.9 0.4 multiply_reduce_fusion.1
  99.3 1.3 copy-done
  100.6 1.2 multiply_reduce_fusion
  101.8 0.5 multiply_convert_fusion
  102.3 0.4 slice-done.1
  102.8 3.5 %fusion.45 = f32[512,1280]{1,0:T(8,128)S(1)} fusion(bf16[512,2560]{1,0:T(8,128)(2,1)S(1)} %multiply_convert_fusion, bf16[2560,1280]{1,0:T(8,128)(2,1)S(1)} %bitcast.17), kind=kOutput, calls=%fused_computation.66 | convolution fusion | flops 3355443200 | bytes 11796480 | tf_op jit(solution)/shard_map/feed_forward/dot_general | solution.py:432
  106.3 3.8 %fusion.5 = bf16[512,1280]{1,0:T(8,128)(2,1)S(1)} fusion(bf16[512,2560]{1,0:T(8,128)(2,1)S(1)} %multiply_convert_fusion, bf16[2560,1280]{1,0:T(8,128)(2,1)S(1)} %bitcast.19, f32[512,1280]{1,0:T(8,128)S(1)} %fusion.45), kind=kOutput, calls=%fused_computation.15 | convolution fusion | flops 3361996800 | bytes 13107200 | tf_op jit(solution)/shard_map/feed_forward/dot_general | solution.py:433
  110.2 5.7 %fusion.46.refs_0_ = f32[512,2560]{1,0:T(8,128)S(1)} fusion(bf16[512,1280]{1,0:T(8,128)(2,1)S(1)} %fusion.5, bf16[1280,2560]{1,0:T(8,128)(2,1)} %param.31), kind=kOutput, calls=%fused_computation.67 | convolution fusion | flops 3355443200 | bytes 13107200 | tf_op jit(solution)/shard_map/feed_forward/dot_general | solution.py:437
  115.9 22.5 %feed_forward.1 = f32[64,2560]{1,0:T(8,128)S(1)} custom-call(f32[512,2560]{1,0:T(8,128)S(1)} %fusion.46.refs_0_), custom_call_target="tpu_custom_call" | custom-call | flops 1310720 | bytes 10485760 | tf_op jit(solution)/shard_map/feed_forward/pallas_call | solution.py:324
  138.4 0.1 multiply_reduce_fusion.2
  138.6 0.9 add_convert_fusion
  (34 shorter events, 0.1 us)
Async XLA Ops:
  6.5 57.9 %all-gather.3.cloned.1.call-start = ((), (), s32[]{:S(2)}) async-start(), calls=%async_computation | async-start | bytes 4456448 | tf_op jit(solution)/shard_map/prefix_gather/all_gather | solution.py:384
  10.3 53.9 %copy-start.7 = (s32[16]{0:T(128)S(1)}, s32[16]{0:T(128)}, u32[]{:S(2)}) copy-start(s32[16]{0:T(128)} %param.23) | copy-start | bytes 196
  64.2 3.8 %copy-start.8 = (s32[1,3]{1,0:T(1,128)S(1)}, s32[1,3]{1,0:T(1,128)}, u32[]{:S(2)}) copy-start(s32[1,3]{1,0:T(1,128)} %param.21) | copy-start | bytes 40
  64.2 6.2 %copy-start.1 = (bf16[512,256]{1,0:T(8,128)(2,1)S(1)}, bf16[512,256]{1,0:T(8,128)(2,1)}, u32[]{:S(2)}) copy-start(bf16[512,256]{1,0:T(8,128)(2,1)} %param.16) | copy-start | bytes 786436
  64.4 6.2 %copy-start.5 = (f32[256]{0:T(256)S(1)}, f32[256]{0:T(256)}, u32[]{:S(2)}) copy-start(f32[256]{0:T(256)} %param.20) | copy-start | bytes 3076
  67.3 4.7 %collective-permute-start = (bf16[2048,512]{1,0:T(8,128)(2,1)S(1)}, bf16[2048,512]{1,0:T(8,128)(2,1)}, u32[]{:S(2)}, u32[]{:S(2)}) collective-permute-start(bf16[2048,512]{1,0:T(8,128)(2,1)S(1)} %bitcast.11), channel_id=1, source_target_pairs={{0,1},{1,0},{2,3},{3,2},{4,5},{5,4},{6,7},{7,6},{8,9},{9,8},{10,11... | collective-permute-start | bytes 6291464 | tf_op jit(solution)/shard_map/prefix_gather/ppermute | solution.py:391
  71.9 1.4 copy-start.6
  98.9 1.7 %copy-start = (bf16[512,2560]{1,0:T(8,128)(2,1)S(1)}, bf16[512,2560]{1,0:T(8,128)(2,1)}, u32[]{:S(2)}) copy-start(bf16[512,2560]{1,0:T(8,128)(2,1)} %param.24) | copy-start | bytes 7864324
  98.9 1.7 %copy-start.2 = (f32[2560]{0:T(1024)S(1)}, f32[2560]{0:T(1024)}, u32[]{:S(2)}) copy-start(f32[2560]{0:T(1024)} %param.26) | copy-start | bytes 30724
  98.9 3.4 %slice-start = ((s8[6553600]{0:T(1024)(128)(4,1)}), s8[4194304]{0:T(1024)(128)(4,1)S(1)}, s32[]{:S(2)}) async-start(s8[6553600]{0:T(1024)(128)(4,1)} %bitcast.16), calls=%async_computation.1 | async-start | bytes 8388608
  100.6 1.2 copy-start.3
  100.6 2.2 %slice-start.1 = ((s8[6553600]{0:T(1024)(128)(4,1)}), s8[2359296]{0:T(1024)(128)(4,1)S(1)}, s32[]{:S(2)}) async-start(s8[6553600]{0:T(1024)(128)(4,1)} %bitcast.16), calls=%async_computation.2 | async-start | bytes 4718592
  101.8 4.5 %slice-start.2 = ((s8[6553600]{0:T(1024)(128)(4,1)}), s8[4194304]{0:T(1024)(128)(4,1)S(1)}, s32[]{:S(2)}) async-start(s8[6553600]{0:T(1024)(128)(4,1)} %bitcast.18), calls=%async_computation.3 | async-start | bytes 8388608
  102.8 3.6 %slice-start.3 = ((s8[6553600]{0:T(1024)(128)(4,1)}), s8[2359296]{0:T(1024)(128)(4,1)S(1)}, s32[]{:S(2)}) async-start(s8[6553600]{0:T(1024)(128)(4,1)} %bitcast.18), calls=%async_computation.4 | async-start | bytes 4718592
  115.9 22.7 %copy-start.4 = (f32[2560]{0:T(1024)S(1)}, f32[2560]{0:T(1024)}, u32[]{:S(2)}) copy-start(f32[2560]{0:T(1024)} %param.28) | copy-start | bytes 30724
Sparse Core Ops, SparseCore 0:
  9.5 54.8 all-gather.2

commit v16 on v14

--- a/solution.py
+++ b/solution.py
@@ -146,7 +146,7 @@
         lax.rem(partner + tok_count - 2, tok_count),
         lax.rem(partner + 4, tok_count),
     )
-    order = (me, down, up, theirs[0], far) + theirs[1:]
+    order = (me, theirs[0], down, up, theirs[1], theirs[2], far, theirs[3])
 
     def load(idx):
         return pltpu.make_async_copy(w_hbm.at[order[idx]], w_buf.at[idx % 2], load_sem.at[idx % 2])
@@ -185,6 +185,8 @@
     send(att_ref, me, 1, down)
     send(att_ref, me, 4, partner)
     accumulate(0, att_ref, True)
+    arrived(theirs[0], 4, partner)
+    accumulate(1, att_all.at[theirs[0]], False)
     arrived(down, 0, down)
     arrived(up, 1, up)
     for src, index, peer in ((att_all.at[down, first], 2, up), (att_all.at[up, second], 3, down)):
@@ -193,17 +195,17 @@
         sends.append(copy)
     send(att_all.at[up], up, 5, partner)
     send(att_all.at[down], down, 6, partner)
-    accumulate(1, att_all.at[down], False)
-    accumulate(2, att_all.at[up], False)
-    arrived(theirs[0], 4, partner)
-    accumulate(3, att_all.at[theirs[0]], False)
+    accumulate(2, att_all.at[down], False)
+    accumulate(3, att_all.at[up], False)
+    for idx in range(1, 3):
+        arrived(theirs[idx], 4 + idx, partner)
+        accumulate(3 + idx, att_all.at[theirs[idx]], False)
     arrived(far, 2, down, first)
     arrived(far, 3, up, second)
     send(att_all.at[far], far, 7, partner)
-    accumulate(4, att_all.at[far], False)
-    for idx in range(1, 4):
-        arrived(theirs[idx], 4 + idx, partner)
-        accumulate(4 + idx, att_all.at[theirs[idx]], False)
+    accumulate(6, att_all.at[far], False)
+    arrived(theirs[3], 7, partner)
+    accumulate(7, att_all.at[theirs[3]], False)
     for copy in sends:
         copy.wait_send()
 

time: 146 us -> 145 us (level)
  no operation moved by 1% of the time
where the time goes in v16:
time: 145 us; the launch traced here: 144 us
  Pallas kernels  94.3 us (65%)
  matrix products  17.3 us (12%)
  between operations  14.3 us (10%)
  other arithmetic  9.47 us (7%)
  local copies, waits for them, and re-layouts  8.07 us (6%)
    pallas_call x1, Pallas kernels, gather_over_tok(): pl.pallas_call(lambda *refs: gather_tok_kernel(tok_count, *refs), out_sha...  53.9 us
    pallas_call x1, Pallas kernels, scatter_over_tok(): pl.pallas_call(lambda *refs: scatter_tok_kernel(tok_count, *refs), out_sh...  21.3 us
    pallas_call x1, Pallas kernels, project_over_tok(): pl.pallas_call(lambda *refs: project_tok_kernel(tok_count, *refs), out_sh...  19.1 us
    dot_general x1, matrix products, local(): jnp.dot(hidden, w_down, preferred_element_type=jnp.float32)  5.7 us
    dot_general x1, matrix products, local(): upward = jnp.dot(normed, w_up, preferred_element_type=jnp.float32)  3.83 us
    dot_general x1, matrix products, local(): gate = jnp.dot(normed, w_gate, preferred_element_type=jnp.float32)  3.54 us
    reduce_sum x5, other arithmetic, rms_scale(): jnp.mean(values_in * values_in, axis=-1, keepdims=True) + EPSILON  2.98 us
  transfers between devices with their start and end apart: 2, of which 2 were waited for; matrix products, arithmetic and copies ran while one was open for 4% of the time, Pallas kernels for 37%

profile of v16, /device:TPU:1, one launch (start us, length us, event | category | flops | bytes accessed | tf_op | source)
XLA Modules:
  0.0 144.3 jit_solution(4192912011307790000)
XLA Ops:
  6.5 1.1 constant_dynamic-slice_fusion.1
  7.6 0.7 fusion.38
  8.4 1.3 dynamic_slice.27
  10.3 53.9 %prefix_gather.1.refs_1_ = bf16[8,256,2560]{2,1,0:T(8,128)(2,1)} custom-call(bf16[256,2560]{1,0:T(8,128)(2,1)} %refs_0_.1), custom_call_target="tpu_custom_call" | custom-call | bytes 20971520 | tf_op jit(solution)/shard_map/prefix_gather/pallas_call | solution.py:97
  64.3 0.1 dynamic_slice.28
  64.3 0.1 all-gather.3.cloned.1.call-done
  64.4 2.9 %gather_fusion = bf16[8,256,512]{2,1,0:T(8,128)(2,1)S(1)} fusion(bf16[16,256,512]{2,1,0:T(8,128)(2,1)} %bitcast.14, s32[1024]{0:T(1024)S(1)} %pad_clamp_fusion), kind=kCustom, calls=%fused_computation | custom fusion | bytes 4194336 | tf_op jit(solution)/shard_map/prefix_gather/jit(_take)/gather | solution.py:381
  67.3 0.8 collective-permute-start
  68.1 0.2 reduce-window.8
  68.2 1.1 fusion.35
  69.3 0.1 convert_reduce_fusion
  69.4 1.0 constant_dynamic-slice_fusion
  70.4 0.1 fusion.32
  70.6 1.1 fusion.37
  71.7 0.2 fusion.21
  71.9 0.1 collective-permute-done
  72.0 1.4 fusion.20
  73.3 1.6 %fusion.44 = (f32[512]{0:T(512)S(1)}, f32[512,4608]{1,0:T(8,128)S(1)}) fusion(bf16[512,256]{1,0:T(8,128)(2,1)S(1)} %fusion.37, bf16[4096,256]{1,0:T(8,128)(2,1)S(1)} %fusion.20, bf16[512,256]{1,0:T(8,128)(2,1)S(1)} %copy-done.1, f32[256]{0:T(256)S(1)} %copy-done.6, f32[512]{0:T(512)S(1)} %add_rsqrt_fusion.3, pred[512,512]{1,0:T(32,128)(4,1)S(1)} %fusion.21), kind=kOutput, calls=%fused_computation.65 | convolution fusion | flops 1220279808 | bytes 12325888 | tf_op jit(solution)/shard_map/attention/dot_general | solution.py:404
  74.9 1.4 fusion
  76.3 2.7 %fusion.27.refs_0_ = bf16[512,256]{1,0:T(8,128)(2,1)S(1)} fusion(bf16[2048,512]{1,0:T(8,128)(2,1)} %collective-permute-done, bf16[2048,512]{1,0:T(8,128)(2,1)S(1)} %bitcast.13, bf16[512,256]{1,0:T(8,128)(2,1)S(1)} %constant_dynamic-slice_fusion, f32[512,4608]{1,0:T(8,128)S(1)} %get-tuple-element.14, f32[512]{0:T(512)S(1)} %get-tuple-element.13, f32[512]{0:T(512)S(1)} %fusion), kind=kOutput, calls=%fused_computation.34 | convolution fusion | flops 1220018176 | bytes 14159872 | tf_op jit(solution)/shard_map/attention/dot_general | solution.py:409
  79.0 19.1 %out_projection.1 = f32[512,2560]{1,0:T(8,128)S(1)} custom-call(bf16[512,256]{1,0:T(8,128)(2,1)S(1)} %fusion.27.refs_0_, bf16[8,256,2560]{2,1,0:T(8,128)(2,1)} %prefix_gather.1.refs_1_), custom_call_target="tpu_custom_call" | custom-call | flops 5368709120 | bytes 15728640 | tf_op jit(solution)/shard_map/out_projection/pallas_call | solution.py:218
  98.1 0.4 multiply_reduce_fusion.1
  98.5 1.3 copy-done
  99.8 1.2 multiply_reduce_fusion
  101.0 0.5 multiply_convert_fusion
  101.6 0.4 slice-done.1
  102.0 3.5 %fusion.45 = f32[512,1280]{1,0:T(8,128)S(1)} fusion(bf16[512,2560]{1,0:T(8,128)(2,1)S(1)} %multiply_convert_fusion, bf16[2560,1280]{1,0:T(8,128)(2,1)S(1)} %bitcast.17), kind=kOutput, calls=%fused_computation.66 | convolution fusion | flops 3355443200 | bytes 11796480 | tf_op jit(solution)/shard_map/feed_forward/dot_general | solution.py:424
  105.6 3.8 %fusion.5 = bf16[512,1280]{1,0:T(8,128)(2,1)S(1)} fusion(bf16[512,2560]{1,0:T(8,128)(2,1)S(1)} %multiply_convert_fusion, bf16[2560,1280]{1,0:T(8,128)(2,1)S(1)} %bitcast.19, f32[512,1280]{1,0:T(8,128)S(1)} %fusion.45), kind=kOutput, calls=%fused_computation.15 | convolution fusion | flops 3361996800 | bytes 13107200 | tf_op jit(solution)/shard_map/feed_forward/dot_general | solution.py:425
  109.4 5.7 %fusion.46.refs_0_ = f32[512,2560]{1,0:T(8,128)S(1)} fusion(bf16[512,1280]{1,0:T(8,128)(2,1)S(1)} %fusion.5, bf16[1280,2560]{1,0:T(8,128)(2,1)} %param.31), kind=kOutput, calls=%fused_computation.67 | convolution fusion | flops 3355443200 | bytes 13107200 | tf_op jit(solution)/shard_map/feed_forward/dot_general | solution.py:429
  115.1 21.3 %feed_forward.1 = f32[64,2560]{1,0:T(8,128)S(1)} custom-call(f32[512,2560]{1,0:T(8,128)S(1)} %fusion.46.refs_0_), custom_call_target="tpu_custom_call" | custom-call | flops 1310720 | bytes 10485760 | tf_op jit(solution)/shard_map/feed_forward/pallas_call | solution.py:317
  136.4 0.1 multiply_reduce_fusion.2
  136.6 0.9 add_convert_fusion
  (34 shorter events, 0.1 us)
Async XLA Ops:
  6.5 57.9 %all-gather.3.cloned.1.call-start = ((), (), s32[]{:S(2)}) async-start(), calls=%async_computation | async-start | bytes 4456448 | tf_op jit(solution)/shard_map/prefix_gather/all_gather | solution.py:376
  10.3 53.9 %copy-start.7 = (s32[16]{0:T(128)S(1)}, s32[16]{0:T(128)}, u32[]{:S(2)}) copy-start(s32[16]{0:T(128)} %param.23) | copy-start | bytes 196
  64.2 3.8 %copy-start.8 = (s32[1,3]{1,0:T(1,128)S(1)}, s32[1,3]{1,0:T(1,128)}, u32[]{:S(2)}) copy-start(s32[1,3]{1,0:T(1,128)} %param.21) | copy-start | bytes 40
  64.2 6.2 %copy-start.1 = (bf16[512,256]{1,0:T(8,128)(2,1)S(1)}, bf16[512,256]{1,0:T(8,128)(2,1)}, u32[]{:S(2)}) copy-start(bf16[512,256]{1,0:T(8,128)(2,1)} %param.16) | copy-start | bytes 786436
  64.4 6.2 %copy-start.5 = (f32[256]{0:T(256)S(1)}, f32[256]{0:T(256)}, u32[]{:S(2)}) copy-start(f32[256]{0:T(256)} %param.20) | copy-start | bytes 3076
  67.3 4.7 %collective-permute-start = (bf16[2048,512]{1,0:T(8,128)(2,1)S(1)}, bf16[2048,512]{1,0:T(8,128)(2,1)}, u32[]{:S(2)}, u32[]{:S(2)}) collective-permute-start(bf16[2048,512]{1,0:T(8,128)(2,1)S(1)} %bitcast.11), channel_id=1, source_target_pairs={{0,1},{1,0},{2,3},{3,2},{4,5},{5,4},{6,7},{7,6},{8,9},{9,8},{10,11... | collective-permute-start | bytes 6291464 | tf_op jit(solution)/shard_map/prefix_gather/ppermute | solution.py:383
  71.9 1.4 %copy-start.6 = (f32[256]{0:T(256)S(1)}, f32[256]{0:T(256)}, u32[]{:S(2)}) copy-start(f32[256]{0:T(256)} %param.19) | copy-start | bytes 3076
  98.1 1.7 %copy-start = (bf16[512,2560]{1,0:T(8,128)(2,1)S(1)}, bf16[512,2560]{1,0:T(8,128)(2,1)}, u32[]{:S(2)}) copy-start(bf16[512,2560]{1,0:T(8,128)(2,1)} %param.24) | copy-start | bytes 7864324
  98.1 1.7 %copy-start.2 = (f32[2560]{0:T(1024)S(1)}, f32[2560]{0:T(1024)}, u32[]{:S(2)}) copy-start(f32[2560]{0:T(1024)} %param.26) | copy-start | bytes 30724
  98.1 3.4 %slice-start = ((s8[6553600]{0:T(1024)(128)(4,1)}), s8[4194304]{0:T(1024)(128)(4,1)S(1)}, s32[]{:S(2)}) async-start(s8[6553600]{0:T(1024)(128)(4,1)} %bitcast.16), calls=%async_computation.1 | async-start | bytes 8388608
  99.8 1.2 copy-start.3
  99.8 2.2 %slice-start.1 = ((s8[6553600]{0:T(1024)(128)(4,1)}), s8[2359296]{0:T(1024)(128)(4,1)S(1)}, s32[]{:S(2)}) async-start(s8[6553600]{0:T(1024)(128)(4,1)} %bitcast.16), calls=%async_computation.2 | async-start | bytes 4718592
  101.0 4.5 %slice-start.2 = ((s8[6553600]{0:T(1024)(128)(4,1)}), s8[4194304]{0:T(1024)(128)(4,1)S(1)}, s32[]{:S(2)}) async-start(s8[6553600]{0:T(1024)(128)(4,1)} %bitcast.18), calls=%async_computation.3 | async-start | bytes 8388608
  102.0 3.6 %slice-start.3 = ((s8[6553600]{0:T(1024)(128)(4,1)}), s8[2359296]{0:T(1024)(128)(4,1)S(1)}, s32[]{:S(2)}) async-start(s8[6553600]{0:T(1024)(128)(4,1)} %bitcast.18), calls=%async_computation.4 | async-start | bytes 4718592
  115.1 21.5 %copy-start.4 = (f32[2560]{0:T(1024)S(1)}, f32[2560]{0:T(1024)}, u32[]{:S(2)}) copy-start(f32[2560]{0:T(1024)} %param.28) | copy-start | bytes 30724
Sparse Core Ops, SparseCore 0:
  9.5 54.8 all-gather.2

commit v17 on v16

--- a/solution.py
+++ b/solution.py
@@ -367,12 +367,14 @@
     own_count = req_count // GROUPS
 
     with jax.named_scope("prefix_gather"):
-        pref_keys = lax.dynamic_slice_in_dim(prefix_cache, kv_first * HD, HD, 1)
-        pref_vals = lax.dynamic_slice_in_dim(prefix_cache, kv_width + kv_first * HD, HD, 1)
-        pref_kv = jnp.concatenate([pref_keys, pref_vals], axis=1)
-        half_rows = pref_kv.shape[0] // 2
+        half_rows = prefix_cache.shape[0] // 2
         core = tok_index % 2
-        my_half = lax.dynamic_slice_in_dim(pref_kv, core * half_rows, half_rows, 0)
+        first_row_kv = core * half_rows
+        half_keys = lax.dynamic_slice(prefix_cache, (first_row_kv, kv_first * HD), (half_rows, HD))
+        half_vals = lax.dynamic_slice(
+            prefix_cache, (first_row_kv, kv_width + kv_first * HD), (half_rows, HD)
+        )
+        my_half = jnp.concatenate([half_keys, half_vals], axis=1)
         gathered = lax.all_gather(my_half, "req", axis=0, tiled=False)
         w_out_all = gather_over_tok(w_out, tok_count, 0)
         gathered, w_out_all = lax.optimization_barrier((gathered, w_out_all))

time: 145 us -> 145 us (level)
  no operation moved by 1% of the time
where the time goes in v17:
time: 145 us; the launch traced here: 144 us
  Pallas kernels  94.3 us (65%)
  matrix products  17.3 us (12%)
  between operations  14.3 us (10%)
  other arithmetic  9.46 us (7%)
  local copies, waits for them, and re-layouts  7.99 us (6%)
    pallas_call x1, Pallas kernels, gather_over_tok(): pl.pallas_call(lambda *refs: gather_tok_kernel(tok_count, *refs), out_sha...  53.9 us
    pallas_call x1, Pallas kernels, scatter_over_tok(): pl.pallas_call(lambda *refs: scatter_tok_kernel(tok_count, *refs), out_sh...  21.3 us
    pallas_call x1, Pallas kernels, project_over_tok(): pl.pallas_call(lambda *refs: project_tok_kernel(tok_count, *refs), out_sh...  19.1 us
    dot_general x1, matrix products, local(): jnp.dot(hidden, w_down, preferred_element_type=jnp.float32)  5.7 us
    dot_general x1, matrix products, local(): upward = jnp.dot(normed, w_up, preferred_element_type=jnp.float32)  3.83 us
    dot_general x1, matrix products, local(): gate = jnp.dot(normed, w_gate, preferred_element_type=jnp.float32)  3.54 us
    reduce_sum x5, other arithmetic, rms_scale(): jnp.mean(values_in * values_in, axis=-1, keepdims=True) + EPSILON  2.98 us
  transfers between devices with their start and end apart: 2, of which 2 were waited for; matrix products, arithmetic and copies ran while one was open for 4% of the time, Pallas kernels for 37%

profile of v17, /device:TPU:1, one launch (start us, length us, event | category | flops | bytes accessed | tf_op | source)
XLA Modules:
  0.0 144.3 jit_solution(4599935203123681342)
XLA Ops:
  6.5 1.0 fusion.43
  7.5 0.7 pad_maximum_fusion.1
  8.3 1.3 dynamic_slice.23
  10.2 53.9 %prefix_gather.1.refs_1_ = bf16[8,256,2560]{2,1,0:T(8,128)(2,1)} custom-call(bf16[256,2560]{1,0:T(8,128)(2,1)} %refs_0_.1), custom_call_target="tpu_custom_call" | custom-call | bytes 20971520 | tf_op jit(solution)/shard_map/prefix_gather/pallas_call | solution.py:97
  64.2 0.1 dynamic_slice.24
  64.3 0.1 all-gather.3.cloned.1.call-done
  64.4 2.9 %gather_fusion = bf16[8,256,512]{2,1,0:T(8,128)(2,1)S(1)} fusion(bf16[16,256,512]{2,1,0:T(8,128)(2,1)} %bitcast.14, s32[1024]{0:T(1024)S(1)} %pad_clamp_fusion), kind=kCustom, calls=%fused_computation | custom fusion | bytes 4194336 | tf_op jit(solution)/shard_map/prefix_gather/jit(_take)/gather | solution.py:383
  67.3 0.8 collective-permute-start
  68.1 0.2 reduce-window.8
  68.2 1.1 fusion.35
  69.3 0.1 convert_reduce_fusion
  69.4 1.0 constant_dynamic-slice_fusion
  70.4 0.1 fusion.32
  70.6 1.1 fusion.37
  71.7 0.2 fusion.21
  71.9 0.1 collective-permute-done
  72.0 1.4 fusion.20
  73.3 1.6 %fusion.44 = (f32[512]{0:T(512)S(1)}, f32[512,4608]{1,0:T(8,128)S(1)}) fusion(bf16[512,256]{1,0:T(8,128)(2,1)S(1)} %fusion.37, bf16[4096,256]{1,0:T(8,128)(2,1)S(1)} %fusion.20, bf16[512,256]{1,0:T(8,128)(2,1)S(1)} %copy-done.1, f32[256]{0:T(256)S(1)} %copy-done.6, f32[512]{0:T(512)S(1)} %add_rsqrt_fusion.3, pred[512,512]{1,0:T(32,128)(4,1)S(1)} %fusion.21), kind=kOutput, calls=%fused_computation.62 | convolution fusion | flops 1220279808 | bytes 12325888 | tf_op jit(solution)/shard_map/attention/dot_general | solution.py:406
  74.9 1.4 fusion
  76.3 2.7 %fusion.27.refs_0_ = bf16[512,256]{1,0:T(8,128)(2,1)S(1)} fusion(bf16[2048,512]{1,0:T(8,128)(2,1)} %collective-permute-done, bf16[2048,512]{1,0:T(8,128)(2,1)S(1)} %bitcast.13, bf16[512,256]{1,0:T(8,128)(2,1)S(1)} %constant_dynamic-slice_fusion, f32[512,4608]{1,0:T(8,128)S(1)} %get-tuple-element.14, f32[512]{0:T(512)S(1)} %get-tuple-element.13, f32[512]{0:T(512)S(1)} %fusion), kind=kOutput, calls=%fused_computation.34 | convolution fusion | flops 1220018176 | bytes 14159872 | tf_op jit(solution)/shard_map/attention/dot_general | solution.py:411
  79.0 19.1 %out_projection.1 = f32[512,2560]{1,0:T(8,128)S(1)} custom-call(bf16[512,256]{1,0:T(8,128)(2,1)S(1)} %fusion.27.refs_0_, bf16[8,256,2560]{2,1,0:T(8,128)(2,1)} %prefix_gather.1.refs_1_), custom_call_target="tpu_custom_call" | custom-call | flops 5368709120 | bytes 15728640 | tf_op jit(solution)/shard_map/out_projection/pallas_call | solution.py:218
  98.1 0.4 multiply_reduce_fusion.1
  98.5 1.3 copy-done
  99.8 1.2 multiply_reduce_fusion
  101.0 0.5 multiply_convert_fusion
  101.6 0.4 slice-done.1
  102.0 3.5 %fusion.45 = f32[512,1280]{1,0:T(8,128)S(1)} fusion(bf16[512,2560]{1,0:T(8,128)(2,1)S(1)} %multiply_convert_fusion, bf16[2560,1280]{1,0:T(8,128)(2,1)S(1)} %bitcast.17), kind=kOutput, calls=%fused_computation.63 | convolution fusion | flops 3355443200 | bytes 11796480 | tf_op jit(solution)/shard_map/feed_forward/dot_general | solution.py:426
  105.6 3.8 %fusion.5 = bf16[512,1280]{1,0:T(8,128)(2,1)S(1)} fusion(bf16[512,2560]{1,0:T(8,128)(2,1)S(1)} %multiply_convert_fusion, bf16[2560,1280]{1,0:T(8,128)(2,1)S(1)} %bitcast.19, f32[512,1280]{1,0:T(8,128)S(1)} %fusion.45), kind=kOutput, calls=%fused_computation.15 | convolution fusion | flops 3361996800 | bytes 13107200 | tf_op jit(solution)/shard_map/feed_forward/dot_general | solution.py:427
  109.4 5.7 %fusion.46.refs_0_ = f32[512,2560]{1,0:T(8,128)S(1)} fusion(bf16[512,1280]{1,0:T(8,128)(2,1)S(1)} %fusion.5, bf16[1280,2560]{1,0:T(8,128)(2,1)} %param.31), kind=kOutput, calls=%fused_computation.64 | convolution fusion | flops 3355443200 | bytes 13107200 | tf_op jit(solution)/shard_map/feed_forward/dot_general | solution.py:431
  115.1 21.3 %feed_forward.1 = f32[64,2560]{1,0:T(8,128)S(1)} custom-call(f32[512,2560]{1,0:T(8,128)S(1)} %fusion.46.refs_0_), custom_call_target="tpu_custom_call" | custom-call | flops 1310720 | bytes 10485760 | tf_op jit(solution)/shard_map/feed_forward/pallas_call | solution.py:317
  136.4 0.1 multiply_reduce_fusion.2
  136.6 0.9 add_convert_fusion
  (34 shorter events, 0.1 us)
Async XLA Ops:
  6.5 57.9 %all-gather.3.cloned.1.call-start = ((), (), s32[]{:S(2)}) async-start(), calls=%async_computation | async-start | bytes 4456448 | tf_op jit(solution)/shard_map/prefix_gather/all_gather | solution.py:378
  10.2 53.9 %copy-start.7 = (s32[16]{0:T(128)S(1)}, s32[16]{0:T(128)}, u32[]{:S(2)}) copy-start(s32[16]{0:T(128)} %param.23) | copy-start | bytes 196
  64.1 3.9 %copy-start.8 = (s32[1,3]{1,0:T(1,128)S(1)}, s32[1,3]{1,0:T(1,128)}, u32[]{:S(2)}) copy-start(s32[1,3]{1,0:T(1,128)} %param.21) | copy-start | bytes 40
  64.1 6.2 %copy-start.1 = (bf16[512,256]{1,0:T(8,128)(2,1)S(1)}, bf16[512,256]{1,0:T(8,128)(2,1)}, u32[]{:S(2)}) copy-start(bf16[512,256]{1,0:T(8,128)(2,1)} %param.16) | copy-start | bytes 786436
  64.4 6.2 %copy-start.5 = (f32[256]{0:T(256)S(1)}, f32[256]{0:T(256)}, u32[]{:S(2)}) copy-start(f32[256]{0:T(256)} %param.20) | copy-start | bytes 3076
  67.3 4.7 %collective-permute-start = (bf16[2048,512]{1,0:T(8,128)(2,1)S(1)}, bf16[2048,512]{1,0:T(8,128)(2,1)}, u32[]{:S(2)}, u32[]{:S(2)}) collective-permute-start(bf16[2048,512]{1,0:T(8,128)(2,1)S(1)} %bitcast.11), channel_id=1, source_target_pairs={{0,1},{1,0},{2,3},{3,2},{4,5},{5,4},{6,7},{7,6},{8,9},{9,8},{10,11... | collective-permute-start | bytes 6291464 | tf_op jit(solution)/shard_map/prefix_gather/ppermute | solution.py:385
  71.9 1.4 %copy-start.6 = (f32[256]{0:T(256)S(1)}, f32[256]{0:T(256)}, u32[]{:S(2)}) copy-start(f32[256]{0:T(256)} %param.19) | copy-start | bytes 3076
  98.1 1.7 %copy-start = (bf16[512,2560]{1,0:T(8,128)(2,1)S(1)}, bf16[512,2560]{1,0:T(8,128)(2,1)}, u32[]{:S(2)}) copy-start(bf16[512,2560]{1,0:T(8,128)(2,1)} %param.24) | copy-start | bytes 7864324
  98.1 1.7 %copy-start.2 = (f32[2560]{0:T(1024)S(1)}, f32[2560]{0:T(1024)}, u32[]{:S(2)}) copy-start(f32[2560]{0:T(1024)} %param.26) | copy-start | bytes 30724
  98.1 3.4 %slice-start = ((s8[6553600]{0:T(1024)(128)(4,1)}), s8[4194304]{0:T(1024)(128)(4,1)S(1)}, s32[]{:S(2)}) async-start(s8[6553600]{0:T(1024)(128)(4,1)} %bitcast.16), calls=%async_computation.1 | async-start | bytes 8388608
  99.8 1.2 copy-start.3
  99.8 2.2 %slice-start.1 = ((s8[6553600]{0:T(1024)(128)(4,1)}), s8[2359296]{0:T(1024)(128)(4,1)S(1)}, s32[]{:S(2)}) async-start(s8[6553600]{0:T(1024)(128)(4,1)} %bitcast.16), calls=%async_computation.2 | async-start | bytes 4718592
  101.0 4.5 %slice-start.2 = ((s8[6553600]{0:T(1024)(128)(4,1)}), s8[4194304]{0:T(1024)(128)(4,1)S(1)}, s32[]{:S(2)}) async-start(s8[6553600]{0:T(1024)(128)(4,1)} %bitcast.18), calls=%async_computation.3 | async-start | bytes 8388608
  102.0 3.6 %slice-start.3 = ((s8[6553600]{0:T(1024)(128)(4,1)}), s8[2359296]{0:T(1024)(128)(4,1)S(1)}, s32[]{:S(2)}) async-start(s8[6553600]{0:T(1024)(128)(4,1)} %bitcast.18), calls=%async_computation.4 | async-start | bytes 4718592
  115.1 21.5 %copy-start.4 = (f32[2560]{0:T(1024)S(1)}, f32[2560]{0:T(1024)}, u32[]{:S(2)}) copy-start(f32[2560]{0:T(1024)} %param.28) | copy-start | bytes 30724
Sparse Core Ops, SparseCore 0:
  9.5 54.8 all-gather.2

commit v18 on v17

--- a/solution.py
+++ b/solution.py
@@ -112,7 +112,20 @@
 
 
 def project_tok_kernel(
-    tok_count, att_ref, w_hbm, out_ref, att_all, w_buf, send_sem, recv_sem, load_sem
+    tok_count,
+    att_ref,
+    w_hbm,
+    res_ref,
+    attn_gain_ref,
+    ffn_gain_ref,
+    normed_ref,
+    mixed_ref,
+    out_ref,
+    att_all,
+    w_buf,
+    send_sem,
+    recv_sem,
+    load_sem,
 ):
     mesh_ids = pl.DeviceIdType.MESH
     me = lax.axis_index("tok")
@@ -206,21 +219,40 @@
     accumulate(6, att_all.at[far], False)
     arrived(theirs[3], 7, partner)
     accumulate(7, att_all.at[theirs[3]], False)
+
+    share = mixed_ref.shape[0]
+
+    def finish(block):
+        rows = pl.ds(pl.multiple_of(block * share, share), share)
+        mixed = res_ref[rows, :].astype(jnp.float32) + rms_scale(out_ref[rows, :], attn_gain_ref[...])
+        normed_ref[rows, :] = rms_scale(mixed, ffn_gain_ref[...]).astype(normed_ref.dtype)
+
+    pl.loop(0, out_ref.shape[0] // share)(finish)
+    own_rows = pl.ds(pl.multiple_of(me * share, share), share)
+    mixed_ref[...] = res_ref[own_rows, :].astype(jnp.float32) + rms_scale(
+        out_ref[own_rows, :], attn_gain_ref[...]
+    )
     for copy in sends:
         copy.wait_send()
 
 
-def project_over_tok(attention, w_all, tok_count, collective_id):
+def project_over_tok(attention, w_all, residual, attn_gain, ffn_gain, tok_count, collective_id):
     assert tok_count == 8
     rows, width = attention.shape
     cols = w_all.shape[2]
+    share = rows // tok_count
     vmem = pltpu.MemorySpace.VMEM
+    vmem_spec = pl.BlockSpec(memory_space=vmem)
     return pl.pallas_call(
         lambda *refs: project_tok_kernel(tok_count, *refs),
-        out_shape=jax.ShapeDtypeStruct((rows, cols), jnp.float32),
-        in_specs=[pl.BlockSpec(memory_space=vmem), pl.BlockSpec(memory_space=pl.ANY)],
-        out_specs=pl.BlockSpec(memory_space=vmem),
+        out_shape=(
+            jax.ShapeDtypeStruct((rows, cols), jnp.bfloat16),
+            jax.ShapeDtypeStruct((share, cols), jnp.float32),
+        ),
+        in_specs=[vmem_spec, pl.BlockSpec(memory_space=pl.ANY), vmem_spec, vmem_spec, vmem_spec],
+        out_specs=(vmem_spec, vmem_spec),
         scratch_shapes=[
+            pltpu.VMEM((rows, cols), jnp.float32),
             pltpu.VMEM((tok_count, rows, width), attention.dtype),
             pltpu.VMEM((2, width, cols), w_all.dtype),
             pltpu.SemaphoreType.DMA((8,)),
@@ -232,10 +264,10 @@
         ),
         cost_estimate=pl.CostEstimate(
             flops=2 * rows * width * tok_count * cols,
-            transcendentals=0,
+            transcendentals=2 * rows,
             bytes_accessed=tok_count * width * cols * 2 + rows * cols * 4,
         ),
-    )(attention, w_all)
+    )(attention, w_all, residual, attn_gain.reshape(1, cols), ffn_gain.reshape(1, cols))
 
 
 def scatter_tok_kernel(
@@ -417,10 +449,9 @@
     share = row_count // tok_count
     first_row = tok_index * share
     with jax.named_scope("out_projection"):
-        projected = project_over_tok(attention, w_out_all, tok_count, 1)
-        mixed_rows = residual.astype(jnp.float32) + rms_scale(projected, attn_gain)
-        normed = rms_scale(mixed_rows, ffn_in_gain).astype(jnp.bfloat16)
-        mixed_share = lax.dynamic_slice_in_dim(mixed_rows, first_row, share, 0)
+        normed, mixed_share = project_over_tok(
+            attention, w_out_all, residual, attn_gain, ffn_in_gain, tok_count, 1
+        )
     with jax.named_scope("feed_forward"):
         normed = lax.optimization_barrier(normed)
         gate = jnp.dot(normed, w_gate, preferred_element_type=jnp.float32)

time: 145 us -> 144 us (level)
  Pallas kernels: 94.3 us -> 97.2 us
  other arithmetic: 9.46 us -> 7.35 us
  local copies, waits for them, and re-layouts: 7.99 us -> 6.33 us
    pallas_call x1, Pallas kernels: 19.1 us -> 22 us  [project_over_tok(): pl.pallas_call(lambda *refs: project_tok_kernel(tok_count, *refs), out_sh...]
    unnamed x26, local copies, waits for them, and re-layouts: 1.78 us -> 0.08 us
    reduce_sum x5 -> x3, other arithmetic: 2.98 us -> 1.4 us  [rms_scale(): jnp.mean(values_in * values_in, axis=-1, keepdims=True) + EPSILON]
  transfers between devices with their start and end apart: 2 -> 2, of which waited for: 2 -> 1; matrix products, arithmetic and copies ran while one was open for 4% -> 4% of each run, Pallas kernels for 37% -> 38%
where the time goes in v18:
time: 144 us
  Pallas kernels  97.2 us (68%)
  matrix products  17.4 us (12%)
  between operations  14.4 us (10%)
  other arithmetic  7.35 us (5%)
  local copies, waits for them, and re-layouts  6.33 us (4%)
    pallas_call x1, Pallas kernels, gather_over_tok(): pl.pallas_call(lambda *refs: gather_tok_kernel(tok_count, *refs), out_sha...  53.9 us
    pallas_call x1, Pallas kernels, project_over_tok(): pl.pallas_call(lambda *refs: project_tok_kernel(tok_count, *refs), out_sh...  22 us
    pallas_call x1, Pallas kernels, scatter_over_tok(): pl.pallas_call(lambda *refs: scatter_tok_kernel(tok_count, *refs), out_sh...  21.3 us
    dot_general x1, matrix products, local(): jnp.dot(hidden, w_down, preferred_element_type=jnp.float32)  5.7 us
    dot_general x1, matrix products, local(): upward = jnp.dot(normed, w_up, preferred_element_type=jnp.float32)  3.84 us
    dot_general x1, matrix products, local(): gate = jnp.dot(normed, w_gate, preferred_element_type=jnp.float32)  3.54 us
    gather x1, local copies, waits for them, and re-layouts, local(): jnp.take(gathered, owner_ids, axis=0, mode='clip').reshape(-1, 2 * HD)  2.88 us
  transfers between devices with their start and end apart: 2, of which 1 were waited for; matrix products, arithmetic and copies ran while one was open for 4% of the time, Pallas kernels for 38%

profile of v18, /device:TPU:1, one launch (start us, length us, event | category | flops | bytes accessed | tf_op | source)
XLA Modules:
  0.0 143.6 jit_solution(10115491620201416639)
XLA Ops:
  6.5 1.0 fusion.43
  7.5 0.7 pad_maximum_fusion.1
  8.2 0.0 all-gather.3.cloned.1.call-update
  8.3 1.3 dynamic_slice.20
  10.3 53.9 %prefix_gather.1.refs_1_ = bf16[8,256,2560]{2,1,0:T(8,128)(2,1)} custom-call(bf16[256,2560]{1,0:T(8,128)(2,1)} %refs_0_.1), custom_call_target="tpu_custom_call" | custom-call | bytes 20971520 | tf_op jit(solution)/shard_map/prefix_gather/pallas_call | solution.py:97
  64.3 0.1 dynamic_slice.21
  64.4 0.1 all-gather.3.cloned.1.call-done
  64.4 2.9 %gather_fusion = bf16[8,256,512]{2,1,0:T(8,128)(2,1)S(1)} fusion(bf16[16,256,512]{2,1,0:T(8,128)(2,1)} %bitcast.14, s32[1024]{0:T(1024)S(1)} %pad_clamp_fusion), kind=kCustom, calls=%fused_computation | custom fusion | bytes 4194336 | tf_op jit(solution)/shard_map/prefix_gather/jit(_take)/gather | solution.py:415
  67.3 0.8 collective-permute-start
  68.1 0.2 reduce-window.8
  68.3 1.1 fusion.35
  69.4 0.1 convert_reduce_fusion
  69.5 1.0 constant_dynamic-slice_fusion
  70.4 0.1 fusion.32
  70.6 1.1 fusion.37
  71.7 0.2 fusion.21
  72.0 0.0 collective-permute-done
  72.0 1.4 fusion.20
  73.3 1.6 %fusion.44 = (f32[512]{0:T(512)S(1)}, f32[512,4608]{1,0:T(8,128)S(1)}) fusion(bf16[512,256]{1,0:T(8,128)(2,1)S(1)} %fusion.37, bf16[4096,256]{1,0:T(8,128)(2,1)S(1)} %fusion.20, bf16[512,256]{1,0:T(8,128)(2,1)S(1)} %copy-done.1, f32[256]{0:T(256)S(1)} %copy-done.6, f32[512]{0:T(512)S(1)} %add_rsqrt_fusion.1, pred[512,512]{1,0:T(32,128)(4,1)S(1)} %fusion.21), kind=kOutput, calls=%fused_computation.56 | convolution fusion | flops 1220279808 | bytes 12325888 | tf_op jit(solution)/shard_map/attention/dot_general | solution.py:438
  74.9 1.4 fusion
  76.3 0.0 slice-start
  76.3 2.8 %fusion.27.refs_0_ = bf16[512,256]{1,0:T(8,128)(2,1)S(1)} fusion(bf16[2048,512]{1,0:T(8,128)(2,1)} %collective-permute-done, bf16[2048,512]{1,0:T(8,128)(2,1)S(1)} %bitcast.13, bf16[512,256]{1,0:T(8,128)(2,1)S(1)} %constant_dynamic-slice_fusion, f32[512,4608]{1,0:T(8,128)S(1)} %get-tuple-element.16, f32[512]{0:T(512)S(1)} %get-tuple-element.15, f32[512]{0:T(512)S(1)} %fusion), kind=kOutput, calls=%fused_computation.30 | convolution fusion | flops 1220018176 | bytes 14159872 | tf_op jit(solution)/shard_map/attention/dot_general | solution.py:443
  79.2 0.0 slice-start.1
  79.2 0.0 slice-start.2
  79.2 22.0 %out_projection.1 = (bf16[512,2560]{1,0:T(8,128)(2,1)S(1)}, f32[64,2560]{1,0:T(8,128)S(1)}) custom-call(bf16[512,256]{1,0:T(8,128)(2,1)S(1)} %fusion.27.refs_0_, bf16[8,256,2560]{2,1,0:T(8,128)(2,1)} %prefix_gather.1.refs_1_, bf16[512,2560]{1,0:T(8,128)(2,1)S(1)} %copy-done, f32[1,2560]{1,0:T(1,128)S(1)} %reshape.97.refs_3_, f32[1,2560]{1,0:T(1,128)S(1)} %reshape.98.refs_4_), custom_call_target="tpu_custom_call" | custom-call | flops 5368709120 | bytes 15728640 | tf_op jit(solution)/shard_map/out_projection/pallas_call | solution.py:246
  101.2 0.0 slice-start.3
  101.2 3.5 %fusion.45 = f32[512,1280]{1,0:T(8,128)S(1)} fusion(bf16[512,2560]{1,0:T(8,128)(2,1)S(1)} %get-tuple-element.12, bf16[2560,1280]{1,0:T(8,128)(2,1)S(1)} %bitcast.17), kind=kOutput, calls=%fused_computation.57 | convolution fusion | flops 3355443200 | bytes 11796480 | tf_op jit(solution)/shard_map/feed_forward/dot_general | solution.py:457
  104.8 3.8 %fusion.5 = bf16[512,1280]{1,0:T(8,128)(2,1)S(1)} fusion(bf16[512,2560]{1,0:T(8,128)(2,1)S(1)} %get-tuple-element.12, bf16[2560,1280]{1,0:T(8,128)(2,1)S(1)} %bitcast.19, f32[512,1280]{1,0:T(8,128)S(1)} %fusion.45), kind=kOutput, calls=%fused_computation.11 | convolution fusion | flops 3361996800 | bytes 13107200 | tf_op jit(solution)/shard_map/feed_forward/dot_general | solution.py:458
  108.7 5.7 %fusion.46.refs_0_ = f32[512,2560]{1,0:T(8,128)S(1)} fusion(bf16[512,1280]{1,0:T(8,128)(2,1)S(1)} %fusion.5, bf16[1280,2560]{1,0:T(8,128)(2,1)} %param.31), kind=kOutput, calls=%fused_computation.58 | convolution fusion | flops 3355443200 | bytes 13107200 | tf_op jit(solution)/shard_map/feed_forward/dot_general | solution.py:462
  114.4 21.3 %feed_forward.1 = f32[64,2560]{1,0:T(8,128)S(1)} custom-call(f32[512,2560]{1,0:T(8,128)S(1)} %fusion.46.refs_0_), custom_call_target="tpu_custom_call" | custom-call | flops 1310720 | bytes 10485760 | tf_op jit(solution)/shard_map/feed_forward/pallas_call | solution.py:349
  135.7 0.1 multiply_reduce_fusion
  135.9 0.9 add_convert_fusion
  (31 shorter events, 0.1 us)
Async XLA Ops:
  6.5 57.9 %all-gather.3.cloned.1.call-start = ((), (), s32[]{:S(2)}) async-start(), calls=%async_computation | async-start | bytes 4456448 | tf_op jit(solution)/shard_map/prefix_gather/all_gather | solution.py:410
  10.3 54.0 %copy-start.7 = (s32[16]{0:T(128)S(1)}, s32[16]{0:T(128)}, u32[]{:S(2)}) copy-start(s32[16]{0:T(128)} %param.23) | copy-start | bytes 196
  64.2 3.9 %copy-start.8 = (s32[1,3]{1,0:T(1,128)S(1)}, s32[1,3]{1,0:T(1,128)}, u32[]{:S(2)}) copy-start(s32[1,3]{1,0:T(1,128)} %param.21) | copy-start | bytes 40
  64.2 4.0 %copy-start.3 = (f32[2560]{0:T(1024)S(1)}, f32[2560]{0:T(1024)}, u32[]{:S(2)}) copy-start(f32[2560]{0:T(1024)} %param.26) | copy-start | bytes 30724
  64.2 4.0 %copy-start.4 = (f32[2560]{0:T(1024)S(1)}, f32[2560]{0:T(1024)}, u32[]{:S(2)}) copy-start(f32[2560]{0:T(1024)} %param.27) | copy-start | bytes 30724
  64.2 6.2 %copy-start.1 = (bf16[512,256]{1,0:T(8,128)(2,1)S(1)}, bf16[512,256]{1,0:T(8,128)(2,1)}, u32[]{:S(2)}) copy-start(bf16[512,256]{1,0:T(8,128)(2,1)} %param.16) | copy-start | bytes 786436
  64.4 6.2 %copy-start.5 = (f32[256]{0:T(256)S(1)}, f32[256]{0:T(256)}, u32[]{:S(2)}) copy-start(f32[256]{0:T(256)} %param.20) | copy-start | bytes 3076
  67.3 4.7 %collective-permute-start = (bf16[2048,512]{1,0:T(8,128)(2,1)S(1)}, bf16[2048,512]{1,0:T(8,128)(2,1)}, u32[]{:S(2)}, u32[]{:S(2)}) collective-permute-start(bf16[2048,512]{1,0:T(8,128)(2,1)S(1)} %bitcast.11), channel_id=1, source_target_pairs={{0,1},{1,0},{2,3},{3,2},{4,5},{5,4},{6,7},{7,6},{8,9},{9,8},{10,11... | collective-permute-start | bytes 6291464 | tf_op jit(solution)/shard_map/prefix_gather/ppermute | solution.py:417
  71.9 1.4 copy-start.6
  76.3 2.8 %copy-start = (bf16[512,2560]{1,0:T(8,128)(2,1)S(1)}, bf16[512,2560]{1,0:T(8,128)(2,1)}, u32[]{:S(2)}) copy-start(bf16[512,2560]{1,0:T(8,128)(2,1)} %refs_2_.1) | copy-start | bytes 7864324
  76.3 24.9 %slice-start = ((s8[6553600]{0:T(1024)(128)(4,1)}), s8[4194304]{0:T(1024)(128)(4,1)S(1)}, s32[]{:S(2)}) async-start(s8[6553600]{0:T(1024)(128)(4,1)} %bitcast.16), calls=%async_computation.1 | async-start | bytes 8388608
  79.2 22.0 %slice-start.1 = ((s8[6553600]{0:T(1024)(128)(4,1)}), s8[2359296]{0:T(1024)(128)(4,1)S(1)}, s32[]{:S(2)}) async-start(s8[6553600]{0:T(1024)(128)(4,1)} %bitcast.16), calls=%async_computation.2 | async-start | bytes 4718592
  79.2 25.6 %slice-start.2 = ((s8[6553600]{0:T(1024)(128)(4,1)}), s8[2359296]{0:T(1024)(128)(4,1)S(1)}, s32[]{:S(2)}) async-start(s8[6553600]{0:T(1024)(128)(4,1)} %bitcast.18), calls=%async_computation.3 | async-start | bytes 4718592
  101.2 3.6 %slice-start.3 = ((s8[6553600]{0:T(1024)(128)(4,1)}), s8[4194304]{0:T(1024)(128)(4,1)S(1)}, s32[]{:S(2)}) async-start(s8[6553600]{0:T(1024)(128)(4,1)} %bitcast.18), calls=%async_computation.4 | async-start | bytes 8388608
  114.4 21.5 %copy-start.2 = (f32[2560]{0:T(1024)S(1)}, f32[2560]{0:T(1024)}, u32[]{:S(2)}) copy-start(f32[2560]{0:T(1024)} %param.28) | copy-start | bytes 30724
Sparse Core Ops, SparseCore 0:
  9.5 54.8 all-gather.2

commit v19 on v18

--- a/solution.py
+++ b/solution.py
@@ -271,7 +271,18 @@
 
 
 def scatter_tok_kernel(
-    tok_count, part_hbm, out_ref, mine, chip_in, cross_out, cross_in, load_sem, send_sem, recv_sem
+    tok_count,
+    part_hbm,
+    mixed_ref,
+    gain_ref,
+    out_ref,
+    mine,
+    chip_in,
+    cross_out,
+    cross_in,
+    load_sem,
+    send_sem,
+    recv_sem,
 ):
     mesh_ids = pl.DeviceIdType.MESH
     me = lax.axis_index("tok")
@@ -336,20 +347,24 @@
         remote(cross_out.at[idx], cross_in.at[idx], 4 + idx, peer).wait_recv()
     for idx in range(3):
         total = total + cross_in[idx].astype(jnp.float32)
-    out_ref[...] = total
+    out_ref[...] = (mixed_ref[...] + rms_scale(total, gain_ref[...])).astype(out_ref.dtype)
     for copy in sends:
         copy.wait_send()
 
 
-def scatter_over_tok(partial, tok_count, collective_id):
+def scatter_over_tok(partial, mixed_share, gain, tok_count, collective_id):
     assert tok_count == 8
     rows, cols = partial.shape
     share = rows // tok_count
     vmem = pltpu.MemorySpace.VMEM
     return pl.pallas_call(
         lambda *refs: scatter_tok_kernel(tok_count, *refs),
-        out_shape=jax.ShapeDtypeStruct((share, cols), jnp.float32),
-        in_specs=[pl.BlockSpec(memory_space=pltpu.MemorySpace.HBM)],
+        out_shape=jax.ShapeDtypeStruct((share, cols), jnp.bfloat16),
+        in_specs=[
+            pl.BlockSpec(memory_space=pltpu.MemorySpace.HBM),
+            pl.BlockSpec(memory_space=vmem),
+            pl.BlockSpec(memory_space=vmem),
+        ],
         out_specs=pl.BlockSpec(memory_space=vmem),
         scratch_shapes=[
             pltpu.VMEM((4, share, cols), jnp.float32),
@@ -366,7 +381,7 @@
         cost_estimate=pl.CostEstimate(
             flops=8 * share * cols, transcendentals=0, bytes_accessed=rows * cols * 4 * 2
         ),
-    )(partial)
+    )(partial, mixed_share, gain.reshape(1, cols))
 
 
 def local(
@@ -458,12 +473,13 @@
         upward = jnp.dot(normed, w_up, preferred_element_type=jnp.float32)
         hidden = (jax.nn.gelu(gate, approximate=True) * upward).astype(jnp.bfloat16)
         hidden = lax.optimization_barrier(hidden)
-        down_share = scatter_over_tok(
-            jnp.dot(hidden, w_down, preferred_element_type=jnp.float32), tok_count, 2
-        )
-    return (mixed_share + rms_scale(down_share.astype(jnp.float32), ffn_out_gain)).astype(
-        jnp.bfloat16
-    )
+        return scatter_over_tok(
+            jnp.dot(hidden, w_down, preferred_element_type=jnp.float32),
+            mixed_share,
+            ffn_out_gain,
+            tok_count,
+            2,
+        )
 
 
 def solution(mesh):

time: 144 us -> 146 us (1.014)
  matrix products: 17.4 us -> 19.9 us
    dot_general x1, matrix products: 5.7 us -> 8.12 us  [local(): jnp.dot(hidden, w_down, preferred_element_type=jnp.float32)]
  transfers between devices with their start and end apart: 2 -> 2, of which waited for: 1 -> 1; matrix products, arithmetic and copies ran while one was open for 4% -> 4% of each run, Pallas kernels for 38% -> 37%
where the time goes in v19:
time: 146 us
  Pallas kernels  97.5 us (67%)
  matrix products  19.9 us (14%)
  between operations  14.4 us (10%)
  local copies, waits for them, and re-layouts  7.04 us (5%)
  other arithmetic  6.32 us (4%)
    pallas_call x1, Pallas kernels, gather_over_tok(): pl.pallas_call(lambda *refs: gather_tok_kernel(tok_count, *refs), out_sha...  53.9 us
    pallas_call x1, Pallas kernels, project_over_tok(): pl.pallas_call(lambda *refs: project_tok_kernel(tok_count, *refs), out_sh...  22 us
    pallas_call x1, Pallas kernels, scatter_over_tok(): pl.pallas_call(lambda *refs: scatter_tok_kernel(tok_count, *refs), out_sh...  21.7 us
    dot_general x1, matrix products, local(): jnp.dot(hidden, w_down, preferred_element_type=jnp.float32)  8.12 us
    dot_general x1, matrix products, local(): upward = jnp.dot(normed, w_up, preferred_element_type=jnp.float32)  3.85 us
    dot_general x1, matrix products, local(): gate = jnp.dot(normed, w_gate, preferred_element_type=jnp.float32)  3.54 us
  transfers between devices with their start and end apart: 2, of which 1 were waited for; matrix products, arithmetic and copies ran while one was open for 4% of the time, Pallas kernels for 37%

profile of v19, /device:TPU:1, one launch (start us, length us, event | category | flops | bytes accessed | tf_op | source)
XLA Modules:
  0.0 146.0 jit_solution(8263989235382160250)
XLA Ops:
  6.5 1.0 fusion.43
  7.5 0.7 pad_maximum_fusion.1
  8.2 0.0 all-gather.3.cloned.1.call-update
  8.3 1.3 dynamic_slice.20
  10.2 0.0 copy-start.7
  10.2 53.9 %prefix_gather.1.refs_1_ = bf16[8,256,2560]{2,1,0:T(8,128)(2,1)} custom-call(bf16[256,2560]{1,0:T(8,128)(2,1)} %refs_0_.1), custom_call_target="tpu_custom_call" | custom-call | bytes 20971520 | tf_op jit(solution)/shard_map/prefix_gather/pallas_call | solution.py:97
  64.1 0.0 copy-start.8
  64.2 0.1 dynamic_slice.21
  64.3 0.1 all-gather.3.cloned.1.call-done
  64.4 2.9 %gather_fusion = bf16[8,256,512]{2,1,0:T(8,128)(2,1)S(1)} fusion(bf16[16,256,512]{2,1,0:T(8,128)(2,1)} %bitcast.14, s32[1024]{0:T(1024)S(1)} %pad_clamp_fusion), kind=kCustom, calls=%fused_computation | custom fusion | bytes 4194336 | tf_op jit(solution)/shard_map/prefix_gather/jit(_take)/gather | solution.py:430
  67.3 0.7 collective-permute-start
  68.1 0.2 reduce-window.8
  68.3 1.1 fusion.35
  69.4 0.1 convert_reduce_fusion
  69.5 1.0 constant_dynamic-slice_fusion
  70.5 0.1 fusion.32
  70.7 1.1 fusion.37
  71.8 0.2 fusion.21
  72.0 1.4 fusion.20
  73.4 1.6 %fusion.44 = (f32[512]{0:T(512)S(1)}, f32[512,4608]{1,0:T(8,128)S(1)}) fusion(bf16[512,256]{1,0:T(8,128)(2,1)S(1)} %fusion.37, bf16[4096,256]{1,0:T(8,128)(2,1)S(1)} %fusion.20, bf16[512,256]{1,0:T(8,128)(2,1)S(1)} %copy-done.1, f32[256]{0:T(256)S(1)} %copy-done.6, f32[512]{0:T(512)S(1)} %add_rsqrt_fusion.1, pred[512,512]{1,0:T(32,128)(4,1)S(1)} %fusion.21), kind=kOutput, calls=%fused_computation.53 | convolution fusion | flops 1220279808 | bytes 12325888 | tf_op jit(solution)/shard_map/attention/dot_general | solution.py:453
  74.9 1.4 fusion
  76.3 0.0 slice-start
  76.4 2.8 %fusion.27.refs_0_ = bf16[512,256]{1,0:T(8,128)(2,1)S(1)} fusion(bf16[2048,512]{1,0:T(8,128)(2,1)} %collective-permute-done, bf16[2048,512]{1,0:T(8,128)(2,1)S(1)} %bitcast.13, bf16[512,256]{1,0:T(8,128)(2,1)S(1)} %constant_dynamic-slice_fusion, f32[512,4608]{1,0:T(8,128)S(1)} %get-tuple-element.16, f32[512]{0:T(512)S(1)} %get-tuple-element.15, f32[512]{0:T(512)S(1)} %fusion), kind=kOutput, calls=%fused_computation.30 | convolution fusion | flops 1220018176 | bytes 14159872 | tf_op jit(solution)/shard_map/attention/dot_general | solution.py:458
  79.2 0.0 slice-start.1
  79.2 0.0 slice-start.2
  79.2 22.0 %out_projection.1 = (bf16[512,2560]{1,0:T(8,128)(2,1)S(1)}, f32[64,2560]{1,0:T(8,128)S(1)}) custom-call(bf16[512,256]{1,0:T(8,128)(2,1)S(1)} %fusion.27.refs_0_, bf16[8,256,2560]{2,1,0:T(8,128)(2,1)} %prefix_gather.1.refs_1_, bf16[512,2560]{1,0:T(8,128)(2,1)S(1)} %copy-done, f32[1,2560]{1,0:T(1,128)S(1)} %reshape.91.refs_3_, f32[1,2560]{1,0:T(1,128)S(1)} %reshape.92.refs_4_), custom_call_target="tpu_custom_call" | custom-call | flops 5368709120 | bytes 15728640 | tf_op jit(solution)/shard_map/out_projection/pallas_call | solution.py:246
  101.2 0.0 slice-start.3
  101.3 3.5 %fusion.45 = f32[512,1280]{1,0:T(8,128)S(1)} fusion(bf16[512,2560]{1,0:T(8,128)(2,1)S(1)} %get-tuple-element.11, bf16[2560,1280]{1,0:T(8,128)(2,1)S(1)} %bitcast.17), kind=kOutput, calls=%fused_computation.54 | convolution fusion | flops 3355443200 | bytes 11796480 | tf_op jit(solution)/shard_map/feed_forward/dot_general | solution.py:472
  104.8 3.8 %fusion.5 = bf16[512,1280]{1,0:T(8,128)(2,1)S(1)} fusion(bf16[512,2560]{1,0:T(8,128)(2,1)S(1)} %get-tuple-element.11, bf16[2560,1280]{1,0:T(8,128)(2,1)S(1)} %bitcast.19, f32[512,1280]{1,0:T(8,128)S(1)} %fusion.45), kind=kOutput, calls=%fused_computation.11 | convolution fusion | flops 3361996800 | bytes 13107200 | tf_op jit(solution)/shard_map/feed_forward/dot_general | solution.py:473
  108.7 8.1 %fusion.46.refs_0_ = f32[512,2560]{1,0:T(8,128)} fusion(bf16[512,1280]{1,0:T(8,128)(2,1)S(1)} %fusion.5, bf16[1280,2560]{1,0:T(8,128)(2,1)} %param.31), kind=kOutput, calls=%fused_computation.55 | convolution fusion | flops 3355443200 | bytes 13107200 | tf_op jit(solution)/shard_map/feed_forward/dot_general | solution.py:477
  116.8 21.7 %feed_forward.1 = bf16[64,2560]{1,0:T(8,128)(2,1)S(1)} custom-call(f32[512,2560]{1,0:T(8,128)} %fusion.46.refs_0_, f32[64,2560]{1,0:T(8,128)S(1)} %get-tuple-element.12.refs_1_, f32[1,2560]{1,0:T(1,128)S(1)} %reshape.93.refs_2_), custom_call_target="tpu_custom_call" | custom-call | flops 1310720 | bytes 10485760 | tf_op jit(solution)/shard_map/feed_forward/pallas_call | solution.py:360
  138.5 0.7 copy.20
  (30 shorter events, 0.1 us)
Async XLA Ops:
  6.5 57.9 %all-gather.3.cloned.1.call-start = ((), (), s32[]{:S(2)}) async-start(), calls=%async_computation | async-start | bytes 4456448 | tf_op jit(solution)/shard_map/prefix_gather/all_gather | solution.py:425
  10.2 54.0 %copy-start.7 = (s32[16]{0:T(128)S(1)}, s32[16]{0:T(128)}, u32[]{:S(2)}) copy-start(s32[16]{0:T(128)} %param.23) | copy-start | bytes 196
  64.1 3.9 %copy-start.8 = (s32[1,3]{1,0:T(1,128)S(1)}, s32[1,3]{1,0:T(1,128)}, u32[]{:S(2)}) copy-start(s32[1,3]{1,0:T(1,128)} %param.21) | copy-start | bytes 40
  64.1 4.1 %copy-start.2 = (f32[2560]{0:T(1024)S(1)}, f32[2560]{0:T(1024)}, u32[]{:S(2)}) copy-start(f32[2560]{0:T(1024)} %param.26) | copy-start | bytes 30724
  64.1 4.1 %copy-start.3 = (f32[2560]{0:T(1024)S(1)}, f32[2560]{0:T(1024)}, u32[]{:S(2)}) copy-start(f32[2560]{0:T(1024)} %param.27) | copy-start | bytes 30724
  64.2 4.1 %copy-start.4 = (f32[2560]{0:T(1024)S(1)}, f32[2560]{0:T(1024)}, u32[]{:S(2)}) copy-start(f32[2560]{0:T(1024)} %param.28) | copy-start | bytes 30724
  64.2 6.3 %copy-start.1 = (bf16[512,256]{1,0:T(8,128)(2,1)S(1)}, bf16[512,256]{1,0:T(8,128)(2,1)}, u32[]{:S(2)}) copy-start(bf16[512,256]{1,0:T(8,128)(2,1)} %param.16) | copy-start | bytes 786436
  64.4 6.2 %copy-start.5 = (f32[256]{0:T(256)S(1)}, f32[256]{0:T(256)}, u32[]{:S(2)}) copy-start(f32[256]{0:T(256)} %param.20) | copy-start | bytes 3076
  67.3 4.7 %collective-permute-start = (bf16[2048,512]{1,0:T(8,128)(2,1)S(1)}, bf16[2048,512]{1,0:T(8,128)(2,1)}, u32[]{:S(2)}, u32[]{:S(2)}) collective-permute-start(bf16[2048,512]{1,0:T(8,128)(2,1)S(1)} %bitcast.11), channel_id=1, source_target_pairs={{0,1},{1,0},{2,3},{3,2},{4,5},{5,4},{6,7},{7,6},{8,9},{9,8},{10,11... | collective-permute-start | bytes 6291464 | tf_op jit(solution)/shard_map/prefix_gather/ppermute | solution.py:432
  72.0 1.4 copy-start.6
  76.3 2.9 %copy-start = (bf16[512,2560]{1,0:T(8,128)(2,1)S(1)}, bf16[512,2560]{1,0:T(8,128)(2,1)}, u32[]{:S(2)}) copy-start(bf16[512,2560]{1,0:T(8,128)(2,1)} %refs_2_.1) | copy-start | bytes 7864324
  76.3 24.9 %slice-start = ((s8[6553600]{0:T(1024)(128)(4,1)}), s8[4194304]{0:T(1024)(128)(4,1)S(1)}, s32[]{:S(2)}) async-start(s8[6553600]{0:T(1024)(128)(4,1)} %bitcast.16), calls=%async_computation.1 | async-start | bytes 8388608
  79.2 22.0 %slice-start.1 = ((s8[6553600]{0:T(1024)(128)(4,1)}), s8[2359296]{0:T(1024)(128)(4,1)S(1)}, s32[]{:S(2)}) async-start(s8[6553600]{0:T(1024)(128)(4,1)} %bitcast.16), calls=%async_computation.2 | async-start | bytes 4718592
  79.2 25.6 %slice-start.2 = ((s8[6553600]{0:T(1024)(128)(4,1)}), s8[2359296]{0:T(1024)(128)(4,1)S(1)}, s32[]{:S(2)}) async-start(s8[6553600]{0:T(1024)(128)(4,1)} %bitcast.18), calls=%async_computation.3 | async-start | bytes 4718592
  101.2 3.6 %slice-start.3 = ((s8[6553600]{0:T(1024)(128)(4,1)}), s8[4194304]{0:T(1024)(128)(4,1)S(1)}, s32[]{:S(2)}) async-start(s8[6553600]{0:T(1024)(128)(4,1)} %bitcast.18), calls=%async_computation.4 | async-start | bytes 8388608
Sparse Core Ops, SparseCore 0:
  9.5 54.8 all-gather.2

commit v20 on v18

--- a/solution.py
+++ b/solution.py
@@ -410,7 +410,7 @@
         gathered = lax.all_gather(my_half, "req", axis=0, tiled=False)
         w_out_all = gather_over_tok(w_out, tok_count, 0)
         gathered, w_out_all = lax.optimization_barrier((gathered, w_out_all))
-        own_group = group_of[req_index]
+        own_group = jnp.sum(jnp.where(jnp.arange(req_count) == req_index, group_of, 0))
         owner_ids = lax.dynamic_slice_in_dim(owner_order, own_group * own_count, own_count)
         picked = jnp.take(gathered, owner_ids, axis=0, mode="clip").reshape(-1, 2 * HD)
         partner = [(t, t ^ 1) for t in range(tok_count)]

time: 144 us -> 144 us (level)
  transfers between devices with their start and end apart: 2 -> 2, of which waited for: 1 -> 1; matrix products, arithmetic and copies ran while one was open for 4% -> 3% of each run, Pallas kernels for 38% -> 38%
where the time goes in v20:
time: 144 us
  Pallas kernels  97.2 us (68%)
  matrix products  17.5 us (12%)
  between operations  14.4 us (10%)
  other arithmetic  7.99 us (6%)
  local copies, waits for them, and re-layouts  5.02 us (3%)
    pallas_call x1, Pallas kernels, gather_over_tok(): pl.pallas_call(lambda *refs: gather_tok_kernel(tok_count, *refs), out_sha...  53.9 us
    pallas_call x1, Pallas kernels, project_over_tok(): pl.pallas_call(lambda *refs: project_tok_kernel(tok_count, *refs), out_sh...  22 us
    pallas_call x1, Pallas kernels, scatter_over_tok(): pl.pallas_call(lambda *refs: scatter_tok_kernel(tok_count, *refs), out_sh...  21.3 us
    dot_general x1, matrix products, local(): jnp.dot(hidden, w_down, preferred_element_type=jnp.float32)  5.7 us
    dot_general x1, matrix products, local(): upward = jnp.dot(normed, w_up, preferred_element_type=jnp.float32)  3.84 us
    dot_general x1, matrix products, local(): gate = jnp.dot(normed, w_gate, preferred_element_type=jnp.float32)  3.54 us
    gather x1, local copies, waits for them, and re-layouts, local(): jnp.take(gathered, owner_ids, axis=0, mode='clip').reshape(-1, 2 * HD)  2.88 us
  transfers between devices with their start and end apart: 2, of which 1 were waited for; matrix products, arithmetic and copies ran while one was open for 3% of the time, Pallas kernels for 38%

profile of v20, /device:TPU:1, one launch (start us, length us, event | category | flops | bytes accessed | tf_op | source)
XLA Modules:
  0.0 143.6 jit_solution(8106419448971992535)
XLA Ops:
  6.5 1.0 fusion.44
  7.5 0.7 pad_maximum_fusion.1
  8.2 0.0 all-gather.3.cloned.1.call-update
  8.3 53.9 %prefix_gather.1.refs_1_ = bf16[8,256,2560]{2,1,0:T(8,128)(2,1)} custom-call(bf16[256,2560]{1,0:T(8,128)(2,1)} %refs_0_.1), custom_call_target="tpu_custom_call" | custom-call | bytes 20971520 | tf_op jit(solution)/shard_map/prefix_gather/pallas_call | solution.py:97
  62.3 0.6 fusion.41
  63.5 0.1 dynamic_slice.17
  63.6 0.8 all-gather.3.cloned.1.call-done
  64.4 2.9 %gather_fusion = bf16[8,256,512]{2,1,0:T(8,128)(2,1)S(1)} fusion(bf16[16,256,512]{2,1,0:T(8,128)(2,1)} %bitcast.13, s32[1024]{0:T(1024)S(1)} %pad_clamp_fusion), kind=kCustom, calls=%fused_computation | custom fusion | bytes 4194336 | tf_op jit(solution)/shard_map/prefix_gather/jit(_take)/gather | solution.py:415
  67.3 0.8 collective-permute-start
  68.1 0.2 reduce-window.8
  68.3 1.1 fusion.35
  69.4 0.1 convert_reduce_fusion
  69.5 1.0 constant_dynamic-slice_fusion
  70.4 0.1 fusion.32
  70.6 1.1 fusion.37
  71.7 0.2 fusion.21
  72.0 0.0 collective-permute-done
  72.0 1.4 fusion.20
  73.3 1.6 %fusion.45 = (f32[512]{0:T(512)S(1)}, f32[512,4608]{1,0:T(8,128)S(1)}) fusion(bf16[512,256]{1,0:T(8,128)(2,1)S(1)} %fusion.37, bf16[4096,256]{1,0:T(8,128)(2,1)S(1)} %fusion.20, bf16[512,256]{1,0:T(8,128)(2,1)S(1)} %copy-done.1, f32[256]{0:T(256)S(1)} %copy-done.6, f32[512]{0:T(512)S(1)} %add_rsqrt_fusion.1, pred[512,512]{1,0:T(32,128)(4,1)S(1)} %fusion.21), kind=kOutput, calls=%fused_computation.58 | convolution fusion | flops 1220279808 | bytes 12325888 | tf_op jit(solution)/shard_map/attention/dot_general | solution.py:438
  74.9 1.4 fusion
  76.3 0.0 slice-start
  76.3 2.8 %fusion.27.refs_0_ = bf16[512,256]{1,0:T(8,128)(2,1)S(1)} fusion(bf16[2048,512]{1,0:T(8,128)(2,1)} %collective-permute-done, bf16[2048,512]{1,0:T(8,128)(2,1)S(1)} %bitcast.12, bf16[512,256]{1,0:T(8,128)(2,1)S(1)} %constant_dynamic-slice_fusion, f32[512,4608]{1,0:T(8,128)S(1)} %get-tuple-element.16, f32[512]{0:T(512)S(1)} %get-tuple-element.15, f32[512]{0:T(512)S(1)} %fusion), kind=kOutput, calls=%fused_computation.30 | convolution fusion | flops 1220018176 | bytes 14159872 | tf_op jit(solution)/shard_map/attention/dot_general | solution.py:443
  79.2 0.0 slice-start.1
  79.2 0.0 slice-start.2
  79.2 22.0 %out_projection.1 = (bf16[512,2560]{1,0:T(8,128)(2,1)S(1)}, f32[64,2560]{1,0:T(8,128)S(1)}) custom-call(bf16[512,256]{1,0:T(8,128)(2,1)S(1)} %fusion.27.refs_0_, bf16[8,256,2560]{2,1,0:T(8,128)(2,1)} %prefix_gather.1.refs_1_, bf16[512,2560]{1,0:T(8,128)(2,1)S(1)} %copy-done, f32[1,2560]{1,0:T(1,128)S(1)} %reshape.95.refs_3_, f32[1,2560]{1,0:T(1,128)S(1)} %reshape.96.refs_4_), custom_call_target="tpu_custom_call" | custom-call | flops 5368709120 | bytes 15728640 | tf_op jit(solution)/shard_map/out_projection/pallas_call | solution.py:246
  101.2 0.0 slice-start.3
  101.2 3.5 %fusion.46 = f32[512,1280]{1,0:T(8,128)S(1)} fusion(bf16[512,2560]{1,0:T(8,128)(2,1)S(1)} %get-tuple-element.12, bf16[2560,1280]{1,0:T(8,128)(2,1)S(1)} %bitcast.16), kind=kOutput, calls=%fused_computation.59 | convolution fusion | flops 3355443200 | bytes 11796480 | tf_op jit(solution)/shard_map/feed_forward/dot_general | solution.py:457
  104.8 3.8 %fusion.5 = bf16[512,1280]{1,0:T(8,128)(2,1)S(1)} fusion(bf16[512,2560]{1,0:T(8,128)(2,1)S(1)} %get-tuple-element.12, bf16[2560,1280]{1,0:T(8,128)(2,1)S(1)} %bitcast.18, f32[512,1280]{1,0:T(8,128)S(1)} %fusion.46), kind=kOutput, calls=%fused_computation.11 | convolution fusion | flops 3361996800 | bytes 13107200 | tf_op jit(solution)/shard_map/feed_forward/dot_general | solution.py:458
  108.7 5.7 %fusion.47.refs_0_ = f32[512,2560]{1,0:T(8,128)S(1)} fusion(bf16[512,1280]{1,0:T(8,128)(2,1)S(1)} %fusion.5, bf16[1280,2560]{1,0:T(8,128)(2,1)} %param.31), kind=kOutput, calls=%fused_computation.60 | convolution fusion | flops 3355443200 | bytes 13107200 | tf_op jit(solution)/shard_map/feed_forward/dot_general | solution.py:462
  114.4 21.3 %feed_forward.1 = f32[64,2560]{1,0:T(8,128)S(1)} custom-call(f32[512,2560]{1,0:T(8,128)S(1)} %fusion.47.refs_0_), custom_call_target="tpu_custom_call" | custom-call | flops 1310720 | bytes 10485760 | tf_op jit(solution)/shard_map/feed_forward/pallas_call | solution.py:349
  135.7 0.1 multiply_reduce_fusion
  135.9 0.9 add_convert_fusion
  (33 shorter events, 0.1 us)
Async XLA Ops:
  6.5 57.9 %all-gather.3.cloned.1.call-start = ((), (), s32[]{:S(2)}) async-start(), calls=%async_computation | async-start | bytes 4456448 | tf_op jit(solution)/shard_map/prefix_gather/all_gather | solution.py:410
  8.3 54.0 %copy-start.7 = (s32[16]{0:T(128)S(1)}, s32[16]{0:T(128)}, u32[]{:S(2)}) copy-start(s32[16]{0:T(128)} %param.22) | copy-start | bytes 196
  8.3 55.2 %copy-start.8 = (s32[16]{0:T(128)S(1)}, s32[16]{0:T(128)}, u32[]{:S(2)}) copy-start(s32[16]{0:T(128)} %param.23) | copy-start | bytes 196
  62.2 5.9 %copy-start.9 = (s32[1,3]{1,0:T(1,128)S(1)}, s32[1,3]{1,0:T(1,128)}, u32[]{:S(2)}) copy-start(s32[1,3]{1,0:T(1,128)} %param.21) | copy-start | bytes 40
  62.2 6.0 %copy-start.3 = (f32[2560]{0:T(1024)S(1)}, f32[2560]{0:T(1024)}, u32[]{:S(2)}) copy-start(f32[2560]{0:T(1024)} %param.26) | copy-start | bytes 30724
  62.2 6.0 %copy-start.4 = (f32[2560]{0:T(1024)S(1)}, f32[2560]{0:T(1024)}, u32[]{:S(2)}) copy-start(f32[2560]{0:T(1024)} %param.27) | copy-start | bytes 30724
  62.2 8.2 %copy-start.1 = (bf16[512,256]{1,0:T(8,128)(2,1)S(1)}, bf16[512,256]{1,0:T(8,128)(2,1)}, u32[]{:S(2)}) copy-start(bf16[512,256]{1,0:T(8,128)(2,1)} %param.16) | copy-start | bytes 786436
  64.4 6.2 %copy-start.5 = (f32[256]{0:T(256)S(1)}, f32[256]{0:T(256)}, u32[]{:S(2)}) copy-start(f32[256]{0:T(256)} %param.20) | copy-start | bytes 3076
  67.3 4.7 %collective-permute-start = (bf16[2048,512]{1,0:T(8,128)(2,1)S(1)}, bf16[2048,512]{1,0:T(8,128)(2,1)}, u32[]{:S(2)}, u32[]{:S(2)}) collective-permute-start(bf16[2048,512]{1,0:T(8,128)(2,1)S(1)} %bitcast.10), channel_id=1, source_target_pairs={{0,1},{1,0},{2,3},{3,2},{4,5},{5,4},{6,7},{7,6},{8,9},{9,8},{10,11... | collective-permute-start | bytes 6291464 | tf_op jit(solution)/shard_map/prefix_gather/ppermute | solution.py:417
  71.9 1.4 copy-start.6
  76.3 2.8 %copy-start = (bf16[512,2560]{1,0:T(8,128)(2,1)S(1)}, bf16[512,2560]{1,0:T(8,128)(2,1)}, u32[]{:S(2)}) copy-start(bf16[512,2560]{1,0:T(8,128)(2,1)} %refs_2_.1) | copy-start | bytes 7864324
  76.3 24.9 %slice-start = ((s8[6553600]{0:T(1024)(128)(4,1)}), s8[4194304]{0:T(1024)(128)(4,1)S(1)}, s32[]{:S(2)}) async-start(s8[6553600]{0:T(1024)(128)(4,1)} %bitcast.15), calls=%async_computation.1 | async-start | bytes 8388608
  79.2 22.0 %slice-start.1 = ((s8[6553600]{0:T(1024)(128)(4,1)}), s8[2359296]{0:T(1024)(128)(4,1)S(1)}, s32[]{:S(2)}) async-start(s8[6553600]{0:T(1024)(128)(4,1)} %bitcast.15), calls=%async_computation.2 | async-start | bytes 4718592
  79.2 25.6 %slice-start.2 = ((s8[6553600]{0:T(1024)(128)(4,1)}), s8[2359296]{0:T(1024)(128)(4,1)S(1)}, s32[]{:S(2)}) async-start(s8[6553600]{0:T(1024)(128)(4,1)} %bitcast.17), calls=%async_computation.3 | async-start | bytes 4718592
  101.2 3.6 %slice-start.3 = ((s8[6553600]{0:T(1024)(128)(4,1)}), s8[4194304]{0:T(1024)(128)(4,1)S(1)}, s32[]{:S(2)}) async-start(s8[6553600]{0:T(1024)(128)(4,1)} %bitcast.17), calls=%async_computation.4 | async-start | bytes 8388608
  114.4 21.5 %copy-start.2 = (f32[2560]{0:T(1024)S(1)}, f32[2560]{0:T(1024)}, u32[]{:S(2)}) copy-start(f32[2560]{0:T(1024)} %param.28) | copy-start | bytes 30724
Sparse Core Ops, SparseCore 0:
  9.5 54.8 all-gather.2

commit v21 on v18

--- a/solution.py
+++ b/solution.py
@@ -138,10 +138,6 @@
     tile = 512
     tiles = cols // tile
 
-    barrier = pltpu.get_barrier_semaphore()
-    for peer in (up, down, partner):
-        pl.semaphore_signal(barrier, inc=1, device_id={"tok": peer}, device_id_type=mesh_ids)
-    pl.semaphore_wait(barrier, 3)
 
     def remote(src, dst, slot, peer):
         return pltpu.make_async_remote_copy(
@@ -181,6 +177,10 @@
         pl.loop(0, tiles)(one_tile)
 
     load(0).start()
+    barrier = pltpu.get_barrier_semaphore()
+    for peer in (up, down, partner):
+        pl.semaphore_signal(barrier, inc=1, device_id={"tok": peer}, device_id_type=mesh_ids)
+    pl.semaphore_wait(barrier, 3)
     sends = []
 
     def send(src, slot, index, peer):
@@ -281,10 +281,6 @@
     partner = me + 1 - 2 * lax.rem(me, 2)
     share = out_ref.shape[0]
 
-    barrier = pltpu.get_barrier_semaphore()
-    for peer in (up, down, far, partner):
-        pl.semaphore_signal(barrier, inc=1, device_id={"tok": peer}, device_id_type=mesh_ids)
-    pl.semaphore_wait(barrier, 4)
 
     def remote(src, dst, slot, peer):
         return pltpu.make_async_remote_copy(
@@ -308,18 +304,22 @@
         return pl.ds(pl.multiple_of(block * share, share), share)
 
     order = (3, 1, 2, 0)
+    own = family(me)
+    loads = []
+    for idx in order:
+        load = pltpu.make_async_copy(part_hbm.at[rows_of(own[idx])], mine.at[idx], load_sem.at[idx])
+        load.start()
+        loads.append(load)
+    barrier = pltpu.get_barrier_semaphore()
+    for peer in (up, down, far, partner):
+        pl.semaphore_signal(barrier, inc=1, device_id={"tok": peer}, device_id_type=mesh_ids)
+    pl.semaphore_wait(barrier, 4)
     sends = []
     theirs = family(partner)
     for idx in order:
         copy = remote(part_hbm.at[rows_of(theirs[idx])], chip_in.at[idx], idx, partner)
         copy.start()
         sends.append(copy)
-    own = family(me)
-    loads = []
-    for idx in order:
-        load = pltpu.make_async_copy(part_hbm.at[rows_of(own[idx])], mine.at[idx], load_sem.at[idx])
-        load.start()
-        loads.append(load)
     targets = {1: (up, 1), 2: (down, 0), 3: (far, 2)}
     for pos, idx in enumerate(order[:3]):
         loads[pos].wait()

time: 144 us -> 145 us (level)
  transfers between devices with their start and end apart: 2 -> 2, of which waited for: 1 -> 1; matrix products, arithmetic and copies ran while one was open for 4% -> 4% of each run, Pallas kernels for 38% -> 37%
where the time goes in v21:
time: 145 us; the launch traced here: 144 us
  Pallas kernels  98 us (68%)
  matrix products  17.4 us (12%)
  between operations  14.4 us (10%)
  other arithmetic  7.35 us (5%)
  local copies, waits for them, and re-layouts  6.33 us (4%)
    pallas_call x1, Pallas kernels, gather_over_tok(): pl.pallas_call(lambda *refs: gather_tok_kernel(tok_count, *refs), out_sha...  53.9 us
    pallas_call x1, Pallas kernels, scatter_over_tok(): pl.pallas_call(lambda *refs: scatter_tok_kernel(tok_count, *refs), out_sh...  22.1 us
    pallas_call x1, Pallas kernels, project_over_tok(): pl.pallas_call(lambda *refs: project_tok_kernel(tok_count, *refs), out_sh...  22 us
    dot_general x1, matrix products, local(): jnp.dot(hidden, w_down, preferred_element_type=jnp.float32)  5.7 us
    dot_general x1, matrix products, local(): upward = jnp.dot(normed, w_up, preferred_element_type=jnp.float32)  3.84 us
    dot_general x1, matrix products, local(): gate = jnp.dot(normed, w_gate, preferred_element_type=jnp.float32)  3.54 us
  transfers between devices with their start and end apart: 2, of which 1 were waited for; matrix products, arithmetic and copies ran while one was open for 4% of the time, Pallas kernels for 37%

profile of v21, /device:TPU:1, one launch (start us, length us, event | category | flops | bytes accessed | tf_op | source)
XLA Modules:
  0.0 144.4 jit_solution(15880077252729996174)
XLA Ops:
  6.5 1.0 fusion.43
  7.5 0.7 pad_maximum_fusion.1
  8.2 0.0 all-gather.3.cloned.1.call-update
  8.3 1.3 dynamic_slice.20
  10.3 53.9 %prefix_gather.1.refs_1_ = bf16[8,256,2560]{2,1,0:T(8,128)(2,1)} custom-call(bf16[256,2560]{1,0:T(8,128)(2,1)} %refs_0_.1), custom_call_target="tpu_custom_call" | custom-call | bytes 20971520 | tf_op jit(solution)/shard_map/prefix_gather/pallas_call | solution.py:97
  64.3 0.1 dynamic_slice.21
  64.4 0.1 all-gather.3.cloned.1.call-done
  64.4 2.9 %gather_fusion = bf16[8,256,512]{2,1,0:T(8,128)(2,1)S(1)} fusion(bf16[16,256,512]{2,1,0:T(8,128)(2,1)} %bitcast.14, s32[1024]{0:T(1024)S(1)} %pad_clamp_fusion), kind=kCustom, calls=%fused_computation | custom fusion | bytes 4194336 | tf_op jit(solution)/shard_map/prefix_gather/jit(_take)/gather | solution.py:415
  67.3 0.8 collective-permute-start
  68.1 0.2 reduce-window.8
  68.3 1.1 fusion.35
  69.4 0.1 convert_reduce_fusion
  69.5 1.0 constant_dynamic-slice_fusion
  70.4 0.1 fusion.32
  70.6 1.1 fusion.37
  71.7 0.2 fusion.21
  72.0 0.0 collective-permute-done
  72.0 1.4 fusion.20
  73.3 1.6 %fusion.44 = (f32[512]{0:T(512)S(1)}, f32[512,4608]{1,0:T(8,128)S(1)}) fusion(bf16[512,256]{1,0:T(8,128)(2,1)S(1)} %fusion.37, bf16[4096,256]{1,0:T(8,128)(2,1)S(1)} %fusion.20, bf16[512,256]{1,0:T(8,128)(2,1)S(1)} %copy-done.1, f32[256]{0:T(256)S(1)} %copy-done.6, f32[512]{0:T(512)S(1)} %add_rsqrt_fusion.1, pred[512,512]{1,0:T(32,128)(4,1)S(1)} %fusion.21), kind=kOutput, calls=%fused_computation.56 | convolution fusion | flops 1220279808 | bytes 12325888 | tf_op jit(solution)/shard_map/attention/dot_general | solution.py:438
  74.9 1.4 fusion
  76.3 0.0 slice-start
  76.3 2.8 %fusion.27.refs_0_ = bf16[512,256]{1,0:T(8,128)(2,1)S(1)} fusion(bf16[2048,512]{1,0:T(8,128)(2,1)} %collective-permute-done, bf16[2048,512]{1,0:T(8,128)(2,1)S(1)} %bitcast.13, bf16[512,256]{1,0:T(8,128)(2,1)S(1)} %constant_dynamic-slice_fusion, f32[512,4608]{1,0:T(8,128)S(1)} %get-tuple-element.16, f32[512]{0:T(512)S(1)} %get-tuple-element.15, f32[512]{0:T(512)S(1)} %fusion), kind=kOutput, calls=%fused_computation.30 | convolution fusion | flops 1220018176 | bytes 14159872 | tf_op jit(solution)/shard_map/attention/dot_general | solution.py:443
  79.2 0.0 slice-start.1
  79.2 0.0 slice-start.2
  79.2 22.0 %out_projection.1 = (bf16[512,2560]{1,0:T(8,128)(2,1)S(1)}, f32[64,2560]{1,0:T(8,128)S(1)}) custom-call(bf16[512,256]{1,0:T(8,128)(2,1)S(1)} %fusion.27.refs_0_, bf16[8,256,2560]{2,1,0:T(8,128)(2,1)} %prefix_gather.1.refs_1_, bf16[512,2560]{1,0:T(8,128)(2,1)S(1)} %copy-done, f32[1,2560]{1,0:T(1,128)S(1)} %reshape.97.refs_3_, f32[1,2560]{1,0:T(1,128)S(1)} %reshape.98.refs_4_), custom_call_target="tpu_custom_call" | custom-call | flops 5368709120 | bytes 15728640 | tf_op jit(solution)/shard_map/out_projection/pallas_call | solution.py:246
  101.2 0.0 slice-start.3
  101.3 3.5 %fusion.45 = f32[512,1280]{1,0:T(8,128)S(1)} fusion(bf16[512,2560]{1,0:T(8,128)(2,1)S(1)} %get-tuple-element.12, bf16[2560,1280]{1,0:T(8,128)(2,1)S(1)} %bitcast.17), kind=kOutput, calls=%fused_computation.57 | convolution fusion | flops 3355443200 | bytes 11796480 | tf_op jit(solution)/shard_map/feed_forward/dot_general | solution.py:457
  104.8 3.8 %fusion.5 = bf16[512,1280]{1,0:T(8,128)(2,1)S(1)} fusion(bf16[512,2560]{1,0:T(8,128)(2,1)S(1)} %get-tuple-element.12, bf16[2560,1280]{1,0:T(8,128)(2,1)S(1)} %bitcast.19, f32[512,1280]{1,0:T(8,128)S(1)} %fusion.45), kind=kOutput, calls=%fused_computation.11 | convolution fusion | flops 3361996800 | bytes 13107200 | tf_op jit(solution)/shard_map/feed_forward/dot_general | solution.py:458
  108.7 5.7 %fusion.46.refs_0_ = f32[512,2560]{1,0:T(8,128)S(1)} fusion(bf16[512,1280]{1,0:T(8,128)(2,1)S(1)} %fusion.5, bf16[1280,2560]{1,0:T(8,128)(2,1)} %param.31), kind=kOutput, calls=%fused_computation.58 | convolution fusion | flops 3355443200 | bytes 13107200 | tf_op jit(solution)/shard_map/feed_forward/dot_general | solution.py:462
  114.4 22.1 %feed_forward.1 = f32[64,2560]{1,0:T(8,128)S(1)} custom-call(f32[512,2560]{1,0:T(8,128)S(1)} %fusion.46.refs_0_), custom_call_target="tpu_custom_call" | custom-call | flops 1310720 | bytes 10485760 | tf_op jit(solution)/shard_map/feed_forward/pallas_call | solution.py:349
  136.5 0.1 multiply_reduce_fusion
  136.7 0.9 add_convert_fusion
  (31 shorter events, 0.1 us)
Async XLA Ops:
  6.5 57.9 %all-gather.3.cloned.1.call-start = ((), (), s32[]{:S(2)}) async-start(), calls=%async_computation | async-start | bytes 4456448 | tf_op jit(solution)/shard_map/prefix_gather/all_gather | solution.py:410
  10.3 54.0 %copy-start.7 = (s32[16]{0:T(128)S(1)}, s32[16]{0:T(128)}, u32[]{:S(2)}) copy-start(s32[16]{0:T(128)} %param.23) | copy-start | bytes 196
  64.2 3.9 %copy-start.8 = (s32[1,3]{1,0:T(1,128)S(1)}, s32[1,3]{1,0:T(1,128)}, u32[]{:S(2)}) copy-start(s32[1,3]{1,0:T(1,128)} %param.21) | copy-start | bytes 40
  64.2 4.0 %copy-start.3 = (f32[2560]{0:T(1024)S(1)}, f32[2560]{0:T(1024)}, u32[]{:S(2)}) copy-start(f32[2560]{0:T(1024)} %param.26) | copy-start | bytes 30724
  64.2 4.0 %copy-start.4 = (f32[2560]{0:T(1024)S(1)}, f32[2560]{0:T(1024)}, u32[]{:S(2)}) copy-start(f32[2560]{0:T(1024)} %param.27) | copy-start | bytes 30724
  64.2 6.2 %copy-start.1 = (bf16[512,256]{1,0:T(8,128)(2,1)S(1)}, bf16[512,256]{1,0:T(8,128)(2,1)}, u32[]{:S(2)}) copy-start(bf16[512,256]{1,0:T(8,128)(2,1)} %param.16) | copy-start | bytes 786436
  64.4 6.2 %copy-start.5 = (f32[256]{0:T(256)S(1)}, f32[256]{0:T(256)}, u32[]{:S(2)}) copy-start(f32[256]{0:T(256)} %param.20) | copy-start | bytes 3076
  67.3 4.7 %collective-permute-start = (bf16[2048,512]{1,0:T(8,128)(2,1)S(1)}, bf16[2048,512]{1,0:T(8,128)(2,1)}, u32[]{:S(2)}, u32[]{:S(2)}) collective-permute-start(bf16[2048,512]{1,0:T(8,128)(2,1)S(1)} %bitcast.11), channel_id=1, source_target_pairs={{0,1},{1,0},{2,3},{3,2},{4,5},{5,4},{6,7},{7,6},{8,9},{9,8},{10,11... | collective-permute-start | bytes 6291464 | tf_op jit(solution)/shard_map/prefix_gather/ppermute | solution.py:417
  71.9 1.4 copy-start.6
  76.3 2.8 %copy-start = (bf16[512,2560]{1,0:T(8,128)(2,1)S(1)}, bf16[512,2560]{1,0:T(8,128)(2,1)}, u32[]{:S(2)}) copy-start(bf16[512,2560]{1,0:T(8,128)(2,1)} %refs_2_.1) | copy-start | bytes 7864324
  76.3 24.9 %slice-start = ((s8[6553600]{0:T(1024)(128)(4,1)}), s8[4194304]{0:T(1024)(128)(4,1)S(1)}, s32[]{:S(2)}) async-start(s8[6553600]{0:T(1024)(128)(4,1)} %bitcast.16), calls=%async_computation.1 | async-start | bytes 8388608
  79.2 22.1 %slice-start.1 = ((s8[6553600]{0:T(1024)(128)(4,1)}), s8[2359296]{0:T(1024)(128)(4,1)S(1)}, s32[]{:S(2)}) async-start(s8[6553600]{0:T(1024)(128)(4,1)} %bitcast.16), calls=%async_computation.2 | async-start | bytes 4718592
  79.2 25.6 %slice-start.2 = ((s8[6553600]{0:T(1024)(128)(4,1)}), s8[2359296]{0:T(1024)(128)(4,1)S(1)}, s32[]{:S(2)}) async-start(s8[6553600]{0:T(1024)(128)(4,1)} %bitcast.18), calls=%async_computation.3 | async-start | bytes 4718592
  101.2 3.6 %slice-start.3 = ((s8[6553600]{0:T(1024)(128)(4,1)}), s8[4194304]{0:T(1024)(128)(4,1)S(1)}, s32[]{:S(2)}) async-start(s8[6553600]{0:T(1024)(128)(4,1)} %bitcast.18), calls=%async_computation.4 | async-start | bytes 8388608
  114.4 22.3 %copy-start.2 = (f32[2560]{0:T(1024)S(1)}, f32[2560]{0:T(1024)}, u32[]{:S(2)}) copy-start(f32[2560]{0:T(1024)} %param.28) | copy-start | bytes 30724
Sparse Core Ops, SparseCore 0:
  9.5 54.8 all-gather.2

commit v22 on v18

--- a/solution.py
+++ b/solution.py
@@ -135,7 +135,7 @@
     partner = me + 1 - 2 * lax.rem(me, 2)
     half = att_ref.shape[0] // 2
     cols = out_ref.shape[1]
-    tile = 512
+    tile = 1280
     tiles = cols // tile
 
     barrier = pltpu.get_barrier_semaphore()

time: 144 us -> 143 us (level)
  no operation moved by 1% of the time
where the time goes in v22:
time: 143 us; the launch traced here: 142 us
  Pallas kernels  95.8 us (67%)
  matrix products  17.4 us (12%)
  between operations  14.4 us (10%)
  other arithmetic  7.35 us (5%)
  local copies, waits for them, and re-layouts  6.33 us (4%)
    pallas_call x1, Pallas kernels, gather_over_tok(): pl.pallas_call(lambda *refs: gather_tok_kernel(tok_count, *refs), out_sha...  53.9 us
    pallas_call x1, Pallas kernels, scatter_over_tok(): pl.pallas_call(lambda *refs: scatter_tok_kernel(tok_count, *refs), out_sh...  21 us
    pallas_call x1, Pallas kernels, project_over_tok(): pl.pallas_call(lambda *refs: project_tok_kernel(tok_count, *refs), out_sh...  20.9 us
    dot_general x1, matrix products, local(): jnp.dot(hidden, w_down, preferred_element_type=jnp.float32)  5.7 us
    dot_general x1, matrix products, local(): upward = jnp.dot(normed, w_up, preferred_element_type=jnp.float32)  3.84 us
    dot_general x1, matrix products, local(): gate = jnp.dot(normed, w_gate, preferred_element_type=jnp.float32)  3.54 us
    gather x1, local copies, waits for them, and re-layouts, local(): jnp.take(gathered, owner_ids, axis=0, mode='clip').reshape(-1, 2 * HD)  2.88 us
  transfers between devices with their start and end apart: 2, of which 1 were waited for; matrix products, arithmetic and copies ran while one was open for 4% of the time, Pallas kernels for 38%

profile of v22, /device:TPU:1, one launch (start us, length us, event | category | flops | bytes accessed | tf_op | source)
XLA Modules:
  0.0 142.2 jit_solution(13437990062729837028)
XLA Ops:
  6.5 1.0 fusion.43
  7.5 0.7 pad_maximum_fusion.1
  8.2 0.0 all-gather.3.cloned.1.call-update
  8.3 1.3 dynamic_slice.20
  10.3 53.9 %prefix_gather.1.refs_1_ = bf16[8,256,2560]{2,1,0:T(8,128)(2,1)} custom-call(bf16[256,2560]{1,0:T(8,128)(2,1)} %refs_0_.1), custom_call_target="tpu_custom_call" | custom-call | bytes 20971520 | tf_op jit(solution)/shard_map/prefix_gather/pallas_call | solution.py:97
  64.3 0.1 dynamic_slice.21
  64.4 0.1 all-gather.3.cloned.1.call-done
  64.4 2.9 %gather_fusion = bf16[8,256,512]{2,1,0:T(8,128)(2,1)S(1)} fusion(bf16[16,256,512]{2,1,0:T(8,128)(2,1)} %bitcast.14, s32[1024]{0:T(1024)S(1)} %pad_clamp_fusion), kind=kCustom, calls=%fused_computation | custom fusion | bytes 4194336 | tf_op jit(solution)/shard_map/prefix_gather/jit(_take)/gather | solution.py:415
  67.3 0.8 collective-permute-start
  68.1 0.2 reduce-window.8
  68.3 1.1 fusion.35
  69.4 0.1 convert_reduce_fusion
  69.5 1.0 constant_dynamic-slice_fusion
  70.4 0.1 fusion.32
  70.6 1.1 fusion.37
  71.7 0.2 fusion.21
  72.0 0.0 collective-permute-done
  72.0 1.4 fusion.20
  73.3 1.6 %fusion.44 = (f32[512]{0:T(512)S(1)}, f32[512,4608]{1,0:T(8,128)S(1)}) fusion(bf16[512,256]{1,0:T(8,128)(2,1)S(1)} %fusion.37, bf16[4096,256]{1,0:T(8,128)(2,1)S(1)} %fusion.20, bf16[512,256]{1,0:T(8,128)(2,1)S(1)} %copy-done.1, f32[256]{0:T(256)S(1)} %copy-done.6, f32[512]{0:T(512)S(1)} %add_rsqrt_fusion.1, pred[512,512]{1,0:T(32,128)(4,1)S(1)} %fusion.21), kind=kOutput, calls=%fused_computation.56 | convolution fusion | flops 1220279808 | bytes 12325888 | tf_op jit(solution)/shard_map/attention/dot_general | solution.py:438
  74.9 1.4 fusion
  76.3 0.0 slice-start
  76.3 2.8 %fusion.27.refs_0_ = bf16[512,256]{1,0:T(8,128)(2,1)S(1)} fusion(bf16[2048,512]{1,0:T(8,128)(2,1)} %collective-permute-done, bf16[2048,512]{1,0:T(8,128)(2,1)S(1)} %bitcast.13, bf16[512,256]{1,0:T(8,128)(2,1)S(1)} %constant_dynamic-slice_fusion, f32[512,4608]{1,0:T(8,128)S(1)} %get-tuple-element.16, f32[512]{0:T(512)S(1)} %get-tuple-element.15, f32[512]{0:T(512)S(1)} %fusion), kind=kOutput, calls=%fused_computation.30 | convolution fusion | flops 1220018176 | bytes 14159872 | tf_op jit(solution)/shard_map/attention/dot_general | solution.py:443
  79.2 0.0 slice-start.1
  79.2 0.0 slice-start.2
  79.2 20.9 %out_projection.1 = (bf16[512,2560]{1,0:T(8,128)(2,1)S(1)}, f32[64,2560]{1,0:T(8,128)S(1)}) custom-call(bf16[512,256]{1,0:T(8,128)(2,1)S(1)} %fusion.27.refs_0_, bf16[8,256,2560]{2,1,0:T(8,128)(2,1)} %prefix_gather.1.refs_1_, bf16[512,2560]{1,0:T(8,128)(2,1)S(1)} %copy-done, f32[1,2560]{1,0:T(1,128)S(1)} %reshape.97.refs_3_, f32[1,2560]{1,0:T(1,128)S(1)} %reshape.98.refs_4_), custom_call_target="tpu_custom_call" | custom-call | flops 5368709120 | bytes 15728640 | tf_op jit(solution)/shard_map/out_projection/pallas_call | solution.py:246
  100.1 0.0 slice-start.3
  100.2 3.5 %fusion.45 = f32[512,1280]{1,0:T(8,128)S(1)} fusion(bf16[512,2560]{1,0:T(8,128)(2,1)S(1)} %get-tuple-element.12, bf16[2560,1280]{1,0:T(8,128)(2,1)S(1)} %bitcast.17), kind=kOutput, calls=%fused_computation.57 | convolution fusion | flops 3355443200 | bytes 11796480 | tf_op jit(solution)/shard_map/feed_forward/dot_general | solution.py:457
  103.7 3.8 %fusion.5 = bf16[512,1280]{1,0:T(8,128)(2,1)S(1)} fusion(bf16[512,2560]{1,0:T(8,128)(2,1)S(1)} %get-tuple-element.12, bf16[2560,1280]{1,0:T(8,128)(2,1)S(1)} %bitcast.19, f32[512,1280]{1,0:T(8,128)S(1)} %fusion.45), kind=kOutput, calls=%fused_computation.11 | convolution fusion | flops 3361996800 | bytes 13107200 | tf_op jit(solution)/shard_map/feed_forward/dot_general | solution.py:458
  107.6 5.7 %fusion.46.refs_0_ = f32[512,2560]{1,0:T(8,128)S(1)} fusion(bf16[512,1280]{1,0:T(8,128)(2,1)S(1)} %fusion.5, bf16[1280,2560]{1,0:T(8,128)(2,1)} %param.31), kind=kOutput, calls=%fused_computation.58 | convolution fusion | flops 3355443200 | bytes 13107200 | tf_op jit(solution)/shard_map/feed_forward/dot_general | solution.py:462
  113.3 21.0 %feed_forward.1 = f32[64,2560]{1,0:T(8,128)S(1)} custom-call(f32[512,2560]{1,0:T(8,128)S(1)} %fusion.46.refs_0_), custom_call_target="tpu_custom_call" | custom-call | flops 1310720 | bytes 10485760 | tf_op jit(solution)/shard_map/feed_forward/pallas_call | solution.py:349
  134.3 0.1 multiply_reduce_fusion
  134.5 0.9 add_convert_fusion
  (31 shorter events, 0.1 us)
Async XLA Ops:
  6.5 57.9 %all-gather.3.cloned.1.call-start = ((), (), s32[]{:S(2)}) async-start(), calls=%async_computation | async-start | bytes 4456448 | tf_op jit(solution)/shard_map/prefix_gather/all_gather | solution.py:410
  10.3 54.0 %copy-start.7 = (s32[16]{0:T(128)S(1)}, s32[16]{0:T(128)}, u32[]{:S(2)}) copy-start(s32[16]{0:T(128)} %param.23) | copy-start | bytes 196
  64.2 3.9 %copy-start.8 = (s32[1,3]{1,0:T(1,128)S(1)}, s32[1,3]{1,0:T(1,128)}, u32[]{:S(2)}) copy-start(s32[1,3]{1,0:T(1,128)} %param.21) | copy-start | bytes 40
  64.2 4.0 %copy-start.3 = (f32[2560]{0:T(1024)S(1)}, f32[2560]{0:T(1024)}, u32[]{:S(2)}) copy-start(f32[2560]{0:T(1024)} %param.26) | copy-start | bytes 30724
  64.2 4.0 %copy-start.4 = (f32[2560]{0:T(1024)S(1)}, f32[2560]{0:T(1024)}, u32[]{:S(2)}) copy-start(f32[2560]{0:T(1024)} %param.27) | copy-start | bytes 30724
  64.2 6.2 %copy-start.1 = (bf16[512,256]{1,0:T(8,128)(2,1)S(1)}, bf16[512,256]{1,0:T(8,128)(2,1)}, u32[]{:S(2)}) copy-start(bf16[512,256]{1,0:T(8,128)(2,1)} %param.16) | copy-start | bytes 786436
  64.4 6.2 %copy-start.5 = (f32[256]{0:T(256)S(1)}, f32[256]{0:T(256)}, u32[]{:S(2)}) copy-start(f32[256]{0:T(256)} %param.20) | copy-start | bytes 3076
  67.3 4.7 %collective-permute-start = (bf16[2048,512]{1,0:T(8,128)(2,1)S(1)}, bf16[2048,512]{1,0:T(8,128)(2,1)}, u32[]{:S(2)}, u32[]{:S(2)}) collective-permute-start(bf16[2048,512]{1,0:T(8,128)(2,1)S(1)} %bitcast.11), channel_id=1, source_target_pairs={{0,1},{1,0},{2,3},{3,2},{4,5},{5,4},{6,7},{7,6},{8,9},{9,8},{10,11... | collective-permute-start | bytes 6291464 | tf_op jit(solution)/shard_map/prefix_gather/ppermute | solution.py:417
  71.9 1.4 copy-start.6
  76.3 2.8 %copy-start = (bf16[512,2560]{1,0:T(8,128)(2,1)S(1)}, bf16[512,2560]{1,0:T(8,128)(2,1)}, u32[]{:S(2)}) copy-start(bf16[512,2560]{1,0:T(8,128)(2,1)} %refs_2_.1) | copy-start | bytes 7864324
  76.3 23.8 %slice-start = ((s8[6553600]{0:T(1024)(128)(4,1)}), s8[4194304]{0:T(1024)(128)(4,1)S(1)}, s32[]{:S(2)}) async-start(s8[6553600]{0:T(1024)(128)(4,1)} %bitcast.16), calls=%async_computation.1 | async-start | bytes 8388608
  79.2 21.0 %slice-start.1 = ((s8[6553600]{0:T(1024)(128)(4,1)}), s8[2359296]{0:T(1024)(128)(4,1)S(1)}, s32[]{:S(2)}) async-start(s8[6553600]{0:T(1024)(128)(4,1)} %bitcast.16), calls=%async_computation.2 | async-start | bytes 4718592
  79.2 24.5 %slice-start.2 = ((s8[6553600]{0:T(1024)(128)(4,1)}), s8[2359296]{0:T(1024)(128)(4,1)S(1)}, s32[]{:S(2)}) async-start(s8[6553600]{0:T(1024)(128)(4,1)} %bitcast.18), calls=%async_computation.3 | async-start | bytes 4718592
  100.1 3.6 %slice-start.3 = ((s8[6553600]{0:T(1024)(128)(4,1)}), s8[4194304]{0:T(1024)(128)(4,1)S(1)}, s32[]{:S(2)}) async-start(s8[6553600]{0:T(1024)(128)(4,1)} %bitcast.18), calls=%async_computation.4 | async-start | bytes 8388608
  113.3 21.2 %copy-start.2 = (f32[2560]{0:T(1024)S(1)}, f32[2560]{0:T(1024)}, u32[]{:S(2)}) copy-start(f32[2560]{0:T(1024)} %param.28) | copy-start | bytes 30724
Sparse Core Ops, SparseCore 0:
  9.5 54.8 all-gather.2
